TPU v7x, 128 devices: a whole 4x4x4 slice. The times are simulated.
128 devices in a mesh: grp: 8 (over z, core), dom: 16 (over y, x).
Axes of the slice: x: 4, y: 4, z: 4, core: 2. Of those that a mesh axis runs over, the one named last changes fastest.
Arguments:
- parent_local: float32 [8192, 296], P(('grp', 'dom')), may hold values from -6 to 6
- parent_slot: int32 [65536], P(('grp', 'dom')), may hold values from 0 to 79, as said below
- child_octant: int32 [65536], P(('grp', 'dom')), may hold values from 0 to 7
- child_m2l: float32 [65536, 296], P(('grp', 'dom')), may hold values from -6 to 6
- l2l_ops: float32 [8, 296, 296], replicated, may hold values from -0.375 to 0.375
- leaf_center: float32 [65536, 3], P(('grp', 'dom')), may hold values from 0 to 2
- src_coords: float32 [65536, 3, 128], P(('grp', 'dom')), may hold values from 0 to 2
- src_charge: float32 [65536, 128], P(('grp', 'dom')), may hold values from -6 to 6
- obs_owner: int32 [65536], replicated, may hold values from 0 to 127, as said below
- obs_offset: float32 [131072, 3, 128], P(('grp', 'dom')), may hold values from -1 to 1
- near_slots: int32 [131072, 8], P(('grp', 'dom')), may hold values from 0 to 1023, as said below
Outputs:
- leaf_local: float32 [65536, 296], P(('grp', 'dom'))
- potential: float32 [131072, 128], P(('grp', 'dom'))
Inputs may be any that keep to these rules, and one draw needn't show every extreme that they name: `parent_slot`: values below 16 name the last 16 parents of the previous device in the flat order over grp and dom; a value v of 16 or more names the device's own parent v - 16. Nondecreasing within a device; the first device names only its own parents. `obs_owner`: among one device's 512 leaves at most 8 share an owner; one owner receives exactly 8 leaves from every device. `near_slots`: the first entry of a row is the row's own index within its device; the others are rows of the same device that hold a leaf.
All inputs are finite; a program needn't handle non-finite values.
Results may differ from a plain program's by a relative error of at most 0.0003.
Values sent between devices are 32-bit elements; how exact they have to be, the bound alone decides.
A program may use at most 64 MiB of HBM per device.

v0:
```python
import math

import jax
import jax.numpy as jnp
import numpy as np
from jax import lax
from jax.sharding import PartitionSpec as P

ORDER = 8
RIM = 16


RADIUS = 2.95
half_width = 0.5
soft_sq = 0.0025
four_pi = 4.0 * math.pi


def side_by_side(arrays, axis, split_dim, concat_dim, along):
    columns = [a.reshape(*a.shape[:along], -1) for a in arrays]
    both = jnp.concatenate(columns, axis=along)
    out, at, gathered = (
        lax.all_to_all(both, axis, split_axis=split_dim, concat_axis=concat_dim, tiled=True),
        0,
        [],
    )
    for a, column in zip(arrays, columns):
        share = out[..., at : at + column.shape[along]]
        gathered.append(share.reshape(*share.shape[:along], *a.shape[along:]))
        at += column.shape[along]
    return tuple(gathered)


def from_behind(block, axis, distance):
    devices = range(lax.axis_size(axis))
    route = [(i - distance, i) for i in devices if i - distance in devices]
    return lax.ppermute(block, axis, route)


def cut_along(array, dim, peers):
    shape = array.shape
    parts = array.reshape(*shape[:dim], peers, shape[dim] // peers, *shape[dim + 1 :])
    return jnp.moveaxis(parts, dim, 0)


def cut_rows(length, count):
    hop = length // count
    if hop >= 8:
        hop -= hop % 8
    return [hop * k for k in range(1, count)]


def laid_out(parts, dim):
    parts = jnp.moveaxis(parts, 0, dim)
    shape = parts.shape
    return parts.reshape(*shape[:dim], shape[dim] * shape[dim + 1], *shape[dim + 2 :])


def exchange_in_pieces(array, axis, pieces, split_dim, concat_dim):
    parts = cut_along(array, split_dim, lax.axis_size(axis))
    cut = max(range(1, max(2, parts.ndim - 1)), key=lambda d: parts.shape[d])
    gathered = []
    for share in jnp.split(parts, cut_rows(parts.shape[cut], pieces), axis=cut):
        if share.size:
            gathered.append(lax.all_to_all(share, axis, split_axis=0, concat_axis=0, tiled=True))
    return laid_out(jnp.concatenate(gathered, axis=cut), concat_dim)


def surface_points():
    grid = np.linspace(-1.0, 1.0, ORDER)
    points = np.stack(np.meshgrid(grid, grid, grid, indexing="ij"), 0).reshape(3, -1)
    on_surface = np.max(np.abs(points), axis=0) > 1.0 - 1e-09
    return jnp.asarray(points[:, on_surface] * RADIUS, dtype=jnp.float32)


def far_block(densities, offsets):
    surface = surface_points()
    dist_sq = jnp.zeros((offsets.shape[0], surface.shape[1], offsets.shape[2]), jnp.float32)
    for component in range(3):
        separation = offsets[:, component, None, :] - surface[component][None, :, None]
        dist_sq = dist_sq + separation * separation
    kernel = 1.0 / (four_pi * half_width * jnp.sqrt(dist_sq))
    return jnp.sum(densities[:, :, None] * kernel, axis=1)


def near_block(targets, fetch_rows, neighbours):
    summed = jnp.zeros((targets.shape[0], targets.shape[2]), jnp.float32)
    for column in range(neighbours.shape[1]):
        coords, charges = fetch_rows(neighbours[:, column])
        dist_sq = jnp.full(
            (targets.shape[0], targets.shape[2], coords.shape[2]), soft_sq, jnp.float32
        )
        for component in range(3):
            separation = targets[:, component, :, None] - coords[:, component, None, :]
            dist_sq = dist_sq + separation * separation
        summed = summed + jnp.sum(charges[:, None, :] * lax.rsqrt(dist_sq), axis=2)
    return summed / four_pi


def on_device(
    parent_local,
    parent_slot,
    child_octant,
    child_m2l,
    l2l_ops,
    leaf_center,
    src_coords,
    src_charge,
    obs_owner,
    obs_offset,
    near_slots,
):
    device_list = lax.axis_size(("grp", "dom"))
    leaf_dev = child_m2l.shape[0]
    slot_table = obs_offset.shape[0]
    points = obs_offset.shape[2]
    width = child_m2l.shape[1]
    capacity = slot_table // device_list
    my_index = lax.axis_index(("grp", "dom"))
    mine = lax.dynamic_slice_in_dim(obs_owner, my_index * leaf_dev, leaf_dev)
    onehot = (mine[:, None] == jnp.arange(device_list, dtype=jnp.int32)[None, :]).astype(jnp.int32)
    before = jnp.cumsum(onehot, axis=0) - onehot
    leaf_rank = jnp.sum(before * onehot, axis=1)
    dest_row = mine * capacity + leaf_rank
    counts = jnp.sum(
        (obs_owner.reshape(device_list, leaf_dev) == my_index).astype(jnp.int32), axis=1
    )
    is_live = (jnp.arange(capacity, dtype=jnp.int32)[None, :] < counts[:, None]).reshape(slot_table)
    packed_coords = jnp.zeros((slot_table, 3, points), jnp.float32).at[dest_row].set(src_coords)
    packed_charge = jnp.zeros((slot_table, points), jnp.float32).at[dest_row].set(src_charge)
    packed_center = jnp.zeros((slot_table, 3), jnp.float32).at[dest_row].set(leaf_center)
    recv_coords, recv_charge, recv_center = side_by_side(
        (
            packed_coords.reshape(device_list, capacity, 3, points),
            packed_charge.reshape(device_list, capacity, points),
            packed_center.reshape(device_list, capacity, 3),
        ),
        ("grp", "dom"),
        0,
        0,
        2,
    )
    recv_coords = recv_coords.reshape(slot_table, 3, points)
    recv_charge = recv_charge.reshape(slot_table, points)
    recv_center = recv_center.reshape(slot_table, 3)
    rim_rows = from_behind(parent_local[parent_local.shape[0] - RIM :], ("grp", "dom"), 1)
    parents = jnp.concatenate([rim_rows, parent_local], axis=0)
    moved = jnp.einsum("pr,oqr->opq", parents, l2l_ops, precision=lax.Precision.HIGHEST)
    stacked = moved.reshape(8 * parents.shape[0], width)
    leaf_local = child_m2l + stacked[child_octant * parents.shape[0] + parent_slot]
    packed_dens = jnp.zeros((slot_table, width), jnp.float32).at[dest_row].set(leaf_local)
    recv_dens = exchange_in_pieces(
        packed_dens.reshape(device_list, capacity, width), ("grp", "dom"), 2, 0, 0
    )
    recv_dens = recv_dens.reshape(slot_table, width)

    def fetch_rows(index):
        return (recv_coords[index], recv_charge[index])

    def block_total(pieces):
        densities, offsets, centers, block_near = pieces
        targets = centers[:, :, None] + half_width * offsets
        return far_block(densities, offsets) + near_block(targets, fetch_rows, block_near)

    block = math.gcd(slot_table, 512)
    count_blocks = slot_table // block
    totals = lax.map(
        block_total,
        (
            recv_dens.reshape(count_blocks, block, width),
            obs_offset.reshape(count_blocks, block, 3, points),
            recv_center.reshape(count_blocks, block, 3),
            near_slots.reshape(count_blocks, block, near_slots.shape[1]),
        ),
    )
    potential = jnp.where(is_live[:, None], totals.reshape(slot_table, points), 0.0)
    return (leaf_local, potential)


def solution(mesh):
    placed = (
        P(("grp", "dom"), None),
        P(("grp", "dom")),
        P(("grp", "dom")),
        P(("grp", "dom"), None),
        P(),
        P(("grp", "dom"), None),
        P(("grp", "dom"), None, None),
        P(("grp", "dom"), None),
        P(),
        P(("grp", "dom"), None, None),
        P(("grp", "dom"), None),
    )
    return jax.shard_map(
        on_device,
        mesh=mesh,
        in_specs=placed,
        out_specs=(P(("grp", "dom"), None), P(("grp", "dom"), None)),
        check_vma=False,
    )
```

profile of v0, /device:TPU:1, one launch (start us, length us, event | category | flops | bytes accessed | tf_op | source)
XLA Modules:
  0.0 829.4 jit_solution(8171133530468201811)
XLA Ops:
  1.4 3.9 collective-permute-start
  11.1 6.3 fusion.18
  17.4 2.3 gather_fusion.16
  20.9 2.6 scatter_custom_fusion
  24.7 26.4 %all_to_all.15 = f32[128,1,4,296]{3,2,1,0:T(4,128)} all-to-all(f32[128,1,4,296]{3,2,1,0:T(4,128)S(1)} %get-tuple-element.171), channel_id=1, replica_groups=mesh['grp'=8,'dom'=16] {'grp','dom'}, dimensions={0} | all-to-all | bytes 1212416 | tf_op jit(solution)/shard_map/all_to_all | solution.py:65
  51.1 5.2 all-to-all-start
  56.5 2.5 scatter_custom_fusion.3
  59.0 3.1 scatter_custom_fusion.2
  62.9 13.6 %scatter_fusion = f32[1024,3,128]{2,1,0:T(4,128)S(1)} fusion(f32[1024,3,128]{2,1,0:T(4,128)S(1)} %broadcast_in_dim.42, s32[512]{0:T(512)S(1)} %compare_select_fusion.8, f32[512,3,128]{2,1,0:T(4,128)S(1)} %copy.41), kind=kCustom, calls=%fused_computation.18 | custom fusion | bytes 2361344 | tf_op jit(solution)/shard_map/scatter | solution.py:129
  76.5 1.8 reshape_reshape.13
  78.3 3.1 pad_maximum_fusion
  81.4 9.9 %all-to-all-start.2 = ((f32[128,8,515]{2,1,0:T(8,128)}), f32[128,8,515]{2,1,0:T(8,128)S(1)}, u32[]{:S(2)}, u32[]{:S(2)}) async-start(f32[128,8,515]{2,1,0:T(8,128)} %pad_maximum_fusion), calls=%async_computation.2 | async-start | bytes 5242880 | tf_op jit(solution)/shard_map/all_to_all | solution.py:23
  91.3 1.7 compare_convert_fusion
  93.0 1.7 reshape.155
  96.5 2.2 copy.45
  98.7 2.6 pad_maximum_fusion.1
  101.3 25.3 %all-to-all-done.2 = f32[128,8,515]{2,1,0:T(8,128)S(1)} async-done(((f32[128,8,515]{2,1,0:T(8,128)}), f32[128,8,515]{2,1,0:T(8,128)S(1)}, u32[]{:S(2)}, u32[]{:S(2)}) %all-to-all-start.2) | async-done | bytes 2109472 | tf_op jit(solution)/shard_map/all_to_all | solution.py:23
  129.4 2.5 reshape_reshape.15
  133.0 693.9 %while.11 = (s32[]{:T(128)}, f32[2,512,128]{2,1,0:T(8,128)}, f32[2,512,296]{2,1,0:T(8,128)}, f32[2,512,3,128]{3,1,0,2:T(8,128)}, s32[2,512,8]{1,2,0:T(8,128)S(1)...) while((s32[]{:T(128)}, f32[2,512,128]{2,1,0:T(8,128)}, ...), condition=%wide.region_18.19_spmd.clone, body=%wide.region_8.18_spmd.sunk.clone.sunk | while | flops 971395072 | bytes 66869072 | solution.py:167
  152.2 66.6 %fusion.41 = f32[512,128]{1,0:T(8,128)} fusion(f32[296]{0:T(512)S(1)} %get-tuple-element.350, f32[296]{0:T(512)S(1)} %get-tuple-element.351, f32[296]{0:T(512)S(1)} %get-tuple-element.352, f32[512,128]{1,0:T(8,128)S(1)} %get-tuple-element.271, f32[512,128]{1,0:T(8,128)S(1)} %get-tuple-element.272, f32[512,128]{1,0:T(8,128)S(1)} %get-tuple-element.273, ...), kind=kLoop, calls=%fused_computation.30.clone.1 | loop fusion | flops 232718336 | bytes 1658336 | tf_op jit(solution)/shard_map/while/body/eval_jaxpr/reduce_sum | solution.py:83
  218.9 2.6 gather_fusion
  221.5 3.6 fusion.42
  225.1 1.6 gather_fusion.1
  226.8 2.6 gather_fusion.2
  229.4 3.7 fusion.43
  234.8 2.6 gather_fusion.4
  237.4 3.7 fusion.44
  242.7 2.6 gather_fusion.6
  245.3 3.6 fusion.45
  249.0 1.6 gather_fusion.7
  250.6 103.2 %multiply_reduce_fusion.10 = (f32[512,128]{1,0:T(8,128)}, f32[512,128]{1,0:T(8,128)}, f32[512,128]{1,0:T(8,128)}, f32[512,128]{1,0:T(8,128)}) fusion(f32[512,128]{1,0:T(8,128)} %bitcast.172, f32[512,128]{1,0:T(8,128)S(1)} %get-tuple-element.276, f32[512,128]{1,0:T(8,128)} %bitcast.171, f32[512,128]{1,0:T(8,128)S(1)} %get-tuple-element.278, ...), kind=kLoop, calls=%fused_computation.38.clone.1 | loop fusion | flops 368836608 | bytes 6029312 | tf_op jit(solution)/shard_map/while/body/eval_jaxpr/reduce_sum | solution.py:96
  353.8 2.6 gather_fusion.8
  356.4 3.6 fusion.46
  360.1 1.6 gather_fusion.9
  361.7 2.6 gather_fusion.10
  364.3 3.7 fusion.47
  369.7 2.6 gather_fusion.12
  372.3 3.7 fusion.48
  377.6 2.6 gather_fusion.14
  380.3 3.6 fusion.49
  383.9 1.6 gather_fusion.15
  385.6 102.2 %multiply_reduce_fusion.11 = (f32[512,128]{1,0:T(8,128)S(1)}, f32[512,128]{1,0:T(8,128)S(1)}, f32[512,128]{1,0:T(8,128)S(1)}, f32[512,128]{1,0:T(8,128)S(1)}) fusion(f32[512,128]{1,0:T(8,128)} %bitcast.169, f32[512,128]{1,0:T(8,128)} %bitcast.168, f32[512,128]{1,0:T(8,128)} %bitcast.167, f32[512,128]{1,0:T(8,128)} %gather_fusion.9, ...), kind=kLoop, calls=%fused_computation.37.clone.1 | loop fusion | flops 368836608 | bytes 6029312 | tf_op jit(solution)/shard_map/while/body/eval_jaxpr/reduce_sum | solution.py:96
  490.4 66.6 %fusion.41 = f32[512,128]{1,0:T(8,128)} fusion(f32[296]{0:T(512)S(1)} %get-tuple-element.350, f32[296]{0:T(512)S(1)} %get-tuple-element.351, f32[296]{0:T(512)S(1)} %get-tuple-element.352, f32[512,128]{1,0:T(8,128)S(1)} %get-tuple-element.271, f32[512,128]{1,0:T(8,128)S(1)} %get-tuple-element.272, f32[512,128]{1,0:T(8,128)S(1)} %get-tuple-element.273, ...), kind=kLoop, calls=%fused_computation.30.clone.1 | loop fusion | flops 232718336 | bytes 1658336 | tf_op jit(solution)/shard_map/while/body/eval_jaxpr/reduce_sum | solution.py:83
  557.1 2.6 gather_fusion
  559.7 3.6 fusion.42
  563.4 1.6 gather_fusion.1
  565.0 2.6 gather_fusion.2
  567.7 3.7 fusion.43
  573.0 2.6 gather_fusion.4
  575.6 3.7 fusion.44
  580.9 2.6 gather_fusion.6
  583.6 3.6 fusion.45
  588.9 103.2 %multiply_reduce_fusion.10 = (f32[512,128]{1,0:T(8,128)}, f32[512,128]{1,0:T(8,128)}, f32[512,128]{1,0:T(8,128)}, f32[512,128]{1,0:T(8,128)}) fusion(f32[512,128]{1,0:T(8,128)} %bitcast.172, f32[512,128]{1,0:T(8,128)S(1)} %get-tuple-element.276, f32[512,128]{1,0:T(8,128)} %bitcast.171, f32[512,128]{1,0:T(8,128)S(1)} %get-tuple-element.278, ...), kind=kLoop, calls=%fused_computation.38.clone.1 | loop fusion | flops 368836608 | bytes 6029312 | tf_op jit(solution)/shard_map/while/body/eval_jaxpr/reduce_sum | solution.py:96
  692.0 2.6 gather_fusion.8
  694.7 3.6 fusion.46
  698.3 1.6 gather_fusion.9
  699.9 2.6 gather_fusion.10
  702.6 3.7 fusion.47
  707.9 2.6 gather_fusion.12
  710.5 3.7 fusion.48
  715.8 2.6 gather_fusion.14
  718.5 3.6 fusion.49
  723.8 102.2 %multiply_reduce_fusion.11 = (f32[512,128]{1,0:T(8,128)S(1)}, f32[512,128]{1,0:T(8,128)S(1)}, f32[512,128]{1,0:T(8,128)S(1)}, f32[512,128]{1,0:T(8,128)S(1)}) fusion(f32[512,128]{1,0:T(8,128)} %bitcast.169, f32[512,128]{1,0:T(8,128)} %bitcast.168, f32[512,128]{1,0:T(8,128)} %bitcast.167, f32[512,128]{1,0:T(8,128)} %gather_fusion.9, ...), kind=kLoop, calls=%fused_computation.37.clone.1 | loop fusion | flops 368836608 | bytes 6029312 | tf_op jit(solution)/shard_map/while/body/eval_jaxpr/reduce_sum | solution.py:96
  826.9 2.0 bitcast_select_fusion
  (127 shorter events, 37.3 us)
Async XLA Ops:
  1.4 9.7 %collective-permute-start = (f32[16,296]{1,0:T(8,128)S(1)}, f32[16,296]{1,0:T(8,128)S(1)}, u32[]{:S(2)}, u32[]{:S(2)}) collective-permute-start(f32[16,296]{1,0:T(8,128)S(1)} %slice.162), channel_id=1, source_target_pairs={{0,1},{1,2},{2,3},{3,4},{4,5},{5,6},{6,7},{7,8},{8,9},{9,10},{10,1... | collective-permute-start | bytes 56840 | tf_op jit(solution)/shard_map/ppermute | solution.py:37
  20.9 30.2 %copy-start.8 = (f32[512,296]{1,0:T(8,128)}, f32[512,296]{1,0:T(8,128)S(1)}, u32[]{:S(2)}) copy-start(f32[512,296]{1,0:T(8,128)S(1)} %add.223) | copy-start | bytes 1818628
  20.9 35.4 %copy-start.15 = (f32[512,3]{0,1:T(4,128)S(1)}, f32[512,3]{0,1:T(4,128)}, u32[]{:S(2)}) copy-start(f32[512,3]{0,1:T(4,128)} %param.19) | copy-start | bytes 18436
  24.7 37.4 %copy-start.11 = (f32[512,3,128]{2,0,1:T(8,128)S(1)}, f32[512,3,128]{2,0,1:T(8,128)}, u32[]{:S(2)}) copy-start(f32[512,3,128]{2,0,1:T(8,128)} %param.20) | copy-start | bytes 2359300
  51.1 30.3 %all-to-all-start = ((f32[128,1,4,296]{3,2,1,0:T(4,128)}), f32[128,1,4,296]{3,2,1,0:T(4,128)}, u32[]{:S(2)}, u32[]{:S(2)}) async-start(f32[128,1,4,296]{3,2,1,0:T(4,128)} %get-tuple-element.170), calls=%async_computation | async-start | bytes 1572864 | tf_op jit(solution)/shard_map/all_to_all | solution.py:65
  76.5 1.8 copy-start.9
  76.5 1.8 copy-start.10
  81.4 17.3 %copy-start.7 = (f32[128,1,4,296]{3,2,1,0:T(4,128)S(1)}, f32[128,1,4,296]{3,2,1,0:T(4,128)}, u32[]{:S(2)}) copy-start(f32[128,1,4,296]{3,2,1,0:T(4,128)} %all_to_all.15) | copy-start | bytes 1818628
  81.4 45.2 %all-to-all-start.2 = ((f32[128,8,515]{2,1,0:T(8,128)}), f32[128,8,515]{2,1,0:T(8,128)S(1)}, u32[]{:S(2)}, u32[]{:S(2)}) async-start(f32[128,8,515]{2,1,0:T(8,128)} %pad_maximum_fusion), calls=%async_computation.2 | async-start | bytes 5242880 | tf_op jit(solution)/shard_map/all_to_all | solution.py:23
  126.6 1.5 copy-start.1
  128.1 4.9 copy-start.14
  128.1 4.9 copy-start.17
  128.1 4.9 copy-start.18
  128.1 4.9 copy-start.19
  133.0 693.9 %copy-start.16 = (pred[1024]{0:T(1024)(128)(4,1)S(1)}, pred[1024]{0:T(1024)(128)(4,1)}, u32[]{:S(2)}) copy-start(pred[1024]{0:T(1024)(128)(4,1)} %lt.79) | copy-start | bytes 3076
  150.5 1.7 copy-start
  385.5 102.2 %copy-start.2 = (f32[512,128]{1,0:T(8,128)S(1)}, f32[512,128]{1,0:T(8,128)}, u32[]{:S(2)}) copy-start(f32[512,128]{1,0:T(8,128)} %fusion.41) | copy-start | bytes 786436 | tf_op jit(solution)/shard_map/while
  385.5 102.2 %copy-start.3 = (f32[512,128]{1,0:T(8,128)S(1)}, f32[512,128]{1,0:T(8,128)}, u32[]{:S(2)}) copy-start(f32[512,128]{1,0:T(8,128)} %get-tuple-element.315) | copy-start | bytes 786436 | tf_op jit(solution)/shard_map/while
  385.5 102.2 %copy-start.4 = (f32[512,128]{1,0:T(8,128)S(1)}, f32[512,128]{1,0:T(8,128)}, u32[]{:S(2)}) copy-start(f32[512,128]{1,0:T(8,128)} %get-tuple-element.295) | copy-start | bytes 786436 | tf_op jit(solution)/shard_map/while
  385.5 102.2 %copy-start.5 = (f32[512,128]{1,0:T(8,128)S(1)}, f32[512,128]{1,0:T(8,128)}, u32[]{:S(2)}) copy-start(f32[512,128]{1,0:T(8,128)} %get-tuple-element.294) | copy-start | bytes 786436 | tf_op jit(solution)/shard_map/while
  385.5 102.2 %copy-start.6 = (f32[512,128]{1,0:T(8,128)S(1)}, f32[512,128]{1,0:T(8,128)}, u32[]{:S(2)}) copy-start(f32[512,128]{1,0:T(8,128)} %get-tuple-element.293) | copy-start | bytes 786436 | tf_op jit(solution)/shard_map/while
  385.6 102.2 %copy-start.12 = (f32[2,512,128]{2,1,0:T(8,128)S(1)}, f32[2,512,128]{2,1,0:T(8,128)}, u32[]{:S(2)}) copy-start(f32[2,512,128]{2,1,0:T(8,128)} %get-tuple-element.330) | copy-start | bytes 1572868 | tf_op jit(solution)/shard_map/while
  487.9 0.8 copy-start.13
  488.7 1.6 copy-start
  723.8 102.2 %copy-start.2 = (f32[512,128]{1,0:T(8,128)S(1)}, f32[512,128]{1,0:T(8,128)}, u32[]{:S(2)}) copy-start(f32[512,128]{1,0:T(8,128)} %fusion.41) | copy-start | bytes 786436 | tf_op jit(solution)/shard_map/while
  723.8 102.2 %copy-start.3 = (f32[512,128]{1,0:T(8,128)S(1)}, f32[512,128]{1,0:T(8,128)}, u32[]{:S(2)}) copy-start(f32[512,128]{1,0:T(8,128)} %get-tuple-element.315) | copy-start | bytes 786436 | tf_op jit(solution)/shard_map/while
  723.8 102.2 %copy-start.4 = (f32[512,128]{1,0:T(8,128)S(1)}, f32[512,128]{1,0:T(8,128)}, u32[]{:S(2)}) copy-start(f32[512,128]{1,0:T(8,128)} %get-tuple-element.295) | copy-start | bytes 786436 | tf_op jit(solution)/shard_map/while
  723.8 102.2 %copy-start.5 = (f32[512,128]{1,0:T(8,128)S(1)}, f32[512,128]{1,0:T(8,128)}, u32[]{:S(2)}) copy-start(f32[512,128]{1,0:T(8,128)} %get-tuple-element.294) | copy-start | bytes 786436 | tf_op jit(solution)/shard_map/while
  723.8 102.2 %copy-start.6 = (f32[512,128]{1,0:T(8,128)S(1)}, f32[512,128]{1,0:T(8,128)}, u32[]{:S(2)}) copy-start(f32[512,128]{1,0:T(8,128)} %get-tuple-element.293) | copy-start | bytes 786436 | tf_op jit(solution)/shard_map/while
  723.8 102.2 %copy-start.12 = (f32[2,512,128]{2,1,0:T(8,128)S(1)}, f32[2,512,128]{2,1,0:T(8,128)}, u32[]{:S(2)}) copy-start(f32[2,512,128]{2,1,0:T(8,128)} %get-tuple-element.330) | copy-start | bytes 1572868 | tf_op jit(solution)/shard_map/while
  826.2 0.8 copy-start.13
where the time goes:
time: 839 us; the launch traced here: 829 us
  other arithmetic  561 us (67%)
  local copies, waits for them, and re-layouts  172 us (21%)
  blocking collectives  26.4 us (3%)
  waiting for transfers between devices  26.1 us (3%)
  starting transfers between devices  19.1 us (2%)
  loops' own time  17.7 us (2%)
    reduce_sum x4, other arithmetic, near_block(): summed = summed + jnp.sum(charges[:, None, :] * lax.rsqrt(dist_sq), axis=2)  411 us
    reduce_sum x2, other arithmetic, far_block(): return jnp.sum(densities[:, :, None] * kernel, axis=1)  133 us
    gather x32, local copies, waits for them, and re-layouts, fetch_rows(): return (recv_coords[index], recv_charge[index])  68.5 us
    slice x16, local copies, waits for them, and re-layouts, near_block(): separation = targets[:, component, :, None] - coords[:, component, None, :]  58.4 us
    all_to_all x1, blocking collectives, exchange_in_pieces(): lax.all_to_all(share, axis, split_axis=0, concat_axis=0, tiled=True)  26.4 us
    all_to_all x1, waiting for transfers between devices, side_by_side(): lax.all_to_all(both, axis, split_axis=split_dim, concat_axis=concat_dim,...  25.3 us
    another operation x1, loops' own time, on_device(): lax.map(block_total, (recv_dens.reshape(count_blocks, block, width), obs_...  17.7 us
  transfers between devices with their start and end apart: 3, of which 2 were waited for; matrix products, arithmetic and copies ran while one was open for 5% of the time, Pallas kernels for 0%

commit v1 on v0

v1 whole, which is shorter than its diff:
```python
import functools
import math

import jax
import jax.numpy as jnp
import numpy as np
from jax import lax
from jax.experimental import pallas as pl
from jax.experimental.pallas import tpu as pltpu
from jax.sharding import PartitionSpec as P

ORDER = 8
RIM = 16
RADIUS = 2.95
HALF = 0.5
SOFT_SQ = 0.0025
AXES = ("grp", "dom")
F32 = jnp.float32
BF16 = jnp.bfloat16
FEATURES = 32


def from_behind(block, axis, distance):
    devices = range(lax.axis_size(axis))
    route = [(i - distance, i) for i in devices if i - distance in devices]
    return lax.ppermute(block, axis, route)


def pack_kernel(capacity, owner, coords, charge, center, out, dest, count, tail):
    devices = out.shape[0]
    leaves = coords.shape[0]
    out[...] = jnp.zeros_like(out)
    tail[:, 0:3] = center[...]
    tail[:, 3:4] = jnp.ones((leaves, 1), F32)

    def clear(i, carry):
        count[i] = 0
        return carry

    lax.fori_loop(0, devices, clear, 0, unroll=8)

    def place(j, carry):
        o = owner[j]
        rank = count[o]
        count[o] = rank + 1
        dest[j] = o * capacity + rank
        row = coords[j]
        for c in range(3):
            out[o, c, pl.ds(rank, 1), :] = row[c : c + 1]
        out[o, 3, pl.ds(rank, 1), :] = charge[pl.ds(j, 1), :]
        out[o, 4, pl.ds(rank, 1), 0:4] = tail[pl.ds(j, 1), :]
        return carry

    lax.fori_loop(0, leaves, place, 0, unroll=4)


def pack(owner, coords, charge, center, devices, capacity):
    leaves = coords.shape[0]
    vmem = pl.BlockSpec(memory_space=pltpu.VMEM)
    return pl.pallas_call(
        functools.partial(pack_kernel, capacity),
        out_shape=(
            jax.ShapeDtypeStruct((devices, 5, capacity, 128), F32),
            jax.ShapeDtypeStruct((leaves,), jnp.int32),
        ),
        in_specs=[pl.BlockSpec(memory_space=pltpu.SMEM), vmem, vmem, vmem],
        out_specs=(vmem, pl.BlockSpec(memory_space=pltpu.SMEM)),
        scratch_shapes=[pltpu.SMEM((devices,), jnp.int32), pltpu.VMEM((leaves, 4), F32)],
        compiler_params=pltpu.CompilerParams(vmem_limit_bytes=24 << 20),
        name="pack",
    )(owner, coords, charge, center)


def leaf_kernel(which, dest, stacked, m2l, leaf, dens):
    leaves = m2l.shape[0]
    dens[...] = jnp.zeros_like(dens)

    def place(j, carry):
        row = m2l[pl.ds(j, 1), :] + stacked[pl.ds(which[j], 1), :]
        leaf[pl.ds(j, 1), :] = row
        dens[pl.ds(dest[j], 1), :] = row
        return carry

    lax.fori_loop(0, leaves, place, 0, unroll=8)


def leaf_rows(which, dest, stacked, m2l, slots):
    width = m2l.shape[1]
    vmem = pl.BlockSpec(memory_space=pltpu.VMEM)
    smem = pl.BlockSpec(memory_space=pltpu.SMEM)
    return pl.pallas_call(
        leaf_kernel,
        out_shape=(
            jax.ShapeDtypeStruct(m2l.shape, F32),
            jax.ShapeDtypeStruct((slots, width), F32),
        ),
        in_specs=[smem, smem, vmem, vmem],
        out_specs=(vmem, vmem),
        compiler_params=pltpu.CompilerParams(vmem_limit_bytes=24 << 20),
        name="leaf_rows",
    )(which, dest, stacked, m2l)


def split3(v):
    high = v.astype(BF16).astype(F32)
    rest = v - high
    middle = rest.astype(BF16).astype(F32)
    return high, middle, rest - middle


def target_features(x, y, z):
    out = []
    for v in (x, y, z):
        h, m, l = split3(v)
        out += [h, h, h, m, m, l]
    return out + list(split3(x * x + y * y + z * z + SOFT_SQ))


def source_features(x, y, z):
    out = []
    for v in (x, y, z):
        h, m, l = split3(-2.0 * v)
        out += [h, m, l, h, m, h]
    return out, list(split3(x * x + y * y + z * z))


def near_kernel(group, unroll, near_list, src, off, out, table, charges, tfeat, sfeat):
    step = pl.program_id(0)
    senders, _, cap, _ = src.shape
    ones = jnp.ones((8, 128), F32)
    zeros = jnp.zeros((8, 128), F32)

    @pl.when(step == 0)
    def _():
        for f in range(18, 21):
            sfeat[8 * f : 8 * f + 8] = ones
        for f in range(24, FEATURES):
            sfeat[8 * f : 8 * f + 8] = zeros
        for u in range(unroll):
            for f in range(21, 24):
                tfeat[u, 8 * f : 8 * f + 8] = ones
            for f in range(24, FEATURES):
                tfeat[u, 8 * f : 8 * f + 8] = zeros

        def prepare(i, carry):
            cross, square = source_features(*(src[i, c] - 1.0 for c in range(3)))
            for f, v in list(enumerate(cross)) + list(enumerate(square, 21)):
                sfeat[8 * f : 8 * f + 8] = v
            for s in range(8):
                table[i * 8 + s] = sfeat[pl.ds(s, FEATURES, stride=8), :].astype(BF16)
            charges[pl.ds(i * 8, 8)] = src[i, 3] * (0.25 / math.pi)
            return carry

        lax.fori_loop(0, senders, prepare, 0)

    lane_part = lax.broadcasted_iota(jnp.int32, (128, 128), 1) // FEATURES

    def rows(i, carry):
        for u in range(unroll):
            local = i * unroll + u
            block = step * group + local
            info = src[block, 4]
            shift = off[local]
            place = [(info[:, c : c + 1] - 1.0) + HALF * shift[:, c] for c in range(3)]
            for f, v in enumerate(target_features(*place)):
                tfeat[u, 8 * f : 8 * f + 8] = v
            for s in range(8):
                feat = tfeat[u, pl.ds(s, FEATURES, stride=8), :]
                turned = jnp.concatenate([feat.astype(BF16)] * 4, axis=0).T
                left = jnp.concatenate(
                    [jnp.where(lane_part == k, turned, jnp.zeros_like(turned)) for k in range(4)],
                    axis=0,
                )
                at = [near_list[(block * 8 + s) * 8 + j] for j in range(8)]
                right = jnp.concatenate(
                    [
                        jnp.concatenate([table[at[2 * k]], table[at[2 * k + 1]]], axis=1)
                        for k in range(4)
                    ],
                    axis=0,
                )
                dist_sq = jnp.dot(left, right, preferred_element_type=F32)
                total = None
                for k in range(4):
                    for h in range(2):
                        weight = charges[pl.ds(at[2 * k + h], 1), :]
                        part = dist_sq[128 * k : 128 * k + 128, 128 * h : 128 * h + 128]
                        term = lax.rsqrt(part) * weight
                        total = term if total is None else total + term
                out[pl.ds(local * 8 + s, 1), :] = jnp.sum(total.T, axis=0, keepdims=True)
            live = info[:, 3:4] > 0.5
            out[pl.ds(local * 8, 8), :] = jnp.where(live, out[pl.ds(local * 8, 8), :], 0.0)
        return carry

    lax.fori_loop(0, group // unroll, rows, 0)


def near_field(src, offsets, near_slots, group=16, unroll=2):
    senders, _, cap, _ = src.shape
    slots = senders * cap
    return pl.pallas_call(
        functools.partial(near_kernel, group, unroll),
        out_shape=jax.ShapeDtypeStruct((slots, 128), F32),
        grid_spec=pltpu.PrefetchScalarGridSpec(
            num_scalar_prefetch=1,
            grid=(senders // group,),
            in_specs=[
                pl.BlockSpec(src.shape, lambda g, n: (0, 0, 0, 0)),
                pl.BlockSpec((group, cap, 3, 128), lambda g, n: (g, 0, 0, 0)),
            ],
            out_specs=pl.BlockSpec((group * cap, 128), lambda g, n: (g, 0)),
            scratch_shapes=[
                pltpu.VMEM((slots, FEATURES, 128), BF16),
                pltpu.VMEM((slots, 128), F32),
                pltpu.VMEM((unroll, FEATURES * 8, 128), F32),
                pltpu.VMEM((FEATURES * 8, 128), F32),
            ],
        ),
        compiler_params=pltpu.CompilerParams(vmem_limit_bytes=40 << 20),
        cost_estimate=pl.CostEstimate(
            flops=2 * slots * 512 * 128 * 256, bytes_accessed=8 << 20, transcendentals=slots << 17
        ),
        name="near_field",
    )(near_slots, src, offsets)


def far_kernel(dens, off, near, out):
    grid = [float(v) for v in (np.linspace(-1.0, 1.0, ORDER) * RADIUS).astype(np.float32)]
    edge = (0, ORDER - 1)

    def block(i, carry):
        shift = off[i]
        axis_sq = []
        for c in range(3):
            o = shift[:, c]
            axis_sq.append([(o - v) * (o - v) for v in grid])
        weights = dens[pl.ds(i * 8, 8), :]
        sums = [None] * 4
        q = 0
        for a in range(ORDER):
            for b in range(ORDER):
                plane = axis_sq[0][a] + axis_sq[1][b]
                last = range(ORDER) if a in edge or b in edge else edge
                for c in last:
                    term = weights[:, q : q + 1] * lax.rsqrt(plane + axis_sq[2][c])
                    sums[q % 4] = term if sums[q % 4] is None else sums[q % 4] + term
                    q += 1
        total = (sums[0] + sums[1]) + (sums[2] + sums[3])
        out[pl.ds(i * 8, 8), :] = near[pl.ds(i * 8, 8), :] + total * (0.25 / (math.pi * HALF))
        return carry

    lax.fori_loop(0, off.shape[0], block, 0)


def far_field(dens, offsets, near, group=32):
    senders, cap, _, points = offsets.shape
    slots, width = dens.shape
    return pl.pallas_call(
        far_kernel,
        out_shape=jax.ShapeDtypeStruct((slots, points), F32),
        grid=(senders // group,),
        in_specs=[
            pl.BlockSpec((group * cap, width), lambda g: (g, 0)),
            pl.BlockSpec((group, cap, 3, points), lambda g: (g, 0, 0, 0)),
            pl.BlockSpec((group * cap, points), lambda g: (g, 0)),
        ],
        out_specs=pl.BlockSpec((group * cap, points), lambda g: (g, 0)),
        cost_estimate=pl.CostEstimate(
            flops=4 * slots * points * width,
            bytes_accessed=4 << 20,
            transcendentals=slots * points * width,
        ),
        name="far_field",
    )(dens, offsets, near)


def on_device(
    parent_local,
    parent_slot,
    child_octant,
    child_m2l,
    l2l_ops,
    leaf_center,
    src_coords,
    src_charge,
    obs_owner,
    obs_offset,
    near_slots,
):
    devices = lax.axis_size(AXES)
    leaf_dev, width = child_m2l.shape
    slots, _, points = obs_offset.shape
    cap = slots // devices
    me = lax.axis_index(AXES)
    mine = lax.dynamic_slice_in_dim(obs_owner, me * leaf_dev, leaf_dev)

    packed, dest = pack(mine, src_coords, src_charge, leaf_center, devices, cap)
    received = lax.all_to_all(packed, AXES, 0, 0, tiled=True)

    rim = from_behind(parent_local[parent_local.shape[0] - RIM :], AXES, 1)
    parents = jnp.concatenate([rim, parent_local], axis=0)
    moved = jnp.einsum("pr,oqr->opq", parents, l2l_ops, precision=lax.Precision.HIGHEST)
    stacked = moved.reshape(l2l_ops.shape[0] * parents.shape[0], width)
    which = child_octant * parents.shape[0] + parent_slot
    leaf_local, dens = leaf_rows(which, dest, stacked, child_m2l, slots)
    dens = lax.all_to_all(dens.reshape(devices, cap, width), AXES, 0, 0, tiled=True)

    offsets = obs_offset.reshape(devices, cap, 3, points)
    near = near_field(received, offsets, near_slots.reshape(-1))
    potential = far_field(dens.reshape(slots, width), offsets, near)
    return (leaf_local, potential)


def solution(mesh):
    placed = (
        P(AXES, None),
        P(AXES),
        P(AXES),
        P(AXES, None),
        P(),
        P(AXES, None),
        P(AXES, None, None),
        P(AXES, None),
        P(),
        P(AXES, None, None),
        P(AXES, None),
    )
    return jax.shard_map(
        on_device,
        mesh=mesh,
        in_specs=placed,
        out_specs=(P(AXES, None), P(AXES, None)),
        check_vma=False,
    )
```

time: 839 us -> 364 us (0.43); the launches traced: 829 us -> 363 us
  other arithmetic: 561 us -> 0.01 us
  Pallas kernels: 0 us -> 294 us
  local copies, waits for them, and re-layouts: 172 us -> 18.8 us
  blocking collectives: 26.4 us -> 0 us
  loops' own time: 17.7 us -> 0 us
    reduce_sum x8 -> x0, other arithmetic: 545 us -> none  [the longest x4 411 us: near_block(): summed = summed + jnp.sum(charges[:, None, :] * lax.rsqrt(dist_sq), axis=2)]
    pallas_call x0 -> x4, Pallas kernels: none -> 294 us  [the longest x1 181 us: far_field(): pl.pallas_call(far_kernel, out_shape=jax.ShapeDtypeStruct((slots, points)...]
    gather x33 -> x0, local copies, waits for them, and re-layouts: 70.8 us -> none  [the longest x32 68.5 us: fetch_rows(): return (recv_coords[index], recv_charge[index])]
    slice x19 -> x1, local copies, waits for them, and re-layouts: 60.5 us -> 0.61 us  [on_device(): rim = from_behind(parent_local[parent_local.shape[0] - RIM:], AXES, 1)]
    all_to_all x1 -> x0, blocking collectives: 26.4 us -> none  [exchange_in_pieces(): lax.all_to_all(share, axis, split_axis=0, concat_axis=0, tiled=True)]
    all_to_all x2, waiting for transfers between devices: 25.3 us -> 0.01 us  [the longest x1 0.01 us: on_device(): lax.all_to_all(dens.reshape(devices, cap, width), AXES, 0, 0, tiled=True)]
    ppermute x1, waiting for transfers between devices: 0.76 us -> 24 us  [from_behind(): return lax.ppermute(block, axis, route)]
    scatter x4 -> x0, local copies, waits for them, and re-layouts: 21.8 us -> none  [the longest x1 13.6 us: on_device(): jnp.zeros((slot_table, 3, points), jnp.float32).at[dest_row].set(src_coords)]
  transfers between devices with their start and end apart: 3 -> 3, of which waited for: 2 -> 1; matrix products, arithmetic and copies ran while one was open for 5% -> 4% of each run, Pallas kernels for 0% -> 30%
where the time goes in v1:
time: 364 us; the launch traced here: 363 us
  Pallas kernels  294 us (81%)
  waiting for transfers between devices  24 us (7%)
  starting transfers between devices  20.8 us (6%)
  local copies, waits for them, and re-layouts  18.8 us (5%)
  matrix products  4.97 us (1%)
    pallas_call x1, Pallas kernels, far_field(): pl.pallas_call(far_kernel, out_shape=jax.ShapeDtypeStruct((slots, points)...  181 us
    pallas_call x1, Pallas kernels, near_field(): pl.pallas_call(functools.partial(near_kernel, group, unroll), out_shape=j...  105 us
    ppermute x1, waiting for transfers between devices, from_behind(): return lax.ppermute(block, axis, route)  24 us
    unnamed x28, local copies, waits for them, and re-layouts  17.2 us
    all_to_all x1, starting transfers between devices, on_device(): received = lax.all_to_all(packed, AXES, 0, 0, tiled=True)  11.5 us
  transfers between devices with their start and end apart: 3, of which 1 were waited for; matrix products, arithmetic and copies ran while one was open for 4% of the time, Pallas kernels for 30%

profile of v1, /device:TPU:1, one launch (start us, length us, event | category | flops | bytes accessed | tf_op | source)
XLA Modules:
  0.0 363.5 jit_solution(5498757747669245945)
XLA Ops:
  0.6 0.8 copy.19.center
  1.5 1.7 copy.18.coords
  3.2 0.8 dynamic_slice.3.owner
  3.9 0.0 copy-start.4
  3.9 0.9 copy-done.4
  4.9 4.6 %pack.1 = (f32[128,5,8,128]{3,2,1,0:T(8,128)S(1)}, s32[512]{0:T(512)S(1)}) custom-call(s32[512]{0:T(512)S(1)} %dynamic_slice.3.owner, f32[512,3,128]{2,1,0:T(4,128)S(1)} %copy.18.coords, f32[512,128]{1,0:T(8,128)S(1)} %copy-done.4, f32[512,3]{1,0:T(8,128)S(1)} %copy.19.center), custom_call_target="tpu_custom_call" | custom-call | tf_op jit(solution)/shard_map/pack/pallas_call | solution.py:60
  9.5 0.0 copy-start
  9.5 1.5 copy-done
  11.0 0.0 copy-start.7
  11.0 0.0 copy-start.9
  11.0 0.0 copy-start.10
  11.0 0.0 copy-start.8
  11.0 11.5 %all-to-all-start.1 = ((f32[128,5,8,128]{3,2,1,0:T(8,128)}), f32[128,5,8,128]{3,2,1,0:T(8,128)S(1)}, u32[]{:S(2)}, u32[]{:S(2)}) async-start(f32[128,5,8,128]{3,2,1,0:T(8,128)} %copy-done), calls=%async_computation.1 | async-start | bytes 5242880 | tf_op jit(solution)/shard_map/all_to_all | solution.py:298
  22.5 0.0 copy-done.7
  22.6 0.6 slice.3
  23.2 3.3 collective-permute-start
  26.5 0.0 copy-done.9
  26.5 0.0 copy-done.10
  26.5 0.0 copy-done.8
  26.5 0.2 copy.22
  26.7 0.3 reshape.23.near_list
  27.0 1.3 copy.20.m2l
  28.3 0.0 copy-start.6
  28.3 4.0 %copy.21 = f32[1024,3,128]{2,1,0:T(4,128)} copy(f32[1024,3,128]{2,0,1:T(8,128)} %param.20) | data formatting | bytes 3145728 | tf_op args[9]
  32.3 24.0 %collective-permute-done = f32[16,296]{1,0:T(8,128)} collective-permute-done((f32[16,296]{1,0:T(8,128)}, f32[16,296]{1,0:T(8,128)}, u32[]{:S(2)}, u32[]{:S(2)}) %collective-permute-start) | collective-permute-done | bytes 18976 | tf_op jit(solution)/shard_map/ppermute | solution.py:26
  56.3 0.0 copy-done.6
  56.3 5.0 %fusion = f32[80,8,296]{2,0,1:T(8,128)S(1)} fusion(f32[8,296,296]{2,1,0:T(8,128)S(1)} %copy-done.6, f32[64,296]{1,0:T(8,128)S(1)} %copy-done.7, f32[16,296]{1,0:T(8,128)} %collective-permute-done), kind=kOutput, calls=%fused_computation.1 | convolution fusion | flops 672914560 | bytes 3656192 | tf_op jit(solution)/shard_map/pr,oqr->opq/dot_general | solution.py:302
  61.3 3.6 leaf_rows.1
  64.9 0.0 copy-start.2
  64.9 1.2 copy-done.2
  66.1 0.0 copy-start.3
  66.1 0.9 copy-done.3
  67.0 2.2 copy.23
  69.2 0.0 all-to-all-done.1.src
  69.2 6.0 %all-to-all-start = ((f32[128,8,296]{2,1,0:T(8,128)}), f32[128,8,296]{2,1,0:T(8,128)}, u32[]{:S(2)}, u32[]{:S(2)}) async-start(f32[128,8,296]{2,1,0:T(8,128)} %bitcast.13), calls=%async_computation | async-start | bytes 3145728 | tf_op jit(solution)/shard_map/all_to_all | solution.py:306
  75.3 0.0 copy-start.1
  75.3 1.6 copy-done.1
  76.9 104.7 %near_field.1.near = f32[1024,128]{1,0:T(8,128)S(1)} custom-call(s32[8192]{0:T(1024)S(1)} %reshape.23.near_list, f32[128,5,8,128]{3,2,1,0:T(8,128)S(1)} %all-to-all-done.1.src, f32[128,8,3,128]{3,2,1,0:T(4,128)S(1)} %bitcast.12), custom_call_target="tpu_custom_call" | custom-call | flops 34359738368 | bytes 8388608 | tf_op jit(solution)/shard_map/near_field/pallas_call | solution.py:201
  181.5 0.0 copy-start.5
  181.6 0.8 copy-done.5
  182.4 0.0 all-to-all-done
  182.4 181.1 %far_field.1 = f32[1024,128]{1,0:T(8,128)} custom-call(f32[1024,296]{1,0:T(8,128)} %bitcast.4.dens, f32[128,8,3,128]{3,2,1,0:T(4,128)} %bitcast.11, f32[1024,128]{1,0:T(8,128)} %copy-done.5), custom_call_target="tpu_custom_call" | custom-call | flops 155189248 | bytes 4194304 | tf_op jit(solution)/shard_map/far_field/pallas_call | solution.py:258
  (1 shorter events, 0.0 us)
Async XLA Ops:
  3.9 0.9 copy-start.4
  9.5 1.5 copy-start
  11.0 11.5 %copy-start.7 = (f32[64,296]{1,0:T(8,128)S(1)}, f32[64,296]{1,0:T(8,128)}, u32[]{:S(2)}) copy-start(f32[64,296]{1,0:T(8,128)} %param.11) | copy-start | bytes 227332
  11.0 15.4 %copy-start.9 = (s32[512]{0:T(512)S(1)}, s32[512]{0:T(512)}, u32[]{:S(2)}) copy-start(s32[512]{0:T(512)} %param.12) | copy-start | bytes 6148
  11.0 15.4 %copy-start.10 = (s32[512]{0:T(512)S(1)}, s32[512]{0:T(512)}, u32[]{:S(2)}) copy-start(s32[512]{0:T(512)} %param.13) | copy-start | bytes 6148
  11.0 15.5 %copy-start.8 = (s32[1024,8]{0,1:T(8,128)S(1)}, s32[1024,8]{0,1:T(8,128)}, u32[]{:S(2)}) copy-start(s32[1024,8]{0,1:T(8,128)} %param.21) | copy-start | bytes 98308
  11.0 58.2 %all-to-all-start.1 = ((f32[128,5,8,128]{3,2,1,0:T(8,128)}), f32[128,5,8,128]{3,2,1,0:T(8,128)S(1)}, u32[]{:S(2)}, u32[]{:S(2)}) async-start(f32[128,5,8,128]{3,2,1,0:T(8,128)} %copy-done), calls=%async_computation.1 | async-start | bytes 5242880 | tf_op jit(solution)/shard_map/all_to_all | solution.py:298
  23.2 33.2 %collective-permute-start = (f32[16,296]{1,0:T(8,128)}, f32[16,296]{1,0:T(8,128)}, u32[]{:S(2)}, u32[]{:S(2)}) collective-permute-start(f32[16,296]{1,0:T(8,128)} %slice.3), channel_id=1, source_target_pairs={{0,1},{1,2},{2,3},{3,4},{4,5},{5,6},{6,7},{7,8},{8,9},{9,10},{10,1... | collective-permute-start | bytes 56840 | tf_op jit(solution)/shard_map/ppermute | solution.py:26
  28.3 28.0 %copy-start.6 = (f32[8,296,296]{2,1,0:T(8,128)S(1)}, f32[8,296,296]{2,1,0:T(8,128)}, u32[]{:S(2)}) copy-start(f32[8,296,296]{2,1,0:T(8,128)} %param.15) | copy-start | bytes 8411140
  64.9 1.2 copy-start.2
  66.1 0.9 copy-start.3
  69.2 113.1 %all-to-all-start = ((f32[128,8,296]{2,1,0:T(8,128)}), f32[128,8,296]{2,1,0:T(8,128)}, u32[]{:S(2)}, u32[]{:S(2)}) async-start(f32[128,8,296]{2,1,0:T(8,128)} %bitcast.13), calls=%async_computation | async-start | bytes 3145728 | tf_op jit(solution)/shard_map/all_to_all | solution.py:306
  75.3 1.6 copy-start.1
  181.5 0.8 copy-start.5

commit v2 on v1

--- a/solution.py
+++ b/solution.py
@@ -3,6 +3,7 @@
 
 import jax
 import jax.numpy as jnp
+import ml_dtypes
 import numpy as np
 from jax import lax
 from jax.experimental import pallas as pl
@@ -71,34 +72,34 @@
     )(owner, coords, charge, center)
 
 
-def leaf_kernel(which, dest, stacked, m2l, leaf, dens):
-    leaves = m2l.shape[0]
+def leaf_kernel(which, stacked, m2l, leaf, dens):
+    leaves, width = m2l.shape
     dens[...] = jnp.zeros_like(dens)
 
     def place(j, carry):
         row = m2l[pl.ds(j, 1), :] + stacked[pl.ds(which[j], 1), :]
         leaf[pl.ds(j, 1), :] = row
-        dens[pl.ds(dest[j], 1), :] = row
+        dens[pl.ds(j, 1), 0:width] = row
         return carry
 
     lax.fori_loop(0, leaves, place, 0, unroll=8)
 
 
-def leaf_rows(which, dest, stacked, m2l, slots):
-    width = m2l.shape[1]
+def leaf_rows(which, stacked, m2l, padded):
     vmem = pl.BlockSpec(memory_space=pltpu.VMEM)
     smem = pl.BlockSpec(memory_space=pltpu.SMEM)
     return pl.pallas_call(
         leaf_kernel,
         out_shape=(
             jax.ShapeDtypeStruct(m2l.shape, F32),
-            jax.ShapeDtypeStruct((slots, width), F32),
-        ),
-        in_specs=[smem, smem, vmem, vmem],
+            jax.ShapeDtypeStruct((m2l.shape[0], padded), F32),
+        ),
+        in_specs=[smem, vmem, vmem],
         out_specs=(vmem, vmem),
         compiler_params=pltpu.CompilerParams(vmem_limit_bytes=24 << 20),
+        cost_estimate=pl.CostEstimate(flops=1 << 18, bytes_accessed=8 << 20, transcendentals=0),
         name="leaf_rows",
-    )(which, dest, stacked, m2l)
+    )(which, stacked, m2l)
 
 
 def split3(v):
@@ -108,12 +109,12 @@
     return high, middle, rest - middle
 
 
-def target_features(x, y, z):
+def target_features(x, y, z, extra):
     out = []
     for v in (x, y, z):
         h, m, l = split3(v)
         out += [h, h, h, m, m, l]
-    return out + list(split3(x * x + y * y + z * z + SOFT_SQ))
+    return out + list(split3(x * x + y * y + z * z + extra))
 
 
 def source_features(x, y, z):
@@ -160,9 +161,10 @@
             local = i * unroll + u
             block = step * group + local
             info = src[block, 4]
-            shift = off[local]
-            place = [(info[:, c : c + 1] - 1.0) + HALF * shift[:, c] for c in range(3)]
-            for f, v in enumerate(target_features(*place)):
+            place = [
+                (info[:, c : c + 1] - 1.0) + HALF * off[c, pl.ds(local * 8, 8), :] for c in range(3)
+            ]
+            for f, v in enumerate(target_features(*place, SOFT_SQ)):
                 tfeat[u, 8 * f : 8 * f + 8] = v
             for s in range(8):
                 feat = tfeat[u, pl.ds(s, FEATURES, stride=8), :]
@@ -195,7 +197,7 @@
     lax.fori_loop(0, group // unroll, rows, 0)
 
 
-def near_field(src, offsets, near_slots, group=16, unroll=2):
+def near_field(src, offsets, near_slots, group=16, unroll=4):
     senders, _, cap, _ = src.shape
     slots = senders * cap
     return pl.pallas_call(
@@ -206,7 +208,7 @@
             grid=(senders // group,),
             in_specs=[
                 pl.BlockSpec(src.shape, lambda g, n: (0, 0, 0, 0)),
-                pl.BlockSpec((group, cap, 3, 128), lambda g, n: (g, 0, 0, 0)),
+                pl.BlockSpec((3, group * cap, 128), lambda g, n: (0, g, 0)),
             ],
             out_specs=pl.BlockSpec((group * cap, 128), lambda g, n: (g, 0)),
             scratch_shapes=[
@@ -224,54 +226,102 @@
     )(near_slots, src, offsets)
 
 
-def far_kernel(dens, off, near, out):
-    grid = [float(v) for v in (np.linspace(-1.0, 1.0, ORDER) * RADIUS).astype(np.float32)]
-    edge = (0, ORDER - 1)
-
-    def block(i, carry):
-        shift = off[i]
-        axis_sq = []
-        for c in range(3):
-            o = shift[:, c]
-            axis_sq.append([(o - v) * (o - v) for v in grid])
-        weights = dens[pl.ds(i * 8, 8), :]
-        sums = [None] * 4
-        q = 0
-        for a in range(ORDER):
-            for b in range(ORDER):
-                plane = axis_sq[0][a] + axis_sq[1][b]
-                last = range(ORDER) if a in edge or b in edge else edge
-                for c in last:
-                    term = weights[:, q : q + 1] * lax.rsqrt(plane + axis_sq[2][c])
-                    sums[q % 4] = term if sums[q % 4] is None else sums[q % 4] + term
-                    q += 1
-        total = (sums[0] + sums[1]) + (sums[2] + sums[3])
-        out[pl.ds(i * 8, 8), :] = near[pl.ds(i * 8, 8), :] + total * (0.25 / (math.pi * HALF))
-        return carry
-
-    lax.fori_loop(0, off.shape[0], block, 0)
-
-
-def far_field(dens, offsets, near, group=32):
-    senders, cap, _, points = offsets.shape
-    slots, width = dens.shape
+def surface_weights():
+    grid = np.linspace(-1.0, 1.0, ORDER)
+    points = np.stack(np.meshgrid(grid, grid, grid, indexing="ij"), 0).reshape(3, -1)
+    on_surface = np.max(np.abs(points), axis=0) > 1.0 - 1e-09
+    points = (points[:, on_surface] * RADIUS).astype(np.float32)
+    fill = 320 - points.shape[1]
+    points = np.concatenate([points, np.repeat(points[:, :1], fill, axis=1)], axis=1)
+
+    def split(v):
+        high = v.astype(ml_dtypes.bfloat16).astype(np.float32)
+        rest = v - high
+        middle = rest.astype(ml_dtypes.bfloat16).astype(np.float32)
+        return high, middle, rest - middle
+
+    rows = []
+    for c in range(3):
+        h, m, l = split(-2.0 * points[c])
+        rows += [h, m, l, h, m, h]
+    rows += [np.ones(320, np.float32)] * 3
+    rows += list(split(np.sum(points * points, axis=0)))
+    rows += [np.zeros(320, np.float32)] * (FEATURES - len(rows))
+    rows = np.stack(rows)
+    main = np.repeat(rows[:, :256], 8, axis=0)
+    last = np.zeros((FEATURES, 8, 512), np.float32)
+    for s in range(8):
+        last[:, s, 64 * s : 64 * s + 64] = rows[:, 256:]
+    last = last.reshape(FEATURES * 8, 512)
+    return main.astype(ml_dtypes.bfloat16), last.astype(ml_dtypes.bfloat16)
+
+
+def far_kernel(unroll, dest, off, dens, main, last, out, tfeat, shift):
+    ones = jnp.ones((8, 128), F32)
+    zeros = jnp.zeros((8, 128), F32)
+    out[...] = jnp.zeros_like(out)
+    for u in range(unroll):
+        for f in range(21, 24):
+            tfeat[u, 8 * f : 8 * f + 8] = ones
+        for f in range(24, FEATURES):
+            tfeat[u, 8 * f : 8 * f + 8] = zeros
+    row_of_lane = lax.broadcasted_iota(jnp.int32, (128, 8 * FEATURES), 1) % 8
+    low_half = lax.broadcasted_iota(jnp.int32, (1, 128), 1) < 64
+
+    def rows(i, carry):
+        for u in range(unroll):
+            first = (i * unroll + u) * 8
+            at = [dest[first + t] for t in range(8)]
+            for t in range(8):
+                for c in range(3):
+                    shift[u, c, t : t + 1, :] = off[at[t] // 8, c, pl.ds(at[t] % 8, 1), :]
+            for f, v in enumerate(target_features(*(shift[u, c] for c in range(3)), 0.0)):
+                tfeat[u, 8 * f : 8 * f + 8] = v
+            turned = tfeat[u].astype(BF16).T
+            weights = [dens[pl.ds(first + t, 1), :] for t in range(8)]
+            tail_sq = jnp.dot(turned, last[...], preferred_element_type=F32)
+            for p in range(4):
+                pair = jnp.where(
+                    low_half,
+                    weights[2 * p][:, 256:384],
+                    pltpu.roll(weights[2 * p + 1][:, 256:384], 64, 1),
+                )
+                tail = lax.rsqrt(tail_sq[:, 128 * p : 128 * p + 128]) * pair
+                for h in range(2):
+                    t = 2 * p + h
+                    left = jnp.where(row_of_lane == t, turned, jnp.zeros_like(turned))
+                    dist_sq = jnp.dot(left, main[...], preferred_element_type=F32)
+                    total = lax.rsqrt(dist_sq[:, :128]) * weights[t][:, :128]
+                    total = total + lax.rsqrt(dist_sq[:, 128:]) * weights[t][:, 128:256]
+                    total = total + jnp.where(low_half == (h == 0), tail, 0.0)
+                    line = jnp.sum(total.T, axis=0, keepdims=True)
+                    out[pl.ds(at[t], 1), :] = line * (0.25 / (math.pi * HALF))
+        return carry
+
+    lax.fori_loop(0, dens.shape[0] // (8 * unroll), rows, 0)
+
+
+def far_field(dest, offsets, dens, unroll=4):
+    devices, _, cap, points = offsets.shape
+    main, last = surface_weights()
+    vmem = pl.BlockSpec(memory_space=pltpu.VMEM)
     return pl.pallas_call(
-        far_kernel,
-        out_shape=jax.ShapeDtypeStruct((slots, points), F32),
-        grid=(senders // group,),
-        in_specs=[
-            pl.BlockSpec((group * cap, width), lambda g: (g, 0)),
-            pl.BlockSpec((group, cap, 3, points), lambda g: (g, 0, 0, 0)),
-            pl.BlockSpec((group * cap, points), lambda g: (g, 0)),
+        functools.partial(far_kernel, unroll),
+        out_shape=jax.ShapeDtypeStruct((devices * cap, points), F32),
+        in_specs=[pl.BlockSpec(memory_space=pltpu.SMEM)] + [vmem] * 4,
+        out_specs=vmem,
+        scratch_shapes=[
+            pltpu.VMEM((unroll, FEATURES * 8, 128), F32),
+            pltpu.VMEM((unroll, 3, 8, 128), F32),
         ],
-        out_specs=pl.BlockSpec((group * cap, points), lambda g: (g, 0)),
+        compiler_params=pltpu.CompilerParams(vmem_limit_bytes=24 << 20),
         cost_estimate=pl.CostEstimate(
-            flops=4 * slots * points * width,
+            flops=2 * dens.shape[0] * 128 * 256 * 384,
             bytes_accessed=4 << 20,
-            transcendentals=slots * points * width,
+            transcendentals=dens.shape[0] * 128 * 320,
         ),
         name="far_field",
-    )(dens, offsets, near)
+    )(dest, offsets, dens, jnp.asarray(main), jnp.asarray(last))
 
 
 def on_device(
@@ -294,21 +344,26 @@
     me = lax.axis_index(AXES)
     mine = lax.dynamic_slice_in_dim(obs_owner, me * leaf_dev, leaf_dev)
 
+    rim = from_behind(parent_local[parent_local.shape[0] - RIM :], AXES, 1)
     packed, dest = pack(mine, src_coords, src_charge, leaf_center, devices, cap)
+
+    offsets = jnp.transpose(obs_offset, (1, 0, 2))
+    outgoing = jnp.transpose(offsets.reshape(3, devices, cap, points), (1, 0, 2, 3))
+    outgoing, rim = lax.optimization_barrier((outgoing, rim))
+    at_leaves = lax.all_to_all(outgoing, AXES, 0, 0, tiled=True)
     received = lax.all_to_all(packed, AXES, 0, 0, tiled=True)
 
-    rim = from_behind(parent_local[parent_local.shape[0] - RIM :], AXES, 1)
     parents = jnp.concatenate([rim, parent_local], axis=0)
     moved = jnp.einsum("pr,oqr->opq", parents, l2l_ops, precision=lax.Precision.HIGHEST)
     stacked = moved.reshape(l2l_ops.shape[0] * parents.shape[0], width)
     which = child_octant * parents.shape[0] + parent_slot
-    leaf_local, dens = leaf_rows(which, dest, stacked, child_m2l, slots)
-    dens = lax.all_to_all(dens.reshape(devices, cap, width), AXES, 0, 0, tiled=True)
-
-    offsets = obs_offset.reshape(devices, cap, 3, points)
+    leaf_local, dens = leaf_rows(which, stacked, child_m2l, 384)
+    far = far_field(dest, at_leaves, dens)
+    received, far = lax.optimization_barrier((received, far))
+    far = lax.all_to_all(far.reshape(devices, cap, points), AXES, 0, 0, tiled=True)
+
     near = near_field(received, offsets, near_slots.reshape(-1))
-    potential = far_field(dens.reshape(slots, width), offsets, near)
-    return (leaf_local, potential)
+    return (leaf_local, near + far.reshape(slots, points))
 
 
 def solution(mesh):

time: 364 us -> 200 us (0.55)
  Pallas kernels: 294 us -> 123 us
  starting transfers between devices: 20.8 us -> 26.8 us
  waiting for transfers between devices: 24 us -> 18.5 us
    pallas_call x1, Pallas kernels: 181 us -> 21.1 us  [far_field(): pl.pallas_call(functools.partial(far_kernel, unroll), out_shape=jax.Shape...]
    ppermute x1, waiting for transfers between devices: 24 us -> 3.23 us  [from_behind(): return lax.ppermute(block, axis, route)]
    all_to_all x1 -> x2, waiting for transfers between devices: 0.01 us -> 15.3 us  [the longest x1 15.3 us: on_device(): at_leaves = lax.all_to_all(outgoing, AXES, 0, 0, tiled=True)]
    all_to_all x1 -> x2, starting transfers between devices: 6.01 us -> 17.9 us  [the longest x1 10.4 us: on_device(): lax.all_to_all(far.reshape(devices, cap, points), AXES, 0, 0, tiled=True)]
    pallas_call x1, Pallas kernels: 105 us -> 94.5 us  [near_field(): pl.pallas_call(functools.partial(near_kernel, group, unroll), out_shape=j...]
    all_to_all x1, starting transfers between devices: 11.5 us -> 4.99 us  [on_device(): received = lax.all_to_all(packed, AXES, 0, 0, tiled=True)]
    unnamed x28 -> x35, local copies, waits for them, and re-layouts: 17.2 us -> 16.7 us
  transfers between devices with their start and end apart: 3 -> 4, of which waited for: 1 -> 2; matrix products, arithmetic and copies ran while one was open for 4% -> 9% of each run, Pallas kernels for 30% -> 62%
where the time goes in v2:
time: 200 us; the launch traced here: 199 us
  Pallas kernels  123 us (62%)
  starting transfers between devices  26.8 us (13%)
  local copies, waits for them, and re-layouts  22.1 us (11%)
  waiting for transfers between devices  18.5 us (9%)
  matrix products  6.25 us (3%)
    pallas_call x1, Pallas kernels, near_field(): pl.pallas_call(functools.partial(near_kernel, group, unroll), out_shape=j...  94.5 us
    pallas_call x1, Pallas kernels, far_field(): pl.pallas_call(functools.partial(far_kernel, unroll), out_shape=jax.Shape...  21.1 us
    unnamed x35, local copies, waits for them, and re-layouts  16.7 us
    all_to_all x1, waiting for transfers between devices, on_device(): at_leaves = lax.all_to_all(outgoing, AXES, 0, 0, tiled=True)  15.3 us
    all_to_all x1, starting transfers between devices, on_device(): lax.all_to_all(far.reshape(devices, cap, points), AXES, 0, 0, tiled=True)  10.4 us
    all_to_all x1, starting transfers between devices, on_device(): at_leaves = lax.all_to_all(outgoing, AXES, 0, 0, tiled=True)  7.49 us
    dot_general x1, matrix products, on_device(): jnp.einsum('pr,oqr->opq', parents, l2l_ops, precision=lax.Precision.HIGHEST)  6.25 us
    all_to_all x1, starting transfers between devices, on_device(): received = lax.all_to_all(packed, AXES, 0, 0, tiled=True)  4.99 us
  transfers between devices with their start and end apart: 4, of which 2 were waited for; matrix products, arithmetic and copies ran while one was open for 9% of the time, Pallas kernels for 62%

profile of v2, /device:TPU:1, one launch (start us, length us, event | category | flops | bytes accessed | tf_op | source)
XLA Modules:
  0.0 199.5 jit_solution(13499972441017108257)
XLA Ops:
  0.6 0.7 slice.3
  1.4 3.9 %collective-permute-start = (f32[16,296]{1,0:T(8,128)S(1)}, f32[16,296]{1,0:T(8,128)}, u32[]{:S(2)}, u32[]{:S(2)}) collective-permute-start(f32[16,296]{1,0:T(8,128)S(1)} %slice.3), channel_id=1, source_target_pairs={{0,1},{1,2},{2,3},{3,4},{4,5},{5,6},{6,7},{7,8},{8,9},{9,10},{10,1... | collective-permute-start | bytes 56840 | tf_op jit(solution)/shard_map/ppermute | solution.py:27
  5.3 2.6 %copy_bitcast_fusion = f32[128,3,8,128]{3,2,1,0:T(8,128)} fusion(f32[1024,3,128]{2,0,1:T(8,128)} %param.22), kind=kLoop, calls=%fused_computation | loop fusion | bytes 3145728 | tf_op jit(solution)/shard_map/transpose | solution.py:351
  8.0 3.2 %collective-permute-done = f32[16,296]{1,0:T(8,128)} collective-permute-done((f32[16,296]{1,0:T(8,128)S(1)}, f32[16,296]{1,0:T(8,128)}, u32[]{:S(2)}, u32[]{:S(2)}) %collective-permute-start) | collective-permute-done | bytes 18976 | tf_op jit(solution)/shard_map/ppermute | solution.py:27
  11.2 7.5 %all-to-all-start.1 = ((f32[128,3,8,128]{3,2,1,0:T(8,128)}), f32[128,3,8,128]{3,2,1,0:T(8,128)S(1)}, u32[]{:S(2)}, u32[]{:S(2)}) async-start(f32[128,3,8,128]{3,2,1,0:T(8,128)} %copy_bitcast_fusion), calls=%async_computation.1 | async-start | bytes 3145728 | tf_op jit(solution)/shard_map/all_to_all | solution.py:353
  18.7 0.0 copy-start.12
  18.7 0.0 copy-start.5
  18.7 1.7 copy.23.coords
  20.4 0.0 copy-done.12
  20.5 0.1 copy.24.center
  20.6 0.8 dynamic_slice.3.owner
  21.4 0.0 copy-done.5
  21.4 4.6 %pack.1 = (f32[128,5,8,128]{3,2,1,0:T(8,128)S(1)}, s32[512]{0:T(512)S(1)}) custom-call(s32[512]{0:T(512)S(1)} %dynamic_slice.3.owner, f32[512,3,128]{2,1,0:T(4,128)S(1)} %copy.23.coords, f32[512,128]{1,0:T(8,128)S(1)} %copy-done.5, f32[512,3]{1,0:T(8,128)S(1)} %copy.24.center), custom_call_target="tpu_custom_call" | custom-call | tf_op jit(solution)/shard_map/pack/pallas_call | solution.py:61
  26.0 0.0 copy-start
  26.0 1.5 copy-done
  27.5 15.3 %all-to-all-done.1.off = f32[128,3,8,128]{3,2,1,0:T(8,128)S(1)} async-done(((f32[128,3,8,128]{3,2,1,0:T(8,128)}), f32[128,3,8,128]{3,2,1,0:T(8,128)S(1)}, u32[]{:S(2)}, u32[]{:S(2)}) %all-to-all-start.1) | async-done | bytes 1572896 | tf_op jit(solution)/shard_map/all_to_all | solution.py:353
  42.8 0.0 copy-start.2
  42.8 1.1 copy-done.2
  43.9 0.0 copy-start.11
  43.9 5.0 %all-to-all-start = ((f32[128,5,8,128]{3,2,1,0:T(8,128)}), f32[128,5,8,128]{3,2,1,0:T(8,128)S(1)}, u32[]{:S(2)}, u32[]{:S(2)}) async-start(f32[128,5,8,128]{3,2,1,0:T(8,128)} %copy-done), calls=%async_computation | async-start | bytes 5242880 | tf_op jit(solution)/shard_map/all_to_all | solution.py:354
  48.9 0.0 copy-start.13
  48.9 0.0 copy-start.14
  49.0 0.0 copy-start.10
  49.0 1.4 copy.21.m2l
  50.3 0.0 copy-done.11
  50.4 1.0 copy.22
  51.4 1.3 reshape.21.near_list
  52.6 0.0 copy-done.13
  52.6 0.0 copy-done.14
  52.6 0.0 copy-done.10
  52.7 6.3 %fusion = f32[80,8,296]{2,0,1:T(8,128)S(1)} fusion(f32[8,296,296]{2,1,0:T(8,128)} %param.17, f32[64,296]{1,0:T(8,128)S(1)} %copy-done.10, f32[16,296]{1,0:T(8,128)} %collective-permute-done), kind=kOutput, calls=%fused_computation.3 | convolution fusion | flops 672914560 | bytes 3656192 | tf_op jit(solution)/shard_map/pr,oqr->opq/dot_general | solution.py:357
  58.9 2.9 %leaf_rows.1 = (f32[512,296]{1,0:T(8,128)S(1)}, f32[512,384]{1,0:T(8,128)S(1)}) custom-call(s32[512]{0:T(512)S(1)} %multiply_add_fusion.which, f32[640,296]{1,0:T(8,128)S(1)} %bitcast.17, f32[512,296]{1,0:T(8,128)S(1)} %copy.21.m2l), custom_call_target="tpu_custom_call" | custom-call | flops 262144 | bytes 8388608 | tf_op jit(solution)/shard_map/leaf_rows/pallas_call | solution.py:91
  61.8 0.0 copy-start.4
  61.8 0.9 copy-done.4
  62.7 0.0 copy-start.6
  62.7 0.9 copy-done.6
  63.6 2.2 %copy.25 = f32[512,296]{0,1:T(8,128)} copy(f32[512,296]{1,0:T(8,128)} %copy-done.4) | data formatting | bytes 1212416
  65.8 0.0 copy-start.3
  65.8 1.4 copy-done.3
  67.2 0.0 copy-start.7
  67.2 1.1 copy-done.7
  68.3 0.0 copy-start.8
  68.3 0.9 copy-done.8
  69.3 0.0 copy-start.9
  69.3 0.9 copy-done.9
  70.2 21.1 %far_field.1 = f32[1024,128]{1,0:T(8,128)} custom-call(s32[512]{0:T(512)S(1)} %get-tuple-element.13.dest, f32[128,3,8,128]{3,2,1,0:T(8,128)S(1)} %copy-done.3, f32[512,384]{1,0:T(8,128)S(1)} %copy-done.7, bf16[256,256]{1,0:T(8,128)(2,1)S(1)} %copy-done.9, bf16[256,512]{1,0:T(8,128)(2,1)S(1)} %copy-done.8), custom_call_target="tpu_custom_call" | custom-call | flops 12884901888 | bytes 4194304 | tf_op jit(solution)/shard_map/far_field/pallas_call | solution.py:308
  91.3 0.0 all-to-all-done.src
  91.3 10.4 %all-to-all-start.2 = ((f32[128,8,128]{2,1,0:T(8,128)}), f32[128,8,128]{2,1,0:T(8,128)}, u32[]{:S(2)}, u32[]{:S(2)}) async-start(f32[128,8,128]{2,1,0:T(8,128)} %bitcast.6), calls=%async_computation.2 | async-start | bytes 1048576 | tf_op jit(solution)/shard_map/all_to_all | solution.py:363
  101.7 0.0 copy-start.1
  101.7 1.4 copy-done.1
  103.1 94.5 %near_field.1 = f32[1024,128]{1,0:T(8,128)S(1)} custom-call(s32[8192]{0:T(1024)S(1)} %reshape.21.near_list, f32[128,5,8,128]{3,2,1,0:T(8,128)S(1)} %all-to-all-done.src, f32[3,1024,128]{2,1,0:T(8,128)S(1)} %bitcast.18), custom_call_target="tpu_custom_call" | custom-call | flops 34359738368 | bytes 8388608 | tf_op jit(solution)/shard_map/near_field/pallas_call | solution.py:203
  197.6 0.0 all-to-all-done.2
  197.6 1.9 bitcast_add_fusion
  (1 shorter events, 0.0 us)
Async XLA Ops:
  1.4 9.8 %collective-permute-start = (f32[16,296]{1,0:T(8,128)S(1)}, f32[16,296]{1,0:T(8,128)}, u32[]{:S(2)}, u32[]{:S(2)}) collective-permute-start(f32[16,296]{1,0:T(8,128)S(1)} %slice.3), channel_id=1, source_target_pairs={{0,1},{1,2},{2,3},{3,4},{4,5},{5,6},{6,7},{7,8},{8,9},{9,10},{10,1... | collective-permute-start | bytes 56840 | tf_op jit(solution)/shard_map/ppermute | solution.py:27
  11.2 31.6 %all-to-all-start.1 = ((f32[128,3,8,128]{3,2,1,0:T(8,128)}), f32[128,3,8,128]{3,2,1,0:T(8,128)S(1)}, u32[]{:S(2)}, u32[]{:S(2)}) async-start(f32[128,3,8,128]{3,2,1,0:T(8,128)} %copy_bitcast_fusion), calls=%async_computation.1 | async-start | bytes 3145728 | tf_op jit(solution)/shard_map/all_to_all | solution.py:353
  18.7 1.8 copy-start.12
  18.7 2.7 %copy-start.5 = (f32[512,128]{1,0:T(8,128)S(1)}, f32[512,128]{1,0:T(8,128)}, u32[]{:S(2)}) copy-start(f32[512,128]{1,0:T(8,128)} %charge.1) | copy-start | bytes 786436
  26.0 1.5 copy-start
  42.8 1.1 copy-start.2
  43.9 6.4 %copy-start.11 = (s32[1024,8]{0,1:T(8,128)S(1)}, s32[1024,8]{0,1:T(8,128)}, u32[]{:S(2)}) copy-start(s32[1024,8]{0,1:T(8,128)} %param.23) | copy-start | bytes 98308
  43.9 47.3 %all-to-all-start = ((f32[128,5,8,128]{3,2,1,0:T(8,128)}), f32[128,5,8,128]{3,2,1,0:T(8,128)S(1)}, u32[]{:S(2)}, u32[]{:S(2)}) async-start(f32[128,5,8,128]{3,2,1,0:T(8,128)} %copy-done), calls=%async_computation | async-start | bytes 5242880 | tf_op jit(solution)/shard_map/all_to_all | solution.py:354
  48.9 3.7 %copy-start.13 = (s32[512]{0:T(512)S(1)}, s32[512]{0:T(512)}, u32[]{:S(2)}) copy-start(s32[512]{0:T(512)} %param.14) | copy-start | bytes 6148
  48.9 3.7 %copy-start.14 = (s32[512]{0:T(512)S(1)}, s32[512]{0:T(512)}, u32[]{:S(2)}) copy-start(s32[512]{0:T(512)} %param.15) | copy-start | bytes 6148
  49.0 3.7 %copy-start.10 = (f32[64,296]{1,0:T(8,128)S(1)}, f32[64,296]{1,0:T(8,128)}, u32[]{:S(2)}) copy-start(f32[64,296]{1,0:T(8,128)} %param.13) | copy-start | bytes 227332
  61.8 0.9 copy-start.4
  62.7 0.9 copy-start.6
  65.8 1.4 copy-start.3
  67.2 1.1 copy-start.7
  68.3 0.9 copy-start.8
  69.3 0.9 copy-start.9
  91.3 106.3 %all-to-all-start.2 = ((f32[128,8,128]{2,1,0:T(8,128)}), f32[128,8,128]{2,1,0:T(8,128)}, u32[]{:S(2)}, u32[]{:S(2)}) async-start(f32[128,8,128]{2,1,0:T(8,128)} %bitcast.6), calls=%async_computation.2 | async-start | bytes 1048576 | tf_op jit(solution)/shard_map/all_to_all | solution.py:363
  101.7 1.4 copy-start.1

commit v3 on v2

--- a/solution.py
+++ b/solution.py
@@ -29,7 +29,7 @@
 
 def pack_kernel(capacity, owner, coords, charge, center, out, dest, count, tail):
     devices = out.shape[0]
-    leaves = coords.shape[0]
+    leaves = charge.shape[0]
     out[...] = jnp.zeros_like(out)
     tail[:, 0:3] = center[...]
     tail[:, 3:4] = jnp.ones((leaves, 1), F32)
@@ -45,9 +45,8 @@
         rank = count[o]
         count[o] = rank + 1
         dest[j] = o * capacity + rank
-        row = coords[j]
         for c in range(3):
-            out[o, c, pl.ds(rank, 1), :] = row[c : c + 1]
+            out[o, c, pl.ds(rank, 1), :] = coords[c, pl.ds(j, 1), :]
         out[o, 3, pl.ds(rank, 1), :] = charge[pl.ds(j, 1), :]
         out[o, 4, pl.ds(rank, 1), 0:4] = tail[pl.ds(j, 1), :]
         return carry
@@ -56,7 +55,7 @@
 
 
 def pack(owner, coords, charge, center, devices, capacity):
-    leaves = coords.shape[0]
+    leaves = charge.shape[0]
     vmem = pl.BlockSpec(memory_space=pltpu.VMEM)
     return pl.pallas_call(
         functools.partial(pack_kernel, capacity),
@@ -67,7 +66,7 @@
         in_specs=[pl.BlockSpec(memory_space=pltpu.SMEM), vmem, vmem, vmem],
         out_specs=(vmem, pl.BlockSpec(memory_space=pltpu.SMEM)),
         scratch_shapes=[pltpu.SMEM((devices,), jnp.int32), pltpu.VMEM((leaves, 4), F32)],
-        compiler_params=pltpu.CompilerParams(vmem_limit_bytes=24 << 20),
+        compiler_params=pltpu.CompilerParams(vmem_limit_bytes=14 << 20),
         name="pack",
     )(owner, coords, charge, center)
 
@@ -96,7 +95,7 @@
         ),
         in_specs=[smem, vmem, vmem],
         out_specs=(vmem, vmem),
-        compiler_params=pltpu.CompilerParams(vmem_limit_bytes=24 << 20),
+        compiler_params=pltpu.CompilerParams(vmem_limit_bytes=14 << 20),
         cost_estimate=pl.CostEstimate(flops=1 << 18, bytes_accessed=8 << 20, transcendentals=0),
         name="leaf_rows",
     )(which, stacked, m2l)
@@ -128,6 +127,7 @@
 def near_kernel(group, unroll, near_list, src, off, out, table, charges, tfeat, sfeat):
     step = pl.program_id(0)
     senders, _, cap, _ = src.shape
+    slots = senders * cap
     ones = jnp.ones((8, 128), F32)
     zeros = jnp.zeros((8, 128), F32)
 
@@ -173,7 +173,7 @@
                     [jnp.where(lane_part == k, turned, jnp.zeros_like(turned)) for k in range(4)],
                     axis=0,
                 )
-                at = [near_list[(block * 8 + s) * 8 + j] for j in range(8)]
+                at = [near_list[j * slots + block * 8 + s] for j in range(8)]
                 right = jnp.concatenate(
                     [
                         jnp.concatenate([table[at[2 * k]], table[at[2 * k + 1]]], axis=1)
@@ -218,7 +218,7 @@
                 pltpu.VMEM((FEATURES * 8, 128), F32),
             ],
         ),
-        compiler_params=pltpu.CompilerParams(vmem_limit_bytes=40 << 20),
+        compiler_params=pltpu.CompilerParams(vmem_limit_bytes=28 << 20),
         cost_estimate=pl.CostEstimate(
             flops=2 * slots * 512 * 128 * 256, bytes_accessed=8 << 20, transcendentals=slots << 17
         ),
@@ -314,7 +314,7 @@
             pltpu.VMEM((unroll, FEATURES * 8, 128), F32),
             pltpu.VMEM((unroll, 3, 8, 128), F32),
         ],
-        compiler_params=pltpu.CompilerParams(vmem_limit_bytes=24 << 20),
+        compiler_params=pltpu.CompilerParams(vmem_limit_bytes=14 << 20),
         cost_estimate=pl.CostEstimate(
             flops=2 * dens.shape[0] * 128 * 256 * 384,
             bytes_accessed=4 << 20,
@@ -345,24 +345,25 @@
     mine = lax.dynamic_slice_in_dim(obs_owner, me * leaf_dev, leaf_dev)
 
     rim = from_behind(parent_local[parent_local.shape[0] - RIM :], AXES, 1)
-    packed, dest = pack(mine, src_coords, src_charge, leaf_center, devices, cap)
+    packed, dest = pack(mine, jnp.transpose(src_coords, (1, 0, 2)), src_charge, leaf_center, devices, cap)
 
     offsets = jnp.transpose(obs_offset, (1, 0, 2))
     outgoing = jnp.transpose(offsets.reshape(3, devices, cap, points), (1, 0, 2, 3))
     outgoing, rim = lax.optimization_barrier((outgoing, rim))
     at_leaves = lax.all_to_all(outgoing, AXES, 0, 0, tiled=True)
-    received = lax.all_to_all(packed, AXES, 0, 0, tiled=True)
 
     parents = jnp.concatenate([rim, parent_local], axis=0)
     moved = jnp.einsum("pr,oqr->opq", parents, l2l_ops, precision=lax.Precision.HIGHEST)
     stacked = moved.reshape(l2l_ops.shape[0] * parents.shape[0], width)
     which = child_octant * parents.shape[0] + parent_slot
     leaf_local, dens = leaf_rows(which, stacked, child_m2l, 384)
+    packed, dens = lax.optimization_barrier((packed, dens))
+    received = lax.all_to_all(packed, AXES, 0, 0, tiled=True)
     far = far_field(dest, at_leaves, dens)
     received, far = lax.optimization_barrier((received, far))
     far = lax.all_to_all(far.reshape(devices, cap, points), AXES, 0, 0, tiled=True)
 
-    near = near_field(received, offsets, near_slots.reshape(-1))
+    near = near_field(received, offsets, jnp.transpose(near_slots).reshape(-1))
     return (leaf_local, near + far.reshape(slots, points))
 
 

time: 200 us -> 188 us (0.940)
  local copies, waits for them, and re-layouts: 22.1 us -> 15.6 us
  starting transfers between devices: 26.8 us -> 21.6 us
  Pallas kernels: 123 us -> 125 us
    all_to_all x1, waiting for transfers between devices: 15.3 us -> 5.14 us  [on_device(): at_leaves = lax.all_to_all(outgoing, AXES, 0, 0, tiled=True)]
    all_to_all x1, waiting for transfers between devices: 0.01 us -> 8.41 us  [on_device(): received = lax.all_to_all(packed, AXES, 0, 0, tiled=True)]
    unnamed x35 -> x32, local copies, waits for them, and re-layouts: 16.7 us -> 11.4 us
    all_to_all x1, starting transfers between devices: 10.4 us -> 5.28 us  [on_device(): lax.all_to_all(far.reshape(devices, cap, points), AXES, 0, 0, tiled=True)]
  transfers between devices with their start and end apart: 4 -> 4, of which waited for: 2 -> 3; matrix products, arithmetic and copies ran while one was open for 9% -> 7% of each run, Pallas kernels for 62% -> 66%
where the time goes in v3:
time: 188 us; the launch traced here: 187 us
  Pallas kernels  125 us (66%)
  starting transfers between devices  21.6 us (11%)
  waiting for transfers between devices  16.7 us (9%)
  local copies, waits for them, and re-layouts  15.6 us (8%)
  matrix products  6.24 us (3%)
  other arithmetic  1.89 us (1%)
    pallas_call x1, Pallas kernels, near_field(): pl.pallas_call(functools.partial(near_kernel, group, unroll), out_shape=j...  94.6 us
    pallas_call x1, Pallas kernels, far_field(): pl.pallas_call(functools.partial(far_kernel, unroll), out_shape=jax.Shape...  21.6 us
    unnamed x32, local copies, waits for them, and re-layouts  11.4 us
    all_to_all x1, waiting for transfers between devices, on_device(): received = lax.all_to_all(packed, AXES, 0, 0, tiled=True)  8.41 us
    all_to_all x1, starting transfers between devices, on_device(): at_leaves = lax.all_to_all(outgoing, AXES, 0, 0, tiled=True)  7.54 us
    dot_general x1, matrix products, on_device(): jnp.einsum('pr,oqr->opq', parents, l2l_ops, precision=lax.Precision.HIGHEST)  6.24 us
    pallas_call x1, Pallas kernels, pack(): pl.pallas_call(functools.partial(pack_kernel, capacity), out_shape=(jax.S...  5.53 us
    all_to_all x1, starting transfers between devices, on_device(): lax.all_to_all(far.reshape(devices, cap, points), AXES, 0, 0, tiled=True)  5.28 us
  transfers between devices with their start and end apart: 4, of which 3 were waited for; matrix products, arithmetic and copies ran while one was open for 7% of the time, Pallas kernels for 66%

profile of v3, /device:TPU:1, one launch (start us, length us, event | category | flops | bytes accessed | tf_op | source)
XLA Modules:
  0.0 187.5 jit_solution(11263900375104617294)
XLA Ops:
  0.6 0.7 slice.3
  1.4 3.9 %collective-permute-start = (f32[16,296]{1,0:T(8,128)S(1)}, f32[16,296]{1,0:T(8,128)S(1)}, u32[]{:S(2)}, u32[]{:S(2)}) collective-permute-start(f32[16,296]{1,0:T(8,128)S(1)} %slice.3), channel_id=1, source_target_pairs={{0,1},{1,2},{2,3},{3,4},{4,5},{5,6},{6,7},{7,8},{8,9},{9,10},{10,1... | collective-permute-start | bytes 56840 | tf_op jit(solution)/shard_map/ppermute | solution.py:27
  5.3 2.7 %copy_bitcast_fusion = f32[128,3,8,128]{3,2,1,0:T(8,128)} fusion(f32[1024,3,128]{2,0,1:T(8,128)} %param.22), kind=kLoop, calls=%fused_computation | loop fusion | bytes 3145728 | tf_op jit(solution)/shard_map/transpose | solution.py:351
  8.0 0.0 copy-start.11
  8.0 3.1 %collective-permute-done = f32[16,296]{1,0:T(8,128)S(1)} collective-permute-done((f32[16,296]{1,0:T(8,128)S(1)}, f32[16,296]{1,0:T(8,128)S(1)}, u32[]{:S(2)}, u32[]{:S(2)}) %collective-permute-start) | collective-permute-done | bytes 18976 | tf_op jit(solution)/shard_map/ppermute | solution.py:27
  11.1 7.5 %all-to-all-start.1 = ((f32[128,3,8,128]{3,2,1,0:T(8,128)}), f32[128,3,8,128]{3,2,1,0:T(8,128)S(1)}, u32[]{:S(2)}, u32[]{:S(2)}) async-start(f32[128,3,8,128]{3,2,1,0:T(8,128)} %copy_bitcast_fusion), calls=%async_computation.1 | async-start | bytes 3145728 | tf_op jit(solution)/shard_map/all_to_all | solution.py:353
  18.6 0.0 copy-start.3
  18.7 0.0 copy-start.12
  18.7 0.0 copy-start.13
  18.7 0.0 copy-start.9
  18.7 0.0 copy-done.11
  18.7 0.1 copy.17.center
  18.9 1.4 copy.16.m2l
  20.3 0.8 dynamic_slice.3.owner
  21.0 0.0 copy-done.3
  21.0 0.0 copy-start.4
  21.1 0.9 copy-done.4
  22.0 5.5 %pack.1 = (f32[128,5,8,128]{3,2,1,0:T(8,128)}, s32[512]{0:T(512)S(1)}) custom-call(s32[512]{0:T(512)S(1)} %dynamic_slice.3.owner, f32[3,512,128]{2,1,0:T(8,128)S(1)} %bitcast.25, f32[512,128]{1,0:T(8,128)S(1)} %copy-done.4, f32[512,3]{1,0:T(8,128)S(1)} %copy.17.center), custom_call_target="tpu_custom_call" | custom-call | tf_op jit(solution)/shard_map/pack/pallas_call | solution.py:60
  27.5 0.0 copy-done.12
  27.5 0.0 copy-done.13
  27.6 0.0 copy-done.9
  27.6 6.2 %fusion = f32[80,8,296]{2,0,1:T(8,128)S(1)} fusion(f32[8,296,296]{2,1,0:T(8,128)} %param.17, f32[64,296]{1,0:T(8,128)S(1)} %copy-done.9, f32[16,296]{1,0:T(8,128)S(1)} %collective-permute-done), kind=kOutput, calls=%fused_computation.3 | convolution fusion | flops 672914560 | bytes 3656192 | tf_op jit(solution)/shard_map/pr,oqr->opq/dot_general | solution.py:356
  33.8 2.9 %leaf_rows.1 = (f32[512,296]{1,0:T(8,128)S(1)}, f32[512,384]{1,0:T(8,128)S(1)}) custom-call(s32[512]{0:T(512)S(1)} %multiply_add_fusion.which, f32[640,296]{1,0:T(8,128)S(1)} %bitcast.23, f32[512,296]{1,0:T(8,128)S(1)} %copy.16.m2l), custom_call_target="tpu_custom_call" | custom-call | flops 262144 | bytes 8388608 | tf_op jit(solution)/shard_map/leaf_rows/pallas_call | solution.py:90
  36.7 0.0 copy-start.5
  36.7 0.9 copy-done.5
  37.6 0.0 copy-start.10
  37.6 5.1 %all-to-all-done.1.off = f32[128,3,8,128]{3,2,1,0:T(8,128)S(1)} async-done(((f32[128,3,8,128]{3,2,1,0:T(8,128)}), f32[128,3,8,128]{3,2,1,0:T(8,128)S(1)}, u32[]{:S(2)}, u32[]{:S(2)}) %all-to-all-start.1) | async-done | bytes 1572896 | tf_op jit(solution)/shard_map/all_to_all | solution.py:353
  42.7 0.0 copy-start.1
  42.7 1.1 copy-done.1
  43.9 4.9 %all-to-all-start = ((f32[128,5,8,128]{3,2,1,0:T(8,128)}), f32[128,5,8,128]{3,2,1,0:T(8,128)S(1)}, u32[]{:S(2)}, u32[]{:S(2)}) async-start(f32[128,5,8,128]{3,2,1,0:T(8,128)} %get-tuple-element.16), calls=%async_computation | async-start | bytes 5242880 | tf_op jit(solution)/shard_map/all_to_all | solution.py:361
  48.7 0.0 copy-done.10
  48.8 1.1 copy.18
  49.8 0.0 copy-start.2
  49.8 1.4 copy-done.2
  51.2 0.0 copy-start.6
  51.3 1.1 copy-done.6
  52.4 0.0 copy-start.7
  52.4 0.9 copy-done.7
  53.3 0.0 copy-start.8
  53.3 0.9 copy-done.8
  54.2 21.6 %far_field.1 = f32[1024,128]{1,0:T(8,128)} custom-call(s32[512]{0:T(512)S(1)} %get-tuple-element.17.dest, f32[128,3,8,128]{3,2,1,0:T(8,128)S(1)} %copy-done.2, f32[512,384]{1,0:T(8,128)S(1)} %copy-done.6, bf16[256,256]{1,0:T(8,128)(2,1)S(1)} %copy-done.8, bf16[256,512]{1,0:T(8,128)(2,1)S(1)} %copy-done.7), custom_call_target="tpu_custom_call" | custom-call | flops 12884901888 | bytes 4194304 | tf_op jit(solution)/shard_map/far_field/pallas_call | solution.py:308
  75.8 8.4 %all-to-all-done.src = f32[128,5,8,128]{3,2,1,0:T(8,128)S(1)} async-done(((f32[128,5,8,128]{3,2,1,0:T(8,128)}), f32[128,5,8,128]{3,2,1,0:T(8,128)S(1)}, u32[]{:S(2)}, u32[]{:S(2)}) %all-to-all-start) | async-done | bytes 2621472 | tf_op jit(solution)/shard_map/all_to_all | solution.py:361
  84.2 5.3 %all-to-all-start.2 = ((f32[128,8,128]{2,1,0:T(8,128)}), f32[128,8,128]{2,1,0:T(8,128)}, u32[]{:S(2)}, u32[]{:S(2)}) async-start(f32[128,8,128]{2,1,0:T(8,128)} %bitcast.8), calls=%async_computation.2 | async-start | bytes 1048576 | tf_op jit(solution)/shard_map/all_to_all | solution.py:364
  89.5 0.0 copy-start
  89.5 1.4 copy-done
  90.9 94.6 %near_field.1 = f32[1024,128]{1,0:T(8,128)S(1)} custom-call(s32[8192]{0:T(1024)S(1)} %bitcast.26, f32[128,5,8,128]{3,2,1,0:T(8,128)S(1)} %all-to-all-done.src, f32[3,1024,128]{2,1,0:T(8,128)S(1)} %bitcast.24), custom_call_target="tpu_custom_call" | custom-call | flops 34359738368 | bytes 8388608 | tf_op jit(solution)/shard_map/near_field/pallas_call | solution.py:203
  185.6 0.0 all-to-all-done.2
  185.6 1.9 %bitcast_add_fusion = f32[1024,128]{1,0:T(8,128)} fusion(f32[1024,128]{1,0:T(8,128)S(1)} %near_field.1, f32[128,8,128]{2,1,0:T(8,128)} %all-to-all-done.2), kind=kLoop, calls=%fused_computation.1 | loop fusion | flops 131072 | bytes 1572864 | tf_op jit(solution)/shard_map/add | solution.py:367
  (2 shorter events, 0.0 us)
Async XLA Ops:
  1.4 9.7 %collective-permute-start = (f32[16,296]{1,0:T(8,128)S(1)}, f32[16,296]{1,0:T(8,128)S(1)}, u32[]{:S(2)}, u32[]{:S(2)}) collective-permute-start(f32[16,296]{1,0:T(8,128)S(1)} %slice.3), channel_id=1, source_target_pairs={{0,1},{1,2},{2,3},{3,4},{4,5},{5,6},{6,7},{7,8},{8,9},{9,10},{10,1... | collective-permute-start | bytes 56840 | tf_op jit(solution)/shard_map/ppermute | solution.py:27
  8.0 10.7 %copy-start.11 = (f32[512,3]{0,1:T(4,128)S(1)}, f32[512,3]{0,1:T(4,128)}, u32[]{:S(2)}) copy-start(f32[512,3]{0,1:T(4,128)} %param.18) | copy-start | bytes 18436
  11.1 31.6 %all-to-all-start.1 = ((f32[128,3,8,128]{3,2,1,0:T(8,128)}), f32[128,3,8,128]{3,2,1,0:T(8,128)S(1)}, u32[]{:S(2)}, u32[]{:S(2)}) async-start(f32[128,3,8,128]{3,2,1,0:T(8,128)} %copy_bitcast_fusion), calls=%async_computation.1 | async-start | bytes 3145728 | tf_op jit(solution)/shard_map/all_to_all | solution.py:353
  18.6 2.4 %copy-start.3 = (f32[512,3,128]{2,0,1:T(8,128)S(1)}, f32[512,3,128]{2,0,1:T(8,128)}, u32[]{:S(2)}) copy-start(f32[512,3,128]{2,0,1:T(8,128)} %param.19) | copy-start | bytes 2359300
  18.7 8.9 %copy-start.12 = (s32[512]{0:T(512)S(1)}, s32[512]{0:T(512)}, u32[]{:S(2)}) copy-start(s32[512]{0:T(512)} %param.14) | copy-start | bytes 6148
  18.7 8.9 %copy-start.13 = (s32[512]{0:T(512)S(1)}, s32[512]{0:T(512)}, u32[]{:S(2)}) copy-start(s32[512]{0:T(512)} %param.15) | copy-start | bytes 6148
  18.7 8.9 %copy-start.9 = (f32[64,296]{1,0:T(8,128)S(1)}, f32[64,296]{1,0:T(8,128)}, u32[]{:S(2)}) copy-start(f32[64,296]{1,0:T(8,128)} %param.13) | copy-start | bytes 227332
  21.0 1.0 copy-start.4
  36.7 0.9 copy-start.5
  37.6 11.2 %copy-start.10 = (s32[1024,8]{0,1:T(8,128)S(1)}, s32[1024,8]{0,1:T(8,128)}, u32[]{:S(2)}) copy-start(s32[1024,8]{0,1:T(8,128)} %param.23) | copy-start | bytes 98308
  42.7 1.1 copy-start.1
  43.9 40.3 %all-to-all-start = ((f32[128,5,8,128]{3,2,1,0:T(8,128)}), f32[128,5,8,128]{3,2,1,0:T(8,128)S(1)}, u32[]{:S(2)}, u32[]{:S(2)}) async-start(f32[128,5,8,128]{3,2,1,0:T(8,128)} %get-tuple-element.16), calls=%async_computation | async-start | bytes 5242880 | tf_op jit(solution)/shard_map/all_to_all | solution.py:361
  49.8 1.4 copy-start.2
  51.2 1.1 copy-start.6
  52.4 0.9 copy-start.7
  53.3 0.9 copy-start.8
  84.2 101.3 %all-to-all-start.2 = ((f32[128,8,128]{2,1,0:T(8,128)}), f32[128,8,128]{2,1,0:T(8,128)}, u32[]{:S(2)}, u32[]{:S(2)}) async-start(f32[128,8,128]{2,1,0:T(8,128)} %bitcast.8), calls=%async_computation.2 | async-start | bytes 1048576 | tf_op jit(solution)/shard_map/all_to_all | solution.py:364
  89.5 1.4 copy-start

commit v4 on v3

--- a/solution.py
+++ b/solution.py
@@ -19,6 +19,7 @@
 F32 = jnp.float32
 BF16 = jnp.bfloat16
 FEATURES = 32
+MESH = pl.DeviceIdType.MESH
 
 
 def from_behind(block, axis, distance):
@@ -124,45 +125,80 @@
     return out, list(split3(x * x + y * y + z * z))
 
 
-def near_kernel(group, unroll, near_list, src, off, out, table, charges, tfeat, sfeat):
-    step = pl.program_id(0)
+def peer_of(me, k, devices, inner):
+    peer = lax.rem(me + k, devices)
+    return peer, (peer // inner, lax.rem(peer, inner))
+
+
+def near_kernel(
+    unroll, inner, near_list, src, off, far, out, table, charges, tfeat, sfeat, arrived, sent, got
+):
     senders, _, cap, _ = src.shape
     slots = senders * cap
+    me = lax.axis_index("grp") * inner + lax.axis_index("dom")
     ones = jnp.ones((8, 128), F32)
     zeros = jnp.zeros((8, 128), F32)
-
-    @pl.when(step == 0)
-    def _():
-        for f in range(18, 21):
-            sfeat[8 * f : 8 * f + 8] = ones
+    barrier = pltpu.get_barrier_semaphore()
+
+    def greet(k, carry):
+        _, device = peer_of(me, k, senders, inner)
+        pl.semaphore_signal(barrier, inc=1, device_id=device, device_id_type=MESH)
+        return carry
+
+    lax.fori_loop(1, senders, greet, 0)
+
+    for f in range(18, 21):
+        sfeat[8 * f : 8 * f + 8] = ones
+    for f in range(24, FEATURES):
+        sfeat[8 * f : 8 * f + 8] = zeros
+    for u in range(unroll):
+        for f in range(21, 24):
+            tfeat[u, 8 * f : 8 * f + 8] = ones
         for f in range(24, FEATURES):
-            sfeat[8 * f : 8 * f + 8] = zeros
-        for u in range(unroll):
-            for f in range(21, 24):
-                tfeat[u, 8 * f : 8 * f + 8] = ones
-            for f in range(24, FEATURES):
-                tfeat[u, 8 * f : 8 * f + 8] = zeros
-
-        def prepare(i, carry):
-            cross, square = source_features(*(src[i, c] - 1.0 for c in range(3)))
-            for f, v in list(enumerate(cross)) + list(enumerate(square, 21)):
-                sfeat[8 * f : 8 * f + 8] = v
-            for s in range(8):
-                table[i * 8 + s] = sfeat[pl.ds(s, FEATURES, stride=8), :].astype(BF16)
-            charges[pl.ds(i * 8, 8)] = src[i, 3] * (0.25 / math.pi)
-            return carry
-
-        lax.fori_loop(0, senders, prepare, 0)
-
+            tfeat[u, 8 * f : 8 * f + 8] = zeros
+
+    def prepare(i, carry):
+        cross, square = source_features(*(src[i, c] - 1.0 for c in range(3)))
+        for f, v in list(enumerate(cross)) + list(enumerate(square, 21)):
+            sfeat[8 * f : 8 * f + 8] = v
+        for s in range(8):
+            table[i * 8 + s] = sfeat[pl.ds(s, FEATURES, stride=8), :].astype(BF16)
+        charges[pl.ds(i * 8, 8)] = src[i, 3] * (0.25 / math.pi)
+        return carry
+
+    lax.fori_loop(0, senders, prepare, 0)
+    pl.semaphore_wait(barrier, senders - 1)
+
+    def send(k):
+        peer, device = peer_of(me, k, senders, inner)
+        pltpu.make_async_remote_copy(
+            src_ref=far.at[peer],
+            dst_ref=arrived.at[me],
+            send_sem=sent,
+            recv_sem=got,
+            device_id=device,
+            device_id_type=MESH,
+        ).start()
+
+    rounds = senders // unroll
+    inline = (senders - 1) // rounds
+    early = senders - rounds * inline
+
+    def send_early(k, carry):
+        send(k)
+        return carry
+
+    lax.fori_loop(1, early, send_early, 0)
     lane_part = lax.broadcasted_iota(jnp.int32, (128, 128), 1) // FEATURES
 
     def rows(i, carry):
         for u in range(unroll):
-            local = i * unroll + u
-            block = step * group + local
+            if u < inline:
+                send(early + i * inline + u)
+            block = i * unroll + u
             info = src[block, 4]
             place = [
-                (info[:, c : c + 1] - 1.0) + HALF * off[c, pl.ds(local * 8, 8), :] for c in range(3)
+                (info[:, c : c + 1] - 1.0) + HALF * off[c, pl.ds(block * 8, 8), :] for c in range(3)
             ]
             for f, v in enumerate(target_features(*place, SOFT_SQ)):
                 tfeat[u, 8 * f : 8 * f + 8] = v
@@ -189,41 +225,58 @@
                         part = dist_sq[128 * k : 128 * k + 128, 128 * h : 128 * h + 128]
                         term = lax.rsqrt(part) * weight
                         total = term if total is None else total + term
-                out[pl.ds(local * 8 + s, 1), :] = jnp.sum(total.T, axis=0, keepdims=True)
+                out[pl.ds(block * 8 + s, 1), :] = jnp.sum(total.T, axis=0, keepdims=True)
             live = info[:, 3:4] > 0.5
-            out[pl.ds(local * 8, 8), :] = jnp.where(live, out[pl.ds(local * 8, 8), :], 0.0)
-        return carry
-
-    lax.fori_loop(0, group // unroll, rows, 0)
-
-
-def near_field(src, offsets, near_slots, group=16, unroll=4):
+            out[pl.ds(block * 8, 8), :] = jnp.where(live, out[pl.ds(block * 8, 8), :], 0.0)
+        return carry
+
+    lax.fori_loop(0, rounds, rows, 0)
+
+    everything = pltpu.make_async_remote_copy(
+        src_ref=far.at[pl.ds(0, senders - 1)],
+        dst_ref=arrived.at[pl.ds(0, senders - 1)],
+        send_sem=sent,
+        recv_sem=got,
+        device_id=peer_of(me, 1, senders, inner)[1],
+        device_id_type=MESH,
+    )
+    everything.wait_send()
+    everything.wait_recv()
+    arrived[me] = far[me]
+
+    def add(i, carry):
+        out[pl.ds(i * 8, 8), :] += arrived[i]
+        return carry
+
+    lax.fori_loop(0, senders, add, 0, unroll=8)
+
+
+def near_field(src, offsets, near_list, far, inner, unroll=8):
     senders, _, cap, _ = src.shape
     slots = senders * cap
+    vmem = pl.BlockSpec(memory_space=pltpu.VMEM)
     return pl.pallas_call(
-        functools.partial(near_kernel, group, unroll),
+        functools.partial(near_kernel, unroll, inner),
         out_shape=jax.ShapeDtypeStruct((slots, 128), F32),
-        grid_spec=pltpu.PrefetchScalarGridSpec(
-            num_scalar_prefetch=1,
-            grid=(senders // group,),
-            in_specs=[
-                pl.BlockSpec(src.shape, lambda g, n: (0, 0, 0, 0)),
-                pl.BlockSpec((3, group * cap, 128), lambda g, n: (0, g, 0)),
-            ],
-            out_specs=pl.BlockSpec((group * cap, 128), lambda g, n: (g, 0)),
-            scratch_shapes=[
-                pltpu.VMEM((slots, FEATURES, 128), BF16),
-                pltpu.VMEM((slots, 128), F32),
-                pltpu.VMEM((unroll, FEATURES * 8, 128), F32),
-                pltpu.VMEM((FEATURES * 8, 128), F32),
-            ],
+        in_specs=[pl.BlockSpec(memory_space=pltpu.SMEM), vmem, vmem, vmem],
+        out_specs=vmem,
+        scratch_shapes=[
+            pltpu.VMEM((slots, FEATURES, 128), BF16),
+            pltpu.VMEM((slots, 128), F32),
+            pltpu.VMEM((unroll, FEATURES * 8, 128), F32),
+            pltpu.VMEM((FEATURES * 8, 128), F32),
+            pltpu.VMEM((senders, cap, 128), F32),
+            pltpu.SemaphoreType.DMA,
+            pltpu.SemaphoreType.DMA,
+        ],
+        compiler_params=pltpu.CompilerParams(
+            vmem_limit_bytes=28 << 20, collective_id=0, has_side_effects=True
         ),
-        compiler_params=pltpu.CompilerParams(vmem_limit_bytes=28 << 20),
         cost_estimate=pl.CostEstimate(
             flops=2 * slots * 512 * 128 * 256, bytes_accessed=8 << 20, transcendentals=slots << 17
         ),
         name="near_field",
-    )(near_slots, src, offsets)
+    )(near_list, src, offsets, far)
 
 
 def surface_weights():
@@ -360,11 +413,10 @@
     packed, dens = lax.optimization_barrier((packed, dens))
     received = lax.all_to_all(packed, AXES, 0, 0, tiled=True)
     far = far_field(dest, at_leaves, dens)
-    received, far = lax.optimization_barrier((received, far))
-    far = lax.all_to_all(far.reshape(devices, cap, points), AXES, 0, 0, tiled=True)
-
-    near = near_field(received, offsets, jnp.transpose(near_slots).reshape(-1))
-    return (leaf_local, near + far.reshape(slots, points))
+    far = far.reshape(devices, cap, points)
+    near_list = jnp.transpose(near_slots).reshape(-1)
+    potential = near_field(received, offsets, near_list, far, lax.axis_size("dom"))
+    return (leaf_local, potential)
 
 
 def solution(mesh):

time: 188 us -> 212 us (1.13)
  Pallas kernels: 125 us -> 154 us
  starting transfers between devices: 21.6 us -> 16.4 us
    pallas_call x1, Pallas kernels: 94.6 us -> 125 us  [near_field(): pl.pallas_call(functools.partial(near_kernel, unroll, inner), out_shape=j...]
    all_to_all x1 -> x0, starting transfers between devices: 5.28 us -> none  [on_device(): lax.all_to_all(far.reshape(devices, cap, points), AXES, 0, 0, tiled=True)]
    unnamed x32 -> x33, local copies, waits for them, and re-layouts: 11.4 us -> 12.3 us
  transfers between devices with their start and end apart: 4 -> 3, of which waited for: 3 -> 3; matrix products, arithmetic and copies ran while one was open for 7% -> 6% of each run, Pallas kernels for 66% -> 14%
where the time goes in v4:
time: 212 us; the launch traced here: 211 us
  Pallas kernels  154 us (73%)
  waiting for transfers between devices  17.2 us (8%)
  local copies, waits for them, and re-layouts  16.4 us (8%)
  starting transfers between devices  16.4 us (8%)
  matrix products  6.24 us (3%)
    pallas_call x1, Pallas kernels, near_field(): pl.pallas_call(functools.partial(near_kernel, unroll, inner), out_shape=j...  125 us
    pallas_call x1, Pallas kernels, far_field(): pl.pallas_call(functools.partial(far_kernel, unroll), out_shape=jax.Shape...  21 us
    unnamed x33, local copies, waits for them, and re-layouts  12.3 us
    all_to_all x1, waiting for transfers between devices, on_device(): received = lax.all_to_all(packed, AXES, 0, 0, tiled=True)  8.94 us
    all_to_all x1, starting transfers between devices, on_device(): at_leaves = lax.all_to_all(outgoing, AXES, 0, 0, tiled=True)  7.55 us
    dot_general x1, matrix products, on_device(): jnp.einsum('pr,oqr->opq', parents, l2l_ops, precision=lax.Precision.HIGHEST)  6.24 us
    pallas_call x1, Pallas kernels, pack(): pl.pallas_call(functools.partial(pack_kernel, capacity), out_shape=(jax.S...  5.52 us
    all_to_all x1, waiting for transfers between devices, on_device(): at_leaves = lax.all_to_all(outgoing, AXES, 0, 0, tiled=True)  5.14 us
  transfers between devices with their start and end apart: 3, of which 3 were waited for; matrix products, arithmetic and copies ran while one was open for 6% of the time, Pallas kernels for 14%

profile of v4, /device:TPU:1, one launch (start us, length us, event | category | flops | bytes accessed | tf_op | source)
XLA Modules:
  0.0 211.2 jit_solution(3571202177198171003)
XLA Ops:
  0.6 0.7 slice.3
  1.4 3.9 %collective-permute-start = (f32[16,296]{1,0:T(8,128)S(1)}, f32[16,296]{1,0:T(8,128)S(1)}, u32[]{:S(2)}, u32[]{:S(2)}) collective-permute-start(f32[16,296]{1,0:T(8,128)S(1)} %slice.3), channel_id=1, source_target_pairs={{0,1},{1,2},{2,3},{3,4},{4,5},{5,6},{6,7},{7,8},{8,9},{9,10},{10,1... | collective-permute-start | bytes 56840 | tf_op jit(solution)/shard_map/ppermute | solution.py:28
  5.3 2.7 %copy_bitcast_fusion = f32[128,3,8,128]{3,2,1,0:T(8,128)} fusion(f32[1024,3,128]{2,0,1:T(8,128)} %param.22), kind=kLoop, calls=%fused_computation | loop fusion | bytes 3145728 | tf_op jit(solution)/shard_map/transpose | solution.py:404
  8.0 0.0 copy-start.11
  8.0 3.1 %collective-permute-done = f32[16,296]{1,0:T(8,128)S(1)} collective-permute-done((f32[16,296]{1,0:T(8,128)S(1)}, f32[16,296]{1,0:T(8,128)S(1)}, u32[]{:S(2)}, u32[]{:S(2)}) %collective-permute-start) | collective-permute-done | bytes 18976 | tf_op jit(solution)/shard_map/ppermute | solution.py:28
  11.1 7.5 %all-to-all-start.1 = ((f32[128,3,8,128]{3,2,1,0:T(8,128)}), f32[128,3,8,128]{3,2,1,0:T(8,128)S(1)}, u32[]{:S(2)}, u32[]{:S(2)}) async-start(f32[128,3,8,128]{3,2,1,0:T(8,128)} %copy_bitcast_fusion), calls=%async_computation.1 | async-start | bytes 3145728 | tf_op jit(solution)/shard_map/all_to_all | solution.py:406
  18.6 0.0 copy-start.3
  18.7 0.0 copy-start.12
  18.7 0.0 copy-start.13
  18.7 0.0 copy-start.9
  18.7 0.0 copy-done.11
  18.7 0.1 copy.17.center
  18.9 1.4 copy.16.m2l
  20.3 0.8 dynamic_slice.3.owner
  21.1 0.0 copy-done.3
  21.1 0.0 copy-start.4
  21.1 0.9 copy-done.4
  22.0 5.5 %pack.1 = (f32[128,5,8,128]{3,2,1,0:T(8,128)}, s32[512]{0:T(512)S(1)}) custom-call(s32[512]{0:T(512)S(1)} %dynamic_slice.3.owner, f32[3,512,128]{2,1,0:T(8,128)S(1)} %bitcast.23, f32[512,128]{1,0:T(8,128)S(1)} %copy-done.4, f32[512,3]{1,0:T(8,128)S(1)} %copy.17.center), custom_call_target="tpu_custom_call" | custom-call | tf_op jit(solution)/shard_map/pack/pallas_call | solution.py:61
  27.5 0.0 copy-done.12
  27.6 0.0 copy-done.13
  27.6 0.0 copy-done.9
  27.6 6.2 %fusion = f32[80,8,296]{2,0,1:T(8,128)S(1)} fusion(f32[8,296,296]{2,1,0:T(8,128)} %param.17, f32[64,296]{1,0:T(8,128)S(1)} %copy-done.9, f32[16,296]{1,0:T(8,128)S(1)} %collective-permute-done), kind=kOutput, calls=%fused_computation.2 | convolution fusion | flops 672914560 | bytes 3656192 | tf_op jit(solution)/shard_map/pr,oqr->opq/dot_general | solution.py:409
  33.8 2.9 %leaf_rows.1 = (f32[512,296]{1,0:T(8,128)S(1)}, f32[512,384]{1,0:T(8,128)S(1)}) custom-call(s32[512]{0:T(512)S(1)} %multiply_add_fusion.which, f32[640,296]{1,0:T(8,128)S(1)} %bitcast.21, f32[512,296]{1,0:T(8,128)S(1)} %copy.16.m2l), custom_call_target="tpu_custom_call" | custom-call | flops 262144 | bytes 8388608 | tf_op jit(solution)/shard_map/leaf_rows/pallas_call | solution.py:91
  36.7 0.0 copy-start.5
  36.7 0.9 copy-done.5
  37.6 0.0 copy-start.10
  37.6 5.1 %all-to-all-done.1.off = f32[128,3,8,128]{3,2,1,0:T(8,128)S(1)} async-done(((f32[128,3,8,128]{3,2,1,0:T(8,128)}), f32[128,3,8,128]{3,2,1,0:T(8,128)S(1)}, u32[]{:S(2)}, u32[]{:S(2)}) %all-to-all-start.1) | async-done | bytes 1572896 | tf_op jit(solution)/shard_map/all_to_all | solution.py:406
  42.7 0.0 copy-start.1
  42.7 1.2 copy-done.1
  43.9 4.9 %all-to-all-start = ((f32[128,5,8,128]{3,2,1,0:T(8,128)}), f32[128,5,8,128]{3,2,1,0:T(8,128)S(1)}, u32[]{:S(2)}, u32[]{:S(2)}) async-start(f32[128,5,8,128]{3,2,1,0:T(8,128)} %get-tuple-element.14), calls=%async_computation | async-start | bytes 5242880 | tf_op jit(solution)/shard_map/all_to_all | solution.py:414
  48.8 0.0 copy-done.10
  48.8 1.1 copy.18
  49.9 0.0 copy-start.2
  49.9 1.4 copy-done.2
  51.3 0.0 copy-start.6
  51.3 1.1 copy-done.6
  52.4 0.0 copy-start.7
  52.4 0.9 copy-done.7
  53.4 0.0 copy-start.8
  53.4 0.9 copy-done.8
  54.3 21.0 %far_field.1 = f32[1024,128]{1,0:T(8,128)S(1)} custom-call(s32[512]{0:T(512)S(1)} %get-tuple-element.15.dest, f32[128,3,8,128]{3,2,1,0:T(8,128)S(1)} %copy-done.2, f32[512,384]{1,0:T(8,128)S(1)} %copy-done.6, bf16[256,256]{1,0:T(8,128)(2,1)S(1)} %copy-done.8, bf16[256,512]{1,0:T(8,128)(2,1)S(1)} %copy-done.7), custom_call_target="tpu_custom_call" | custom-call | flops 12884901888 | bytes 4194304 | tf_op jit(solution)/shard_map/far_field/pallas_call | solution.py:361
  75.3 8.9 %all-to-all-done.src = f32[128,5,8,128]{3,2,1,0:T(8,128)S(1)} async-done(((f32[128,5,8,128]{3,2,1,0:T(8,128)}), f32[128,5,8,128]{3,2,1,0:T(8,128)S(1)}, u32[]{:S(2)}, u32[]{:S(2)}) %all-to-all-start) | async-done | bytes 2621472 | tf_op jit(solution)/shard_map/all_to_all | solution.py:414
  84.2 0.0 copy-start
  84.2 1.4 copy-done
  85.6 124.8 %near_field.1 = f32[1024,128]{1,0:T(8,128)S(1)} custom-call(s32[8192]{0:T(1024)S(1)} %bitcast.24, f32[128,5,8,128]{3,2,1,0:T(8,128)S(1)} %all-to-all-done.src, f32[3,1024,128]{2,1,0:T(8,128)S(1)} %bitcast.22, f32[128,8,128]{2,1,0:T(8,128)S(1)} %bitcast.25), custom_call_target="tpu_custom_call" | custom-call | flops 34359738368 | bytes 8388608 | tf_op jit(solution)/shard_map/near_field/pallas_call | solution.py:258
  210.4 0.8 copy.24
  (2 shorter events, 0.0 us)
Async XLA Ops:
  1.4 9.7 %collective-permute-start = (f32[16,296]{1,0:T(8,128)S(1)}, f32[16,296]{1,0:T(8,128)S(1)}, u32[]{:S(2)}, u32[]{:S(2)}) collective-permute-start(f32[16,296]{1,0:T(8,128)S(1)} %slice.3), channel_id=1, source_target_pairs={{0,1},{1,2},{2,3},{3,4},{4,5},{5,6},{6,7},{7,8},{8,9},{9,10},{10,1... | collective-permute-start | bytes 56840 | tf_op jit(solution)/shard_map/ppermute | solution.py:28
  8.0 10.7 %copy-start.11 = (f32[512,3]{0,1:T(4,128)S(1)}, f32[512,3]{0,1:T(4,128)}, u32[]{:S(2)}) copy-start(f32[512,3]{0,1:T(4,128)} %param.18) | copy-start | bytes 18436
  11.1 31.7 %all-to-all-start.1 = ((f32[128,3,8,128]{3,2,1,0:T(8,128)}), f32[128,3,8,128]{3,2,1,0:T(8,128)S(1)}, u32[]{:S(2)}, u32[]{:S(2)}) async-start(f32[128,3,8,128]{3,2,1,0:T(8,128)} %copy_bitcast_fusion), calls=%async_computation.1 | async-start | bytes 3145728 | tf_op jit(solution)/shard_map/all_to_all | solution.py:406
  18.6 2.4 %copy-start.3 = (f32[512,3,128]{2,0,1:T(8,128)S(1)}, f32[512,3,128]{2,0,1:T(8,128)}, u32[]{:S(2)}) copy-start(f32[512,3,128]{2,0,1:T(8,128)} %param.19) | copy-start | bytes 2359300
  18.7 8.9 %copy-start.12 = (s32[512]{0:T(512)S(1)}, s32[512]{0:T(512)}, u32[]{:S(2)}) copy-start(s32[512]{0:T(512)} %param.14) | copy-start | bytes 6148
  18.7 8.9 %copy-start.13 = (s32[512]{0:T(512)S(1)}, s32[512]{0:T(512)}, u32[]{:S(2)}) copy-start(s32[512]{0:T(512)} %param.15) | copy-start | bytes 6148
  18.7 8.9 %copy-start.9 = (f32[64,296]{1,0:T(8,128)S(1)}, f32[64,296]{1,0:T(8,128)}, u32[]{:S(2)}) copy-start(f32[64,296]{1,0:T(8,128)} %param.13) | copy-start | bytes 227332
  21.1 1.0 copy-start.4
  36.7 0.9 copy-start.5
  37.6 11.2 %copy-start.10 = (s32[1024,8]{0,1:T(8,128)S(1)}, s32[1024,8]{0,1:T(8,128)}, u32[]{:S(2)}) copy-start(s32[1024,8]{0,1:T(8,128)} %param.23) | copy-start | bytes 98308
  42.7 1.2 copy-start.1
  43.9 40.3 %all-to-all-start = ((f32[128,5,8,128]{3,2,1,0:T(8,128)}), f32[128,5,8,128]{3,2,1,0:T(8,128)S(1)}, u32[]{:S(2)}, u32[]{:S(2)}) async-start(f32[128,5,8,128]{3,2,1,0:T(8,128)} %get-tuple-element.14), calls=%async_computation | async-start | bytes 5242880 | tf_op jit(solution)/shard_map/all_to_all | solution.py:414
  49.9 1.4 copy-start.2
  51.3 1.1 copy-start.6
  52.4 0.9 copy-start.7
  53.4 0.9 copy-start.8
  84.2 1.4 copy-start

commit v5 on v4

--- a/solution.py
+++ b/solution.py
@@ -180,21 +180,15 @@
             device_id_type=MESH,
         ).start()
 
-    rounds = senders // unroll
-    inline = (senders - 1) // rounds
-    early = senders - rounds * inline
-
-    def send_early(k, carry):
+    def send_all(k, carry):
         send(k)
         return carry
 
-    lax.fori_loop(1, early, send_early, 0)
+    lax.fori_loop(1, senders, send_all, 0)
     lane_part = lax.broadcasted_iota(jnp.int32, (128, 128), 1) // FEATURES
 
     def rows(i, carry):
         for u in range(unroll):
-            if u < inline:
-                send(early + i * inline + u)
             block = i * unroll + u
             info = src[block, 4]
             place = [
@@ -230,7 +224,7 @@
             out[pl.ds(block * 8, 8), :] = jnp.where(live, out[pl.ds(block * 8, 8), :], 0.0)
         return carry
 
-    lax.fori_loop(0, rounds, rows, 0)
+    lax.fori_loop(0, senders // unroll, rows, 0)
 
     everything = pltpu.make_async_remote_copy(
         src_ref=far.at[pl.ds(0, senders - 1)],

time: 212 us -> 182 us (0.86)
  Pallas kernels: 154 us -> 124 us
    pallas_call x1, Pallas kernels: 125 us -> 94.7 us  [near_field(): pl.pallas_call(functools.partial(near_kernel, unroll, inner), out_shape=j...]
  transfers between devices with their start and end apart: 3 -> 3, of which waited for: 3 -> 3; matrix products, arithmetic and copies ran while one was open for 6% -> 7% of each run, Pallas kernels for 14% -> 16%
where the time goes in v5:
time: 182 us; the launch traced here: 181 us
  Pallas kernels  124 us (68%)
  waiting for transfers between devices  17.2 us (9%)
  local copies, waits for them, and re-layouts  16.4 us (9%)
  starting transfers between devices  16.4 us (9%)
  matrix products  6.24 us (3%)
    pallas_call x1, Pallas kernels, near_field(): pl.pallas_call(functools.partial(near_kernel, unroll, inner), out_shape=j...  94.7 us
    pallas_call x1, Pallas kernels, far_field(): pl.pallas_call(functools.partial(far_kernel, unroll), out_shape=jax.Shape...  21 us
    unnamed x33, local copies, waits for them, and re-layouts  12.3 us
    all_to_all x1, waiting for transfers between devices, on_device(): received = lax.all_to_all(packed, AXES, 0, 0, tiled=True)  8.96 us
    all_to_all x1, starting transfers between devices, on_device(): at_leaves = lax.all_to_all(outgoing, AXES, 0, 0, tiled=True)  7.55 us
    dot_general x1, matrix products, on_device(): jnp.einsum('pr,oqr->opq', parents, l2l_ops, precision=lax.Precision.HIGHEST)  6.24 us
    pallas_call x1, Pallas kernels, pack(): pl.pallas_call(functools.partial(pack_kernel, capacity), out_shape=(jax.S...  5.52 us
    all_to_all x1, waiting for transfers between devices, on_device(): at_leaves = lax.all_to_all(outgoing, AXES, 0, 0, tiled=True)  5.14 us
  transfers between devices with their start and end apart: 3, of which 3 were waited for; matrix products, arithmetic and copies ran while one was open for 7% of the time, Pallas kernels for 16%

profile of v5, /device:TPU:1, one launch (start us, length us, event | category | flops | bytes accessed | tf_op | source)
XLA Modules:
  0.0 181.2 jit_solution(17484212442945579761)
XLA Ops:
  0.6 0.7 slice.3
  1.4 3.9 %collective-permute-start = (f32[16,296]{1,0:T(8,128)S(1)}, f32[16,296]{1,0:T(8,128)S(1)}, u32[]{:S(2)}, u32[]{:S(2)}) collective-permute-start(f32[16,296]{1,0:T(8,128)S(1)} %slice.3), channel_id=1, source_target_pairs={{0,1},{1,2},{2,3},{3,4},{4,5},{5,6},{6,7},{7,8},{8,9},{9,10},{10,1... | collective-permute-start | bytes 56840 | tf_op jit(solution)/shard_map/ppermute | solution.py:28
  5.3 2.7 %copy_bitcast_fusion = f32[128,3,8,128]{3,2,1,0:T(8,128)} fusion(f32[1024,3,128]{2,0,1:T(8,128)} %param.22), kind=kLoop, calls=%fused_computation | loop fusion | bytes 3145728 | tf_op jit(solution)/shard_map/transpose | solution.py:398
  8.0 0.0 copy-start.11
  8.0 3.1 %collective-permute-done = f32[16,296]{1,0:T(8,128)S(1)} collective-permute-done((f32[16,296]{1,0:T(8,128)S(1)}, f32[16,296]{1,0:T(8,128)S(1)}, u32[]{:S(2)}, u32[]{:S(2)}) %collective-permute-start) | collective-permute-done | bytes 18976 | tf_op jit(solution)/shard_map/ppermute | solution.py:28
  11.1 7.5 %all-to-all-start.1 = ((f32[128,3,8,128]{3,2,1,0:T(8,128)}), f32[128,3,8,128]{3,2,1,0:T(8,128)S(1)}, u32[]{:S(2)}, u32[]{:S(2)}) async-start(f32[128,3,8,128]{3,2,1,0:T(8,128)} %copy_bitcast_fusion), calls=%async_computation.1 | async-start | bytes 3145728 | tf_op jit(solution)/shard_map/all_to_all | solution.py:400
  18.6 0.0 copy-start.3
  18.7 0.0 copy-start.12
  18.7 0.0 copy-start.13
  18.7 0.0 copy-start.9
  18.7 0.0 copy-done.11
  18.7 0.1 copy.17.center
  18.9 1.4 copy.16.m2l
  20.3 0.8 dynamic_slice.3.owner
  21.1 0.0 copy-done.3
  21.1 0.0 copy-start.4
  21.1 0.9 copy-done.4
  22.0 5.5 %pack.1 = (f32[128,5,8,128]{3,2,1,0:T(8,128)}, s32[512]{0:T(512)S(1)}) custom-call(s32[512]{0:T(512)S(1)} %dynamic_slice.3.owner, f32[3,512,128]{2,1,0:T(8,128)S(1)} %bitcast.23, f32[512,128]{1,0:T(8,128)S(1)} %copy-done.4, f32[512,3]{1,0:T(8,128)S(1)} %copy.17.center), custom_call_target="tpu_custom_call" | custom-call | tf_op jit(solution)/shard_map/pack/pallas_call | solution.py:61
  27.5 0.0 copy-done.12
  27.6 0.0 copy-done.13
  27.6 0.0 copy-done.9
  27.6 6.2 %fusion = f32[80,8,296]{2,0,1:T(8,128)S(1)} fusion(f32[8,296,296]{2,1,0:T(8,128)} %param.17, f32[64,296]{1,0:T(8,128)S(1)} %copy-done.9, f32[16,296]{1,0:T(8,128)S(1)} %collective-permute-done), kind=kOutput, calls=%fused_computation.2 | convolution fusion | flops 672914560 | bytes 3656192 | tf_op jit(solution)/shard_map/pr,oqr->opq/dot_general | solution.py:403
  33.8 2.9 %leaf_rows.1 = (f32[512,296]{1,0:T(8,128)S(1)}, f32[512,384]{1,0:T(8,128)S(1)}) custom-call(s32[512]{0:T(512)S(1)} %multiply_add_fusion.which, f32[640,296]{1,0:T(8,128)S(1)} %bitcast.21, f32[512,296]{1,0:T(8,128)S(1)} %copy.16.m2l), custom_call_target="tpu_custom_call" | custom-call | flops 262144 | bytes 8388608 | tf_op jit(solution)/shard_map/leaf_rows/pallas_call | solution.py:91
  36.7 0.0 copy-start.5
  36.7 0.9 copy-done.5
  37.6 0.0 copy-start.10
  37.6 5.1 %all-to-all-done.1.off = f32[128,3,8,128]{3,2,1,0:T(8,128)S(1)} async-done(((f32[128,3,8,128]{3,2,1,0:T(8,128)}), f32[128,3,8,128]{3,2,1,0:T(8,128)S(1)}, u32[]{:S(2)}, u32[]{:S(2)}) %all-to-all-start.1) | async-done | bytes 1572896 | tf_op jit(solution)/shard_map/all_to_all | solution.py:400
  42.7 0.0 copy-start.1
  42.7 1.2 copy-done.1
  43.9 4.9 %all-to-all-start = ((f32[128,5,8,128]{3,2,1,0:T(8,128)}), f32[128,5,8,128]{3,2,1,0:T(8,128)S(1)}, u32[]{:S(2)}, u32[]{:S(2)}) async-start(f32[128,5,8,128]{3,2,1,0:T(8,128)} %get-tuple-element.14), calls=%async_computation | async-start | bytes 5242880 | tf_op jit(solution)/shard_map/all_to_all | solution.py:408
  48.8 0.0 copy-done.10
  48.8 1.1 copy.18
  49.9 0.0 copy-start.2
  49.9 1.4 copy-done.2
  51.3 0.0 copy-start.6
  51.3 1.1 copy-done.6
  52.4 0.0 copy-start.7
  52.4 0.9 copy-done.7
  53.4 0.0 copy-start.8
  53.4 0.9 copy-done.8
  54.3 21.0 %far_field.1 = f32[1024,128]{1,0:T(8,128)S(1)} custom-call(s32[512]{0:T(512)S(1)} %get-tuple-element.15.dest, f32[128,3,8,128]{3,2,1,0:T(8,128)S(1)} %copy-done.2, f32[512,384]{1,0:T(8,128)S(1)} %copy-done.6, bf16[256,256]{1,0:T(8,128)(2,1)S(1)} %copy-done.8, bf16[256,512]{1,0:T(8,128)(2,1)S(1)} %copy-done.7), custom_call_target="tpu_custom_call" | custom-call | flops 12884901888 | bytes 4194304 | tf_op jit(solution)/shard_map/far_field/pallas_call | solution.py:355
  75.3 9.0 %all-to-all-done.src = f32[128,5,8,128]{3,2,1,0:T(8,128)S(1)} async-done(((f32[128,5,8,128]{3,2,1,0:T(8,128)}), f32[128,5,8,128]{3,2,1,0:T(8,128)S(1)}, u32[]{:S(2)}, u32[]{:S(2)}) %all-to-all-start) | async-done | bytes 2621472 | tf_op jit(solution)/shard_map/all_to_all | solution.py:408
  84.2 0.0 copy-start
  84.2 1.4 copy-done
  85.6 94.7 %near_field.1 = f32[1024,128]{1,0:T(8,128)S(1)} custom-call(s32[8192]{0:T(1024)S(1)} %bitcast.24, f32[128,5,8,128]{3,2,1,0:T(8,128)S(1)} %all-to-all-done.src, f32[3,1024,128]{2,1,0:T(8,128)S(1)} %bitcast.22, f32[128,8,128]{2,1,0:T(8,128)S(1)} %bitcast.25), custom_call_target="tpu_custom_call" | custom-call | flops 34359738368 | bytes 8388608 | tf_op jit(solution)/shard_map/near_field/pallas_call | solution.py:252
  180.4 0.8 copy.24
  (2 shorter events, 0.0 us)
Async XLA Ops:
  1.4 9.7 %collective-permute-start = (f32[16,296]{1,0:T(8,128)S(1)}, f32[16,296]{1,0:T(8,128)S(1)}, u32[]{:S(2)}, u32[]{:S(2)}) collective-permute-start(f32[16,296]{1,0:T(8,128)S(1)} %slice.3), channel_id=1, source_target_pairs={{0,1},{1,2},{2,3},{3,4},{4,5},{5,6},{6,7},{7,8},{8,9},{9,10},{10,1... | collective-permute-start | bytes 56840 | tf_op jit(solution)/shard_map/ppermute | solution.py:28
  8.0 10.7 %copy-start.11 = (f32[512,3]{0,1:T(4,128)S(1)}, f32[512,3]{0,1:T(4,128)}, u32[]{:S(2)}) copy-start(f32[512,3]{0,1:T(4,128)} %param.18) | copy-start | bytes 18436
  11.1 31.7 %all-to-all-start.1 = ((f32[128,3,8,128]{3,2,1,0:T(8,128)}), f32[128,3,8,128]{3,2,1,0:T(8,128)S(1)}, u32[]{:S(2)}, u32[]{:S(2)}) async-start(f32[128,3,8,128]{3,2,1,0:T(8,128)} %copy_bitcast_fusion), calls=%async_computation.1 | async-start | bytes 3145728 | tf_op jit(solution)/shard_map/all_to_all | solution.py:400
  18.6 2.4 %copy-start.3 = (f32[512,3,128]{2,0,1:T(8,128)S(1)}, f32[512,3,128]{2,0,1:T(8,128)}, u32[]{:S(2)}) copy-start(f32[512,3,128]{2,0,1:T(8,128)} %param.19) | copy-start | bytes 2359300
  18.7 8.9 %copy-start.12 = (s32[512]{0:T(512)S(1)}, s32[512]{0:T(512)}, u32[]{:S(2)}) copy-start(s32[512]{0:T(512)} %param.14) | copy-start | bytes 6148
  18.7 8.9 %copy-start.13 = (s32[512]{0:T(512)S(1)}, s32[512]{0:T(512)}, u32[]{:S(2)}) copy-start(s32[512]{0:T(512)} %param.15) | copy-start | bytes 6148
  18.7 8.9 %copy-start.9 = (f32[64,296]{1,0:T(8,128)S(1)}, f32[64,296]{1,0:T(8,128)}, u32[]{:S(2)}) copy-start(f32[64,296]{1,0:T(8,128)} %param.13) | copy-start | bytes 227332
  21.1 1.0 copy-start.4
  36.7 0.9 copy-start.5
  37.6 11.2 %copy-start.10 = (s32[1024,8]{0,1:T(8,128)S(1)}, s32[1024,8]{0,1:T(8,128)}, u32[]{:S(2)}) copy-start(s32[1024,8]{0,1:T(8,128)} %param.23) | copy-start | bytes 98308
  42.7 1.2 copy-start.1
  43.9 40.3 %all-to-all-start = ((f32[128,5,8,128]{3,2,1,0:T(8,128)}), f32[128,5,8,128]{3,2,1,0:T(8,128)S(1)}, u32[]{:S(2)}, u32[]{:S(2)}) async-start(f32[128,5,8,128]{3,2,1,0:T(8,128)} %get-tuple-element.14), calls=%async_computation | async-start | bytes 5242880 | tf_op jit(solution)/shard_map/all_to_all | solution.py:408
  49.9 1.4 copy-start.2
  51.3 1.1 copy-start.6
  52.4 0.9 copy-start.7
  53.4 0.9 copy-start.8
  84.2 1.4 copy-start

commit v6 on v5

--- a/solution.py
+++ b/solution.py
@@ -28,7 +28,7 @@
     return lax.ppermute(block, axis, route)
 
 
-def pack_kernel(capacity, owner, coords, charge, center, out, dest, count, tail):
+def pack_kernel(capacity, owner, coords, charge, center, out, dest, slot_leaf, count, tail):
     devices = out.shape[0]
     leaves = charge.shape[0]
     out[...] = jnp.zeros_like(out)
@@ -37,6 +37,8 @@
 
     def clear(i, carry):
         count[i] = 0
+        for k in range(capacity):
+            slot_leaf[i * capacity + k] = leaves
         return carry
 
     lax.fori_loop(0, devices, clear, 0, unroll=8)
@@ -46,6 +48,7 @@
         rank = count[o]
         count[o] = rank + 1
         dest[j] = o * capacity + rank
+        slot_leaf[o * capacity + rank] = j
         for c in range(3):
             out[o, c, pl.ds(rank, 1), :] = coords[c, pl.ds(j, 1), :]
         out[o, 3, pl.ds(rank, 1), :] = charge[pl.ds(j, 1), :]
@@ -58,48 +61,20 @@
 def pack(owner, coords, charge, center, devices, capacity):
     leaves = charge.shape[0]
     vmem = pl.BlockSpec(memory_space=pltpu.VMEM)
+    smem = pl.BlockSpec(memory_space=pltpu.SMEM)
     return pl.pallas_call(
         functools.partial(pack_kernel, capacity),
         out_shape=(
             jax.ShapeDtypeStruct((devices, 5, capacity, 128), F32),
             jax.ShapeDtypeStruct((leaves,), jnp.int32),
+            jax.ShapeDtypeStruct((devices * capacity,), jnp.int32),
         ),
-        in_specs=[pl.BlockSpec(memory_space=pltpu.SMEM), vmem, vmem, vmem],
-        out_specs=(vmem, pl.BlockSpec(memory_space=pltpu.SMEM)),
+        in_specs=[smem, vmem, vmem, vmem],
+        out_specs=(vmem, smem, smem),
         scratch_shapes=[pltpu.SMEM((devices,), jnp.int32), pltpu.VMEM((leaves, 4), F32)],
         compiler_params=pltpu.CompilerParams(vmem_limit_bytes=14 << 20),
         name="pack",
     )(owner, coords, charge, center)
-
-
-def leaf_kernel(which, stacked, m2l, leaf, dens):
-    leaves, width = m2l.shape
-    dens[...] = jnp.zeros_like(dens)
-
-    def place(j, carry):
-        row = m2l[pl.ds(j, 1), :] + stacked[pl.ds(which[j], 1), :]
-        leaf[pl.ds(j, 1), :] = row
-        dens[pl.ds(j, 1), 0:width] = row
-        return carry
-
-    lax.fori_loop(0, leaves, place, 0, unroll=8)
-
-
-def leaf_rows(which, stacked, m2l, padded):
-    vmem = pl.BlockSpec(memory_space=pltpu.VMEM)
-    smem = pl.BlockSpec(memory_space=pltpu.SMEM)
-    return pl.pallas_call(
-        leaf_kernel,
-        out_shape=(
-            jax.ShapeDtypeStruct(m2l.shape, F32),
-            jax.ShapeDtypeStruct((m2l.shape[0], padded), F32),
-        ),
-        in_specs=[smem, vmem, vmem],
-        out_specs=(vmem, vmem),
-        compiler_params=pltpu.CompilerParams(vmem_limit_bytes=14 << 20),
-        cost_estimate=pl.CostEstimate(flops=1 << 18, bytes_accessed=8 << 20, transcendentals=0),
-        name="leaf_rows",
-    )(which, stacked, m2l)
 
 
 def split3(v):
@@ -303,10 +278,9 @@
     return main.astype(ml_dtypes.bfloat16), last.astype(ml_dtypes.bfloat16)
 
 
-def far_kernel(unroll, dest, off, dens, main, last, out, tfeat, shift):
+def far_rows(unroll, dest, off, dens, main, last, out, tfeat, shift):
     ones = jnp.ones((8, 128), F32)
     zeros = jnp.zeros((8, 128), F32)
-    out[...] = jnp.zeros_like(out)
     for u in range(unroll):
         for f in range(21, 24):
             tfeat[u, 8 * f : 8 * f + 8] = ones
@@ -342,33 +316,139 @@
                     total = total + lax.rsqrt(dist_sq[:, 128:]) * weights[t][:, 128:256]
                     total = total + jnp.where(low_half == (h == 0), tail, 0.0)
                     line = jnp.sum(total.T, axis=0, keepdims=True)
-                    out[pl.ds(at[t], 1), :] = line * (0.25 / (math.pi * HALF))
+                    out[pl.ds(first + t, 1), :] = line * (0.25 / (math.pi * HALF))
         return carry
 
     lax.fori_loop(0, dens.shape[0] // (8 * unroll), rows, 0)
 
 
-def far_field(dest, offsets, dens, unroll=4):
-    devices, _, cap, points = offsets.shape
+def exchange_kernel(
+    unroll, inner,
+    which, dest, slot_leaf, packed, offsets, rim, own, ops, m2l, main, last,
+    received, leaf, far,
+    stacked, dens, at_leaves, lines, tfeat, shift, off_sent, off_got, src_sent, src_got,
+):
+    devices, _, cap, points = packed.shape
+    leaves, width = m2l.shape
+    me = lax.axis_index("grp") * inner + lax.axis_index("dom")
+    barrier = pltpu.get_barrier_semaphore()
+
+    def greet(k, carry):
+        _, device = peer_of(me, k, devices, inner)
+        pl.semaphore_signal(barrier, inc=1, device_id=device, device_id_type=MESH)
+        return carry
+
+    lax.fori_loop(1, devices, greet, 0)
+    pl.semaphore_wait(barrier, devices - 1)
+
+    def send_offsets(k, carry):
+        peer, device = peer_of(me, k, devices, inner)
+        pltpu.make_async_remote_copy(
+            src_ref=offsets.at[:, pl.ds(peer * cap, cap), :],
+            dst_ref=at_leaves.at[me],
+            send_sem=off_sent,
+            recv_sem=off_got,
+            device_id=device,
+            device_id_type=MESH,
+        ).start()
+        return carry
+
+    lax.fori_loop(1, devices, send_offsets, 0)
+
+    def send_sources(k, carry):
+        peer, device = peer_of(me, k, devices, inner)
+        pltpu.make_async_remote_copy(
+            src_ref=packed.at[peer],
+            dst_ref=received.at[me],
+            send_sem=src_sent,
+            recv_sem=src_got,
+            device_id=device,
+            device_id_type=MESH,
+        ).start()
+        return carry
+
+    lax.fori_loop(1, devices, send_sources, 0)
+    at_leaves[me] = offsets[:, pl.ds(me * cap, cap), :]
+    received[me] = packed[me]
+
+    parents = jnp.concatenate([rim[...], own[...]], axis=0)
+    count = parents.shape[0]
+    for o in range(ops.shape[0]):
+        stacked[o * count : (o + 1) * count, :] = lax.dot_general(
+            parents,
+            ops[o],
+            (((1,), (1,)), ((), ())),
+            precision=lax.Precision.HIGHEST,
+            preferred_element_type=F32,
+        )
+    dens[...] = jnp.zeros_like(dens)
+    lines[leaves:, :] = jnp.zeros((8, points), F32)
+
+    def place(j, carry):
+        row = m2l[pl.ds(j, 1), :] + stacked[pl.ds(which[j], 1), :]
+        leaf[pl.ds(j, 1), :] = row
+        dens[pl.ds(j, 1), 0:width] = row
+        return carry
+
+    lax.fori_loop(0, leaves, place, 0, unroll=8)
+
+    def all_of(ref, sent, got):
+        return pltpu.make_async_remote_copy(
+            src_ref=ref.at[pl.ds(0, devices - 1)],
+            dst_ref=ref.at[pl.ds(0, devices - 1)],
+            send_sem=sent,
+            recv_sem=got,
+            device_id=peer_of(me, 1, devices, inner)[1],
+            device_id_type=MESH,
+        )
+
+    all_of(at_leaves, off_sent, off_got).wait_recv()
+    far_rows(unroll, dest, at_leaves, dens, main, last, lines, tfeat, shift)
+
+    def to_slots(i, carry):
+        for k in range(cap):
+            far[i, k : k + 1, :] = lines[pl.ds(slot_leaf[i * cap + k], 1), :]
+        return carry
+
+    lax.fori_loop(0, devices, to_slots, 0, unroll=2)
+    all_of(received, src_sent, src_got).wait_recv()
+    all_of(at_leaves, off_sent, off_got).wait_send()
+    all_of(received, src_sent, src_got).wait_send()
+
+
+def exchange(which, dest, slot_leaf, packed, offsets, rim, own, ops, m2l, inner, unroll=4):
+    devices, _, cap, points = packed.shape
+    leaves, width = m2l.shape
+    count = rim.shape[0] + own.shape[0]
     main, last = surface_weights()
     vmem = pl.BlockSpec(memory_space=pltpu.VMEM)
+    smem = pl.BlockSpec(memory_space=pltpu.SMEM)
     return pl.pallas_call(
-        functools.partial(far_kernel, unroll),
-        out_shape=jax.ShapeDtypeStruct((devices * cap, points), F32),
-        in_specs=[pl.BlockSpec(memory_space=pltpu.SMEM)] + [vmem] * 4,
-        out_specs=vmem,
+        functools.partial(exchange_kernel, unroll, inner),
+        out_shape=(
+            jax.ShapeDtypeStruct(packed.shape, F32),
+            jax.ShapeDtypeStruct((leaves, width), F32),
+            jax.ShapeDtypeStruct((devices, cap, points), F32),
+        ),
+        in_specs=[smem] * 3 + [vmem] * 8,
+        out_specs=(vmem, vmem, vmem),
         scratch_shapes=[
+            pltpu.VMEM((ops.shape[0] * count, width), F32),
+            pltpu.VMEM((leaves, 384), F32),
+            pltpu.VMEM((devices, 3, cap, points), F32),
+            pltpu.VMEM((leaves + 8, points), F32),
             pltpu.VMEM((unroll, FEATURES * 8, 128), F32),
             pltpu.VMEM((unroll, 3, 8, 128), F32),
-        ],
-        compiler_params=pltpu.CompilerParams(vmem_limit_bytes=14 << 20),
-        cost_estimate=pl.CostEstimate(
-            flops=2 * dens.shape[0] * 128 * 256 * 384,
-            bytes_accessed=4 << 20,
-            transcendentals=dens.shape[0] * 128 * 320,
+        ]
+        + [pltpu.SemaphoreType.DMA] * 4,
+        compiler_params=pltpu.CompilerParams(
+            vmem_limit_bytes=28 << 20, collective_id=1, has_side_effects=True
         ),
-        name="far_field",
-    )(dest, offsets, dens, jnp.asarray(main), jnp.asarray(last))
+        name="exchange",
+    )(
+        which, dest, slot_leaf, packed, offsets, rim, own, ops, m2l,
+        jnp.asarray(main), jnp.asarray(last),
+    )
 
 
 def on_device(
@@ -392,24 +472,17 @@
     mine = lax.dynamic_slice_in_dim(obs_owner, me * leaf_dev, leaf_dev)
 
     rim = from_behind(parent_local[parent_local.shape[0] - RIM :], AXES, 1)
-    packed, dest = pack(mine, jnp.transpose(src_coords, (1, 0, 2)), src_charge, leaf_center, devices, cap)
-
+    packed, dest, slot_leaf = pack(
+        mine, jnp.transpose(src_coords, (1, 0, 2)), src_charge, leaf_center, devices, cap
+    )
+    which = child_octant * (RIM + parent_local.shape[0]) + parent_slot
     offsets = jnp.transpose(obs_offset, (1, 0, 2))
-    outgoing = jnp.transpose(offsets.reshape(3, devices, cap, points), (1, 0, 2, 3))
-    outgoing, rim = lax.optimization_barrier((outgoing, rim))
-    at_leaves = lax.all_to_all(outgoing, AXES, 0, 0, tiled=True)
-
-    parents = jnp.concatenate([rim, parent_local], axis=0)
-    moved = jnp.einsum("pr,oqr->opq", parents, l2l_ops, precision=lax.Precision.HIGHEST)
-    stacked = moved.reshape(l2l_ops.shape[0] * parents.shape[0], width)
-    which = child_octant * parents.shape[0] + parent_slot
-    leaf_local, dens = leaf_rows(which, stacked, child_m2l, 384)
-    packed, dens = lax.optimization_barrier((packed, dens))
-    received = lax.all_to_all(packed, AXES, 0, 0, tiled=True)
-    far = far_field(dest, at_leaves, dens)
-    far = far.reshape(devices, cap, points)
+    inner = lax.axis_size("dom")
+    received, leaf_local, far = exchange(
+        which, dest, slot_leaf, packed, offsets, rim, parent_local, l2l_ops, child_m2l, inner
+    )
     near_list = jnp.transpose(near_slots).reshape(-1)
-    potential = near_field(received, offsets, near_list, far, lax.axis_size("dom"))
+    potential = near_field(received, offsets, near_list, far, inner)
     return (leaf_local, potential)
 
 

time: 182 us -> 201 us (1.10)
  Pallas kernels: 124 us -> 184 us
  waiting for transfers between devices: 17.2 us -> 0.01 us
  starting transfers between devices: 16.4 us -> 3.94 us
  matrix products: 6.24 us -> 0 us
  local copies, waits for them, and re-layouts: 16.4 us -> 11.5 us
    pallas_call x2 -> x1, Pallas kernels: 23.9 us -> 83.6 us  [exchange(): pl.pallas_call(functools.partial(exchange_kernel, unroll, inner), out_sha...]
    all_to_all x2 -> x0, waiting for transfers between devices: 14.1 us -> none  [the longest x1 8.96 us: on_device(): received = lax.all_to_all(packed, AXES, 0, 0, tiled=True)]
    all_to_all x2 -> x0, starting transfers between devices: 12.4 us -> none  [the longest x1 7.55 us: on_device(): at_leaves = lax.all_to_all(outgoing, AXES, 0, 0, tiled=True)]
    dot_general x1 -> x0, matrix products: 6.24 us -> none  [on_device(): jnp.einsum('pr,oqr->opq', parents, l2l_ops, precision=lax.Precision.HIGHEST)]
    ppermute x1, waiting for transfers between devices: 3.11 us -> 0.01 us  [from_behind(): return lax.ppermute(block, axis, route)]
    transpose x1 -> x0, local copies, waits for them, and re-layouts: 2.66 us -> none  [on_device(): jnp.transpose(offsets.reshape(3, devices, cap, points), (1, 0, 2, 3))]
    unnamed x33 -> x19, local copies, waits for them, and re-layouts: 12.3 us -> 9.87 us
  transfers between devices with their start and end apart: 3 -> 1, of which waited for: 3 -> 0; matrix products, arithmetic and copies ran while one was open for 7% -> 2% of each run, Pallas kernels for 16% -> 3%
where the time goes in v6:
time: 201 us
  Pallas kernels  184 us (92%)
  local copies, waits for them, and re-layouts  11.5 us (6%)
  starting transfers between devices  3.94 us (2%)
    pallas_call x1, Pallas kernels, near_field(): pl.pallas_call(functools.partial(near_kernel, unroll, inner), out_shape=j...  94.8 us
    pallas_call x1, Pallas kernels, exchange(): pl.pallas_call(functools.partial(exchange_kernel, unroll, inner), out_sha...  83.6 us
    unnamed x19, local copies, waits for them, and re-layouts  9.87 us
    pallas_call x1, Pallas kernels, pack(): pl.pallas_call(functools.partial(pack_kernel, capacity), out_shape=(jax.S...  5.52 us
  transfers between devices with their start and end apart: 1, of which 0 were waited for; matrix products, arithmetic and copies ran while one was open for 2% of the time, Pallas kernels for 3%

profile of v6, /device:TPU:1, one launch (start us, length us, event | category | flops | bytes accessed | tf_op | source)
XLA Modules:
  0.0 200.8 jit_solution(2739188908809386467)
XLA Ops:
  0.6 0.0 copy-start.6
  0.6 0.0 copy-start.5
  0.7 0.0 copy-start.1
  0.7 0.9 slice.3
  1.5 3.9 %collective-permute-start = (f32[16,296]{1,0:T(8,128)S(1)}, f32[16,296]{1,0:T(8,128)S(1)}, u32[]{:S(2)}, u32[]{:S(2)}) collective-permute-start(f32[16,296]{1,0:T(8,128)S(1)} %slice.3), channel_id=1, source_target_pairs={{0,1},{1,2},{2,3},{3,4},{4,5},{5,6},{6,7},{7,8},{8,9},{9,10},{10,1... | collective-permute-start | bytes 56840 | tf_op jit(solution)/shard_map/ppermute | solution.py:28
  5.5 0.7 multiply_add_fusion.which
  6.2 0.8 copy.15.center
  7.0 1.3 copy.16.m2l
  8.4 0.8 copy.20
  9.1 0.8 dynamic_slice.3.owner
  9.9 0.0 copy-start.2
  9.9 1.1 copy-done.2
  11.0 0.0 copy-start.3
  11.0 0.9 copy-done.3
  12.0 5.5 %pack.1 = (f32[128,5,8,128]{3,2,1,0:T(8,128)S(1)}, s32[512]{0:T(512)S(1)}, s32[1024]{0:T(1024)S(1)}) custom-call(s32[512]{0:T(512)S(1)} %dynamic_slice.3.owner, f32[3,512,128]{2,1,0:T(8,128)S(1)} %bitcast.9, f32[512,128]{1,0:T(8,128)S(1)} %copy-done.3, f32[512,3]{1,0:T(8,128)S(1)} %copy.15.center), custom_call_target="tpu_custom_call" | custom-call | tf_op jit(solution)/shard_map/pack/pallas_call | solution.py:65
  17.5 0.0 collective-permute-done.rim
  17.5 0.0 copy-done.6
  17.5 0.0 copy-done.5
  17.5 0.0 copy-done.1
  17.6 0.0 copy-start
  17.6 2.0 %copy-done = f32[8,296,296]{2,1,0:T(8,128)S(1)} copy-done((f32[8,296,296]{2,1,0:T(8,128)S(1)}, f32[8,296,296]{2,1,0:T(8,128)}, u32[]{:S(2)}) %copy-start) | copy-done | bytes 2803736
  19.6 0.0 copy-start.4
  19.6 0.9 copy-done.4
  20.5 83.6 %exchange.1 = (f32[128,5,8,128]{3,2,1,0:T(8,128)S(1)}, f32[512,296]{1,0:T(8,128)S(1)}, f32[128,8,128]{2,1,0:T(8,128)S(1)}) custom-call(s32[512]{0:T(512)S(1)} %multiply_add_fusion.which, s32[512]{0:T(512)S(1)} %get-tuple-element.8.dest, s32[1024]{0:T(1024)S(1)} %get-tuple-element.9.slot_leaf, f32[128,5,8,128]{3,2,1,0:T(8,128)S(1)} %get-tuple-element.10.packed, ...), custom_call_target="tpu_custom_call" | custom-call | tf_op jit(solution)/shard_map/exchange/pallas_call | solution.py:426
  104.2 94.8 %near_field.1 = f32[1024,128]{1,0:T(8,128)S(1)} custom-call(s32[8192]{0:T(1024)S(1)} %bitcast.10, f32[128,5,8,128]{3,2,1,0:T(8,128)S(1)} %get-tuple-element.12.src, f32[3,1024,128]{2,1,0:T(8,128)S(1)} %bitcast.8, f32[128,8,128]{2,1,0:T(8,128)S(1)} %get-tuple-element.13.far), custom_call_target="tpu_custom_call" | custom-call | flops 34359738368 | bytes 8388608 | tf_op jit(solution)/shard_map/near_field/pallas_call | solution.py:227
  198.9 1.1 copy.17
  200.0 0.8 copy.22
Async XLA Ops:
  0.6 16.9 %copy-start.6 = (bf16[256,256]{1,0:T(8,128)(2,1)S(1)}, bf16[256,256]{1,0:T(8,128)(2,1)}, u32[]{:S(2)}) copy-start(bf16[256,256]{1,0:T(8,128)(2,1)} %constant.23.clone.main) | copy-start | bytes 393220
  0.6 16.9 %copy-start.5 = (f32[64,296]{1,0:T(8,128)S(1)}, f32[64,296]{1,0:T(8,128)}, u32[]{:S(2)}) copy-start(f32[64,296]{1,0:T(8,128)} %own.1) | copy-start | bytes 227332
  0.7 16.9 %copy-start.1 = (f32[1024,3,128]{2,0,1:T(8,128)S(1)}, f32[1024,3,128]{2,0,1:T(8,128)}, u32[]{:S(2)}) copy-start(f32[1024,3,128]{2,0,1:T(8,128)} %param.22) | copy-start | bytes 4718596
  1.5 16.0 %collective-permute-start = (f32[16,296]{1,0:T(8,128)S(1)}, f32[16,296]{1,0:T(8,128)S(1)}, u32[]{:S(2)}, u32[]{:S(2)}) collective-permute-start(f32[16,296]{1,0:T(8,128)S(1)} %slice.3), channel_id=1, source_target_pairs={{0,1},{1,2},{2,3},{3,4},{4,5},{5,6},{6,7},{7,8},{8,9},{9,10},{10,1... | collective-permute-start | bytes 56840 | tf_op jit(solution)/shard_map/ppermute | solution.py:28
  9.9 1.1 copy-start.2
  11.0 0.9 copy-start.3
  17.6 2.0 %copy-start = (f32[8,296,296]{2,1,0:T(8,128)S(1)}, f32[8,296,296]{2,1,0:T(8,128)}, u32[]{:S(2)}) copy-start(f32[8,296,296]{2,1,0:T(8,128)} %ops.1) | copy-start | bytes 8411140
  19.6 0.9 copy-start.4

commit v7 on v5

--- a/solution.py
+++ b/solution.py
@@ -166,7 +166,7 @@
         charges[pl.ds(i * 8, 8)] = src[i, 3] * (0.25 / math.pi)
         return carry
 
-    lax.fori_loop(0, senders, prepare, 0)
+    lax.fori_loop(0, senders, prepare, 0, unroll=4)
     pl.semaphore_wait(barrier, senders - 1)
 
     def send(k):
@@ -245,7 +245,7 @@
     lax.fori_loop(0, senders, add, 0, unroll=8)
 
 
-def near_field(src, offsets, near_list, far, inner, unroll=8):
+def near_field(src, offsets, near_list, far, inner, unroll=16):
     senders, _, cap, _ = src.shape
     slots = senders * cap
     vmem = pl.BlockSpec(memory_space=pltpu.VMEM)

time: 182 us -> 178 us (0.978)
  Pallas kernels: 124 us -> 120 us
    pallas_call x1, Pallas kernels: 94.7 us -> 90.8 us  [near_field(): pl.pallas_call(functools.partial(near_kernel, unroll, inner), out_shape=j...]
  transfers between devices with their start and end apart: 3 -> 3, of which waited for: 3 -> 3; matrix products, arithmetic and copies ran while one was open for 7% -> 7% of each run, Pallas kernels for 16% -> 17%
where the time goes in v7:
time: 178 us; the launch traced here: 177 us
  Pallas kernels  120 us (67%)
  waiting for transfers between devices  17.2 us (10%)
  local copies, waits for them, and re-layouts  16.4 us (9%)
  starting transfers between devices  16.3 us (9%)
  matrix products  6.24 us (4%)
    pallas_call x1, Pallas kernels, near_field(): pl.pallas_call(functools.partial(near_kernel, unroll, inner), out_shape=j...  90.8 us
    pallas_call x1, Pallas kernels, far_field(): pl.pallas_call(functools.partial(far_kernel, unroll), out_shape=jax.Shape...  21 us
    unnamed x33, local copies, waits for them, and re-layouts  12.3 us
    all_to_all x1, waiting for transfers between devices, on_device(): received = lax.all_to_all(packed, AXES, 0, 0, tiled=True)  8.99 us
    all_to_all x1, starting transfers between devices, on_device(): at_leaves = lax.all_to_all(outgoing, AXES, 0, 0, tiled=True)  7.55 us
    dot_general x1, matrix products, on_device(): jnp.einsum('pr,oqr->opq', parents, l2l_ops, precision=lax.Precision.HIGHEST)  6.24 us
    pallas_call x1, Pallas kernels, pack(): pl.pallas_call(functools.partial(pack_kernel, capacity), out_shape=(jax.S...  5.52 us
    all_to_all x1, waiting for transfers between devices, on_device(): at_leaves = lax.all_to_all(outgoing, AXES, 0, 0, tiled=True)  5.14 us
  transfers between devices with their start and end apart: 3, of which 3 were waited for; matrix products, arithmetic and copies ran while one was open for 7% of the time, Pallas kernels for 17%

profile of v7, /device:TPU:1, one launch (start us, length us, event | category | flops | bytes accessed | tf_op | source)
XLA Modules:
  0.0 177.3 jit_solution(18375708160410213388)
XLA Ops:
  0.6 0.7 slice.3
  1.4 3.9 %collective-permute-start = (f32[16,296]{1,0:T(8,128)S(1)}, f32[16,296]{1,0:T(8,128)S(1)}, u32[]{:S(2)}, u32[]{:S(2)}) collective-permute-start(f32[16,296]{1,0:T(8,128)S(1)} %slice.3), channel_id=1, source_target_pairs={{0,1},{1,2},{2,3},{3,4},{4,5},{5,6},{6,7},{7,8},{8,9},{9,10},{10,1... | collective-permute-start | bytes 56840 | tf_op jit(solution)/shard_map/ppermute | solution.py:28
  5.3 2.7 %copy_bitcast_fusion = f32[128,3,8,128]{3,2,1,0:T(8,128)} fusion(f32[1024,3,128]{2,0,1:T(8,128)} %param.22), kind=kLoop, calls=%fused_computation | loop fusion | bytes 3145728 | tf_op jit(solution)/shard_map/transpose | solution.py:398
  8.0 0.0 copy-start.11
  8.0 3.1 %collective-permute-done = f32[16,296]{1,0:T(8,128)S(1)} collective-permute-done((f32[16,296]{1,0:T(8,128)S(1)}, f32[16,296]{1,0:T(8,128)S(1)}, u32[]{:S(2)}, u32[]{:S(2)}) %collective-permute-start) | collective-permute-done | bytes 18976 | tf_op jit(solution)/shard_map/ppermute | solution.py:28
  11.1 7.5 %all-to-all-start.1 = ((f32[128,3,8,128]{3,2,1,0:T(8,128)}), f32[128,3,8,128]{3,2,1,0:T(8,128)S(1)}, u32[]{:S(2)}, u32[]{:S(2)}) async-start(f32[128,3,8,128]{3,2,1,0:T(8,128)} %copy_bitcast_fusion), calls=%async_computation.1 | async-start | bytes 3145728 | tf_op jit(solution)/shard_map/all_to_all | solution.py:400
  18.6 0.0 copy-start.3
  18.7 0.0 copy-start.12
  18.7 0.0 copy-start.13
  18.7 0.0 copy-start.9
  18.7 0.0 copy-done.11
  18.7 0.1 copy.17.center
  18.9 1.4 copy.16.m2l
  20.3 0.8 dynamic_slice.3.owner
  21.1 0.0 copy-done.3
  21.1 0.0 copy-start.4
  21.1 0.9 copy-done.4
  22.0 5.5 %pack.1 = (f32[128,5,8,128]{3,2,1,0:T(8,128)}, s32[512]{0:T(512)S(1)}) custom-call(s32[512]{0:T(512)S(1)} %dynamic_slice.3.owner, f32[3,512,128]{2,1,0:T(8,128)S(1)} %bitcast.23, f32[512,128]{1,0:T(8,128)S(1)} %copy-done.4, f32[512,3]{1,0:T(8,128)S(1)} %copy.17.center), custom_call_target="tpu_custom_call" | custom-call | tf_op jit(solution)/shard_map/pack/pallas_call | solution.py:61
  27.5 0.0 copy-done.12
  27.6 0.0 copy-done.13
  27.6 0.0 copy-done.9
  27.6 6.2 %fusion = f32[80,8,296]{2,0,1:T(8,128)S(1)} fusion(f32[8,296,296]{2,1,0:T(8,128)} %param.17, f32[64,296]{1,0:T(8,128)S(1)} %copy-done.9, f32[16,296]{1,0:T(8,128)S(1)} %collective-permute-done), kind=kOutput, calls=%fused_computation.2 | convolution fusion | flops 672914560 | bytes 3656192 | tf_op jit(solution)/shard_map/pr,oqr->opq/dot_general | solution.py:403
  33.8 2.9 %leaf_rows.1 = (f32[512,296]{1,0:T(8,128)S(1)}, f32[512,384]{1,0:T(8,128)S(1)}) custom-call(s32[512]{0:T(512)S(1)} %multiply_add_fusion.which, f32[640,296]{1,0:T(8,128)S(1)} %bitcast.21, f32[512,296]{1,0:T(8,128)S(1)} %copy.16.m2l), custom_call_target="tpu_custom_call" | custom-call | flops 262144 | bytes 8388608 | tf_op jit(solution)/shard_map/leaf_rows/pallas_call | solution.py:91
  36.7 0.0 copy-start.5
  36.7 0.9 copy-done.5
  37.6 0.0 copy-start.10
  37.6 5.1 %all-to-all-done.1.off = f32[128,3,8,128]{3,2,1,0:T(8,128)S(1)} async-done(((f32[128,3,8,128]{3,2,1,0:T(8,128)}), f32[128,3,8,128]{3,2,1,0:T(8,128)S(1)}, u32[]{:S(2)}, u32[]{:S(2)}) %all-to-all-start.1) | async-done | bytes 1572896 | tf_op jit(solution)/shard_map/all_to_all | solution.py:400
  42.7 0.0 copy-start.1
  42.7 1.2 copy-done.1
  43.9 4.9 %all-to-all-start = ((f32[128,5,8,128]{3,2,1,0:T(8,128)}), f32[128,5,8,128]{3,2,1,0:T(8,128)S(1)}, u32[]{:S(2)}, u32[]{:S(2)}) async-start(f32[128,5,8,128]{3,2,1,0:T(8,128)} %get-tuple-element.14), calls=%async_computation | async-start | bytes 5242880 | tf_op jit(solution)/shard_map/all_to_all | solution.py:408
  48.8 0.0 copy-done.10
  48.8 1.1 copy.18
  49.9 0.0 copy-start.2
  49.9 1.4 copy-done.2
  51.3 0.0 copy-start.6
  51.3 1.1 copy-done.6
  52.4 0.0 copy-start.7
  52.4 0.9 copy-done.7
  53.4 0.0 copy-start.8
  53.4 0.9 copy-done.8
  54.3 21.0 %far_field.1 = f32[1024,128]{1,0:T(8,128)S(1)} custom-call(s32[512]{0:T(512)S(1)} %get-tuple-element.15.dest, f32[128,3,8,128]{3,2,1,0:T(8,128)S(1)} %copy-done.2, f32[512,384]{1,0:T(8,128)S(1)} %copy-done.6, bf16[256,256]{1,0:T(8,128)(2,1)S(1)} %copy-done.8, bf16[256,512]{1,0:T(8,128)(2,1)S(1)} %copy-done.7), custom_call_target="tpu_custom_call" | custom-call | flops 12884901888 | bytes 4194304 | tf_op jit(solution)/shard_map/far_field/pallas_call | solution.py:355
  75.2 9.0 %all-to-all-done.src = f32[128,5,8,128]{3,2,1,0:T(8,128)S(1)} async-done(((f32[128,5,8,128]{3,2,1,0:T(8,128)}), f32[128,5,8,128]{3,2,1,0:T(8,128)S(1)}, u32[]{:S(2)}, u32[]{:S(2)}) %all-to-all-start) | async-done | bytes 2621472 | tf_op jit(solution)/shard_map/all_to_all | solution.py:408
  84.2 0.0 copy-start
  84.2 1.4 copy-done
  85.6 90.8 %near_field.1 = f32[1024,128]{1,0:T(8,128)S(1)} custom-call(s32[8192]{0:T(1024)S(1)} %bitcast.24, f32[128,5,8,128]{3,2,1,0:T(8,128)S(1)} %all-to-all-done.src, f32[3,1024,128]{2,1,0:T(8,128)S(1)} %bitcast.22, f32[128,8,128]{2,1,0:T(8,128)S(1)} %bitcast.25), custom_call_target="tpu_custom_call" | custom-call | flops 34359738368 | bytes 8388608 | tf_op jit(solution)/shard_map/near_field/pallas_call | solution.py:252
  176.5 0.8 copy.24
  (2 shorter events, 0.0 us)
Async XLA Ops:
  1.4 9.7 %collective-permute-start = (f32[16,296]{1,0:T(8,128)S(1)}, f32[16,296]{1,0:T(8,128)S(1)}, u32[]{:S(2)}, u32[]{:S(2)}) collective-permute-start(f32[16,296]{1,0:T(8,128)S(1)} %slice.3), channel_id=1, source_target_pairs={{0,1},{1,2},{2,3},{3,4},{4,5},{5,6},{6,7},{7,8},{8,9},{9,10},{10,1... | collective-permute-start | bytes 56840 | tf_op jit(solution)/shard_map/ppermute | solution.py:28
  8.0 10.7 %copy-start.11 = (f32[512,3]{0,1:T(4,128)S(1)}, f32[512,3]{0,1:T(4,128)}, u32[]{:S(2)}) copy-start(f32[512,3]{0,1:T(4,128)} %param.18) | copy-start | bytes 18436
  11.1 31.7 %all-to-all-start.1 = ((f32[128,3,8,128]{3,2,1,0:T(8,128)}), f32[128,3,8,128]{3,2,1,0:T(8,128)S(1)}, u32[]{:S(2)}, u32[]{:S(2)}) async-start(f32[128,3,8,128]{3,2,1,0:T(8,128)} %copy_bitcast_fusion), calls=%async_computation.1 | async-start | bytes 3145728 | tf_op jit(solution)/shard_map/all_to_all | solution.py:400
  18.6 2.4 %copy-start.3 = (f32[512,3,128]{2,0,1:T(8,128)S(1)}, f32[512,3,128]{2,0,1:T(8,128)}, u32[]{:S(2)}) copy-start(f32[512,3,128]{2,0,1:T(8,128)} %param.19) | copy-start | bytes 2359300
  18.7 8.9 %copy-start.12 = (s32[512]{0:T(512)S(1)}, s32[512]{0:T(512)}, u32[]{:S(2)}) copy-start(s32[512]{0:T(512)} %param.14) | copy-start | bytes 6148
  18.7 8.9 %copy-start.13 = (s32[512]{0:T(512)S(1)}, s32[512]{0:T(512)}, u32[]{:S(2)}) copy-start(s32[512]{0:T(512)} %param.15) | copy-start | bytes 6148
  18.7 8.9 %copy-start.9 = (f32[64,296]{1,0:T(8,128)S(1)}, f32[64,296]{1,0:T(8,128)}, u32[]{:S(2)}) copy-start(f32[64,296]{1,0:T(8,128)} %param.13) | copy-start | bytes 227332
  21.1 1.0 copy-start.4
  36.7 0.9 copy-start.5
  37.6 11.2 %copy-start.10 = (s32[1024,8]{0,1:T(8,128)S(1)}, s32[1024,8]{0,1:T(8,128)}, u32[]{:S(2)}) copy-start(s32[1024,8]{0,1:T(8,128)} %param.23) | copy-start | bytes 98308
  42.7 1.2 copy-start.1
  43.9 40.3 %all-to-all-start = ((f32[128,5,8,128]{3,2,1,0:T(8,128)}), f32[128,5,8,128]{3,2,1,0:T(8,128)S(1)}, u32[]{:S(2)}, u32[]{:S(2)}) async-start(f32[128,5,8,128]{3,2,1,0:T(8,128)} %get-tuple-element.14), calls=%async_computation | async-start | bytes 5242880 | tf_op jit(solution)/shard_map/all_to_all | solution.py:408
  49.9 1.4 copy-start.2
  51.3 1.1 copy-start.6
  52.4 0.9 copy-start.7
  53.4 0.9 copy-start.8
  84.2 1.4 copy-start

commit v8 on v7

--- a/solution.py
+++ b/solution.py
@@ -32,8 +32,10 @@
     devices = out.shape[0]
     leaves = charge.shape[0]
     out[...] = jnp.zeros_like(out)
-    tail[:, 0:3] = center[...]
-    tail[:, 3:4] = jnp.ones((leaves, 1), F32)
+    for h in range(2):
+        tail[:, 4 * h : 4 * h + 3] = center[...]
+        tail[:, 4 * h + 3 : 4 * h + 4] = jnp.ones((leaves, 1), F32)
+    part = lax.broadcasted_iota(jnp.int32, (1, 8), 1) // 4
 
     def clear(i, carry):
         count[i] = 0
@@ -46,10 +48,12 @@
         rank = count[o]
         count[o] = rank + 1
         dest[j] = o * capacity + rank
+        half, row = rank // 4, rank % 4
         for c in range(3):
-            out[o, c, pl.ds(rank, 1), :] = coords[c, pl.ds(j, 1), :]
-        out[o, 3, pl.ds(rank, 1), :] = charge[pl.ds(j, 1), :]
-        out[o, 4, pl.ds(rank, 1), 0:4] = tail[pl.ds(j, 1), :]
+            out[o, 2 * c + half, pl.ds(row, 1), :] = coords[c, pl.ds(j, 1), :]
+        out[o, 6 + half, pl.ds(row, 1), :] = charge[pl.ds(j, 1), :]
+        old = out[o, 8, pl.ds(row, 1), 0:8]
+        out[o, 8, pl.ds(row, 1), 0:8] = jnp.where(part == half, tail[pl.ds(j, 1), :], old)
         return carry
 
     lax.fori_loop(0, leaves, place, 0, unroll=4)
@@ -61,12 +65,12 @@
     return pl.pallas_call(
         functools.partial(pack_kernel, capacity),
         out_shape=(
-            jax.ShapeDtypeStruct((devices, 5, capacity, 128), F32),
+            jax.ShapeDtypeStruct((devices, 9, capacity // 2, 128), F32),
             jax.ShapeDtypeStruct((leaves,), jnp.int32),
         ),
         in_specs=[pl.BlockSpec(memory_space=pltpu.SMEM), vmem, vmem, vmem],
         out_specs=(vmem, pl.BlockSpec(memory_space=pltpu.SMEM)),
-        scratch_shapes=[pltpu.SMEM((devices,), jnp.int32), pltpu.VMEM((leaves, 4), F32)],
+        scratch_shapes=[pltpu.SMEM((devices,), jnp.int32), pltpu.VMEM((leaves, 8), F32)],
         compiler_params=pltpu.CompilerParams(vmem_limit_bytes=14 << 20),
         name="pack",
     )(owner, coords, charge, center)
@@ -130,10 +134,15 @@
     return peer, (peer // inner, lax.rem(peer, inner))
 
 
+def both_halves(src, i, c):
+    return jnp.concatenate([src[i, 2 * c], src[i, 2 * c + 1]], axis=0)
+
+
 def near_kernel(
     unroll, inner, near_list, src, off, far, out, table, charges, tfeat, sfeat, arrived, sent, got
 ):
     senders, _, cap, _ = src.shape
+    cap = 2 * cap
     slots = senders * cap
     me = lax.axis_index("grp") * inner + lax.axis_index("dom")
     ones = jnp.ones((8, 128), F32)
@@ -158,12 +167,14 @@
             tfeat[u, 8 * f : 8 * f + 8] = zeros
 
     def prepare(i, carry):
-        cross, square = source_features(*(src[i, c] - 1.0 for c in range(3)))
+        cross, square = source_features(
+            *(both_halves(src, i, c) - 1.0 for c in range(3))
+        )
         for f, v in list(enumerate(cross)) + list(enumerate(square, 21)):
             sfeat[8 * f : 8 * f + 8] = v
         for s in range(8):
             table[i * 8 + s] = sfeat[pl.ds(s, FEATURES, stride=8), :].astype(BF16)
-        charges[pl.ds(i * 8, 8)] = src[i, 3] * (0.25 / math.pi)
+        charges[pl.ds(i * 8, 8)] = both_halves(src, i, 3) * (0.25 / math.pi)
         return carry
 
     lax.fori_loop(0, senders, prepare, 0, unroll=4)
@@ -190,7 +201,8 @@
     def rows(i, carry):
         for u in range(unroll):
             block = i * unroll + u
-            info = src[block, 4]
+            info = src[block, 8]
+            info = jnp.concatenate([info[:, 0:4], info[:, 4:8]], axis=0)
             place = [
                 (info[:, c : c + 1] - 1.0) + HALF * off[c, pl.ds(block * 8, 8), :] for c in range(3)
             ]
@@ -246,7 +258,7 @@
 
 
 def near_field(src, offsets, near_list, far, inner, unroll=16):
-    senders, _, cap, _ = src.shape
+    senders, cap, _ = far.shape
     slots = senders * cap
     vmem = pl.BlockSpec(memory_space=pltpu.VMEM)
     return pl.pallas_call(

time: 178 us -> 179 us (level)
  waiting for transfers between devices: 17.2 us -> 12.7 us
  Pallas kernels: 120 us -> 124 us
  starting transfers between devices: 16.3 us -> 19 us
    all_to_all x1, waiting for transfers between devices: 5.14 us -> 2.21 us  [on_device(): at_leaves = lax.all_to_all(outgoing, AXES, 0, 0, tiled=True)]
    pallas_call x1, Pallas kernels: 5.52 us -> 8.45 us  [pack(): pl.pallas_call(functools.partial(pack_kernel, capacity), out_shape=(jax.S...]
    all_to_all x1, starting transfers between devices: 4.86 us -> 7.55 us  [on_device(): received = lax.all_to_all(packed, AXES, 0, 0, tiled=True)]
  transfers between devices with their start and end apart: 3 -> 3, of which waited for: 3 -> 3; matrix products, arithmetic and copies ran while one was open for 7% -> 7% of each run, Pallas kernels for 17% -> 18%
where the time goes in v8:
time: 179 us; the launch traced here: 178 us
  Pallas kernels  124 us (69%)
  starting transfers between devices  19 us (11%)
  local copies, waits for them, and re-layouts  15.5 us (9%)
  waiting for transfers between devices  12.7 us (7%)
  matrix products  6.24 us (3%)
    pallas_call x1, Pallas kernels, near_field(): pl.pallas_call(functools.partial(near_kernel, unroll, inner), out_shape=j...  91.7 us
    pallas_call x1, Pallas kernels, far_field(): pl.pallas_call(functools.partial(far_kernel, unroll), out_shape=jax.Shape...  20.6 us
    unnamed x33, local copies, waits for them, and re-layouts  11.3 us
    pallas_call x1, Pallas kernels, pack(): pl.pallas_call(functools.partial(pack_kernel, capacity), out_shape=(jax.S...  8.45 us
    all_to_all x1, starting transfers between devices, on_device(): received = lax.all_to_all(packed, AXES, 0, 0, tiled=True)  7.55 us
    all_to_all x1, starting transfers between devices, on_device(): at_leaves = lax.all_to_all(outgoing, AXES, 0, 0, tiled=True)  7.54 us
    all_to_all x1, waiting for transfers between devices, on_device(): received = lax.all_to_all(packed, AXES, 0, 0, tiled=True)  7.36 us
    dot_general x1, matrix products, on_device(): jnp.einsum('pr,oqr->opq', parents, l2l_ops, precision=lax.Precision.HIGHEST)  6.24 us
  transfers between devices with their start and end apart: 3, of which 3 were waited for; matrix products, arithmetic and copies ran while one was open for 7% of the time, Pallas kernels for 18%

profile of v8, /device:TPU:1, one launch (start us, length us, event | category | flops | bytes accessed | tf_op | source)
XLA Modules:
  0.0 177.9 jit_solution(4936565576411369900)
XLA Ops:
  0.6 0.7 slice.3
  1.4 3.9 %collective-permute-start = (f32[16,296]{1,0:T(8,128)S(1)}, f32[16,296]{1,0:T(8,128)S(1)}, u32[]{:S(2)}, u32[]{:S(2)}) collective-permute-start(f32[16,296]{1,0:T(8,128)S(1)} %slice.3), channel_id=1, source_target_pairs={{0,1},{1,2},{2,3},{3,4},{4,5},{5,6},{6,7},{7,8},{8,9},{9,10},{10,1... | collective-permute-start | bytes 56840 | tf_op jit(solution)/shard_map/ppermute | solution.py:28
  5.3 2.7 %copy_bitcast_fusion = f32[128,3,8,128]{3,2,1,0:T(8,128)} fusion(f32[1024,3,128]{2,0,1:T(8,128)} %param.22), kind=kLoop, calls=%fused_computation | loop fusion | bytes 3145728 | tf_op jit(solution)/shard_map/transpose | solution.py:410
  8.0 0.0 copy-start.11
  8.0 3.1 %collective-permute-done = f32[16,296]{1,0:T(8,128)S(1)} collective-permute-done((f32[16,296]{1,0:T(8,128)S(1)}, f32[16,296]{1,0:T(8,128)S(1)}, u32[]{:S(2)}, u32[]{:S(2)}) %collective-permute-start) | collective-permute-done | bytes 18976 | tf_op jit(solution)/shard_map/ppermute | solution.py:28
  11.1 7.5 %all-to-all-start.1 = ((f32[128,3,8,128]{3,2,1,0:T(8,128)}), f32[128,3,8,128]{3,2,1,0:T(8,128)S(1)}, u32[]{:S(2)}, u32[]{:S(2)}) async-start(f32[128,3,8,128]{3,2,1,0:T(8,128)} %copy_bitcast_fusion), calls=%async_computation.1 | async-start | bytes 3145728 | tf_op jit(solution)/shard_map/all_to_all | solution.py:412
  18.6 0.0 copy-start.3
  18.6 0.0 copy-start.12
  18.7 0.0 copy-start.13
  18.7 0.0 copy-start.9
  18.7 0.0 copy-done.11
  18.7 0.1 copy.17.center
  18.9 1.4 copy.16.m2l
  20.3 0.8 dynamic_slice.3.owner
  21.0 0.0 copy-done.3
  21.0 0.0 copy-start.4
  21.0 0.9 copy-done.4
  22.0 8.4 %pack.1 = (f32[128,9,4,128]{3,2,1,0:T(4,128)}, s32[512]{0:T(512)S(1)}) custom-call(s32[512]{0:T(512)S(1)} %dynamic_slice.3.owner, f32[3,512,128]{2,1,0:T(8,128)S(1)} %bitcast.23, f32[512,128]{1,0:T(8,128)S(1)} %copy-done.4, f32[512,3]{1,0:T(8,128)S(1)} %copy.17.center), custom_call_target="tpu_custom_call" | custom-call | tf_op jit(solution)/shard_map/pack/pallas_call | solution.py:65
  30.5 0.0 copy-done.12
  30.5 0.0 copy-done.13
  30.5 0.0 copy-done.9
  30.5 6.2 %fusion = f32[80,8,296]{2,0,1:T(8,128)S(1)} fusion(f32[8,296,296]{2,1,0:T(8,128)} %param.17, f32[64,296]{1,0:T(8,128)S(1)} %copy-done.9, f32[16,296]{1,0:T(8,128)S(1)} %collective-permute-done), kind=kOutput, calls=%fused_computation.2 | convolution fusion | flops 672914560 | bytes 3656192 | tf_op jit(solution)/shard_map/pr,oqr->opq/dot_general | solution.py:415
  36.7 2.9 %leaf_rows.1 = (f32[512,296]{1,0:T(8,128)S(1)}, f32[512,384]{1,0:T(8,128)S(1)}) custom-call(s32[512]{0:T(512)S(1)} %multiply_add_fusion.which, f32[640,296]{1,0:T(8,128)S(1)} %bitcast.21, f32[512,296]{1,0:T(8,128)S(1)} %copy.16.m2l), custom_call_target="tpu_custom_call" | custom-call | flops 262144 | bytes 8388608 | tf_op jit(solution)/shard_map/leaf_rows/pallas_call | solution.py:95
  39.6 0.0 copy-start.5
  39.6 0.9 copy-done.5
  40.5 0.0 copy-start.10
  40.5 0.0 copy-start.8
  40.5 2.2 %all-to-all-done.1.off = f32[128,3,8,128]{3,2,1,0:T(8,128)S(1)} async-done(((f32[128,3,8,128]{3,2,1,0:T(8,128)}), f32[128,3,8,128]{3,2,1,0:T(8,128)S(1)}, u32[]{:S(2)}, u32[]{:S(2)}) %all-to-all-start.1) | async-done | bytes 1572896 | tf_op jit(solution)/shard_map/all_to_all | solution.py:412
  42.7 0.0 copy-start.1
  42.7 1.1 copy-done.1
  43.9 7.6 %all-to-all-start = ((f32[128,9,4,128]{3,2,1,0:T(4,128)}), f32[128,9,4,128]{3,2,1,0:T(4,128)S(1)}, u32[]{:S(2)}, u32[]{:S(2)}) async-start(f32[128,9,4,128]{3,2,1,0:T(4,128)} %get-tuple-element.14), calls=%async_computation | async-start | bytes 4718592 | tf_op jit(solution)/shard_map/all_to_all | solution.py:420
  51.4 0.0 copy-done.10
  51.5 1.1 copy.18
  52.5 0.0 copy-done.8
  52.5 0.0 copy-start.2
  52.5 1.4 copy-done.2
  53.9 0.0 copy-start.6
  53.9 1.1 copy-done.6
  55.1 0.0 copy-start.7
  55.1 0.9 copy-done.7
  56.0 20.6 %far_field.1 = f32[1024,128]{1,0:T(8,128)S(1)} custom-call(s32[512]{0:T(512)S(1)} %get-tuple-element.15.dest, f32[128,3,8,128]{3,2,1,0:T(8,128)S(1)} %copy-done.2, f32[512,384]{1,0:T(8,128)S(1)} %copy-done.6, bf16[256,256]{1,0:T(8,128)(2,1)S(1)} %copy-done.8, bf16[256,512]{1,0:T(8,128)(2,1)S(1)} %copy-done.7), custom_call_target="tpu_custom_call" | custom-call | flops 12884901888 | bytes 4194304 | tf_op jit(solution)/shard_map/far_field/pallas_call | solution.py:367
  76.6 7.4 %all-to-all-done.src = f32[128,9,4,128]{3,2,1,0:T(4,128)S(1)} async-done(((f32[128,9,4,128]{3,2,1,0:T(4,128)}), f32[128,9,4,128]{3,2,1,0:T(4,128)S(1)}, u32[]{:S(2)}, u32[]{:S(2)}) %all-to-all-start) | async-done | bytes 2359328 | tf_op jit(solution)/shard_map/all_to_all | solution.py:420
  84.0 0.0 copy-start
  84.0 1.4 copy-done
  85.4 91.7 %near_field.1 = f32[1024,128]{1,0:T(8,128)S(1)} custom-call(s32[8192]{0:T(1024)S(1)} %bitcast.24, f32[128,9,4,128]{3,2,1,0:T(4,128)S(1)} %all-to-all-done.src, f32[3,1024,128]{2,1,0:T(8,128)S(1)} %bitcast.22, f32[128,8,128]{2,1,0:T(8,128)S(1)} %bitcast.25), custom_call_target="tpu_custom_call" | custom-call | flops 34359738368 | bytes 8388608 | tf_op jit(solution)/shard_map/near_field/pallas_call | solution.py:264
  177.1 0.8 copy.24
  (2 shorter events, 0.0 us)
Async XLA Ops:
  1.4 9.7 %collective-permute-start = (f32[16,296]{1,0:T(8,128)S(1)}, f32[16,296]{1,0:T(8,128)S(1)}, u32[]{:S(2)}, u32[]{:S(2)}) collective-permute-start(f32[16,296]{1,0:T(8,128)S(1)} %slice.3), channel_id=1, source_target_pairs={{0,1},{1,2},{2,3},{3,4},{4,5},{5,6},{6,7},{7,8},{8,9},{9,10},{10,1... | collective-permute-start | bytes 56840 | tf_op jit(solution)/shard_map/ppermute | solution.py:28
  8.0 10.7 %copy-start.11 = (f32[512,3]{0,1:T(4,128)S(1)}, f32[512,3]{0,1:T(4,128)}, u32[]{:S(2)}) copy-start(f32[512,3]{0,1:T(4,128)} %param.18) | copy-start | bytes 18436
  11.1 31.6 %all-to-all-start.1 = ((f32[128,3,8,128]{3,2,1,0:T(8,128)}), f32[128,3,8,128]{3,2,1,0:T(8,128)S(1)}, u32[]{:S(2)}, u32[]{:S(2)}) async-start(f32[128,3,8,128]{3,2,1,0:T(8,128)} %copy_bitcast_fusion), calls=%async_computation.1 | async-start | bytes 3145728 | tf_op jit(solution)/shard_map/all_to_all | solution.py:412
  18.6 2.4 %copy-start.3 = (f32[512,3,128]{2,0,1:T(8,128)S(1)}, f32[512,3,128]{2,0,1:T(8,128)}, u32[]{:S(2)}) copy-start(f32[512,3,128]{2,0,1:T(8,128)} %param.19) | copy-start | bytes 2359300
  18.6 11.8 %copy-start.12 = (s32[512]{0:T(512)S(1)}, s32[512]{0:T(512)}, u32[]{:S(2)}) copy-start(s32[512]{0:T(512)} %param.14) | copy-start | bytes 6148
  18.7 11.8 %copy-start.13 = (s32[512]{0:T(512)S(1)}, s32[512]{0:T(512)}, u32[]{:S(2)}) copy-start(s32[512]{0:T(512)} %param.15) | copy-start | bytes 6148
  18.7 11.8 %copy-start.9 = (f32[64,296]{1,0:T(8,128)S(1)}, f32[64,296]{1,0:T(8,128)}, u32[]{:S(2)}) copy-start(f32[64,296]{1,0:T(8,128)} %param.13) | copy-start | bytes 227332
  21.0 1.0 copy-start.4
  39.6 0.9 copy-start.5
  40.5 10.9 %copy-start.10 = (s32[1024,8]{0,1:T(8,128)S(1)}, s32[1024,8]{0,1:T(8,128)}, u32[]{:S(2)}) copy-start(s32[1024,8]{0,1:T(8,128)} %param.23) | copy-start | bytes 98308
  40.5 12.0 %copy-start.8 = (bf16[256,256]{1,0:T(8,128)(2,1)S(1)}, bf16[256,256]{1,0:T(8,128)(2,1)}, u32[]{:S(2)}) copy-start(bf16[256,256]{1,0:T(8,128)(2,1)} %constant.23.clone.main) | copy-start | bytes 393220
  42.7 1.1 copy-start.1
  43.9 40.1 %all-to-all-start = ((f32[128,9,4,128]{3,2,1,0:T(4,128)}), f32[128,9,4,128]{3,2,1,0:T(4,128)S(1)}, u32[]{:S(2)}, u32[]{:S(2)}) async-start(f32[128,9,4,128]{3,2,1,0:T(4,128)} %get-tuple-element.14), calls=%async_computation | async-start | bytes 4718592 | tf_op jit(solution)/shard_map/all_to_all | solution.py:420
  52.5 1.4 copy-start.2
  53.9 1.1 copy-start.6
  55.1 0.9 copy-start.7
  84.0 1.4 copy-start

commit v9 on v8

--- a/solution.py
+++ b/solution.py
@@ -28,14 +28,13 @@
     return lax.ppermute(block, axis, route)
 
 
-def pack_kernel(capacity, owner, coords, charge, center, out, dest, count, tail):
+def pack_kernel(capacity, owner, coords, charge, center, out, dest, count, tail, places):
     devices = out.shape[0]
     leaves = charge.shape[0]
     out[...] = jnp.zeros_like(out)
-    for h in range(2):
-        tail[:, 4 * h : 4 * h + 3] = center[...]
-        tail[:, 4 * h + 3 : 4 * h + 4] = jnp.ones((leaves, 1), F32)
-    part = lax.broadcasted_iota(jnp.int32, (1, 8), 1) // 4
+    tail[:, 0:3] = center[...]
+    tail[:, 3:4] = jnp.ones((leaves, 1), F32)
+    places[...] = jnp.zeros_like(places)
 
     def clear(i, carry):
         count[i] = 0
@@ -48,15 +47,21 @@
         rank = count[o]
         count[o] = rank + 1
         dest[j] = o * capacity + rank
-        half, row = rank // 4, rank % 4
+        half, row = rank >> 2, rank & 3
         for c in range(3):
             out[o, 2 * c + half, pl.ds(row, 1), :] = coords[c, pl.ds(j, 1), :]
         out[o, 6 + half, pl.ds(row, 1), :] = charge[pl.ds(j, 1), :]
-        old = out[o, 8, pl.ds(row, 1), 0:8]
-        out[o, 8, pl.ds(row, 1), 0:8] = jnp.where(part == half, tail[pl.ds(j, 1), :], old)
+        places[o, pl.ds(rank, 1), :] = tail[pl.ds(j, 1), :]
         return carry
 
     lax.fori_loop(0, leaves, place, 0, unroll=4)
+
+    def fold(o, carry):
+        out[o, 8, :, 0:4] = places[o, 0:4, :]
+        out[o, 8, :, 4:8] = places[o, 4:8, :]
+        return carry
+
+    lax.fori_loop(0, devices, fold, 0, unroll=8)
 
 
 def pack(owner, coords, charge, center, devices, capacity):
@@ -70,7 +75,7 @@
         ),
         in_specs=[pl.BlockSpec(memory_space=pltpu.SMEM), vmem, vmem, vmem],
         out_specs=(vmem, pl.BlockSpec(memory_space=pltpu.SMEM)),
-        scratch_shapes=[pltpu.SMEM((devices,), jnp.int32), pltpu.VMEM((leaves, 8), F32)],
+        scratch_shapes=[pltpu.SMEM((devices,), jnp.int32), pltpu.VMEM((leaves, 4), F32), pltpu.VMEM((devices, 8, 4), F32)],
         compiler_params=pltpu.CompilerParams(vmem_limit_bytes=14 << 20),
         name="pack",
     )(owner, coords, charge, center)

time: 179 us -> 178 us (level)
  no operation moved by 1% of the time
where the time goes in v9:
time: 178 us; the launch traced here: 177 us
  Pallas kernels  123 us (69%)
  starting transfers between devices  18.2 us (10%)
  local copies, waits for them, and re-layouts  15.5 us (9%)
  waiting for transfers between devices  13.5 us (8%)
  matrix products  6.24 us (4%)
    pallas_call x1, Pallas kernels, near_field(): pl.pallas_call(functools.partial(near_kernel, unroll, inner), out_shape=j...  91.6 us
    pallas_call x1, Pallas kernels, far_field(): pl.pallas_call(functools.partial(far_kernel, unroll), out_shape=jax.Shape...  20.6 us
    unnamed x33, local copies, waits for them, and re-layouts  11.3 us
    pallas_call x1, Pallas kernels, pack(): pl.pallas_call(functools.partial(pack_kernel, capacity), out_shape=(jax.S...  7.63 us
    all_to_all x1, starting transfers between devices, on_device(): at_leaves = lax.all_to_all(outgoing, AXES, 0, 0, tiled=True)  7.54 us
    all_to_all x1, waiting for transfers between devices, on_device(): received = lax.all_to_all(packed, AXES, 0, 0, tiled=True)  7.37 us
    all_to_all x1, starting transfers between devices, on_device(): received = lax.all_to_all(packed, AXES, 0, 0, tiled=True)  6.74 us
    dot_general x1, matrix products, on_device(): jnp.einsum('pr,oqr->opq', parents, l2l_ops, precision=lax.Precision.HIGHEST)  6.24 us
  transfers between devices with their start and end apart: 3, of which 3 were waited for; matrix products, arithmetic and copies ran while one was open for 7% of the time, Pallas kernels for 18%

profile of v9, /device:TPU:1, one launch (start us, length us, event | category | flops | bytes accessed | tf_op | source)
XLA Modules:
  0.0 177.0 jit_solution(13596614185194576256)
XLA Ops:
  0.6 0.7 slice.3
  1.4 3.9 %collective-permute-start = (f32[16,296]{1,0:T(8,128)S(1)}, f32[16,296]{1,0:T(8,128)S(1)}, u32[]{:S(2)}, u32[]{:S(2)}) collective-permute-start(f32[16,296]{1,0:T(8,128)S(1)} %slice.3), channel_id=1, source_target_pairs={{0,1},{1,2},{2,3},{3,4},{4,5},{5,6},{6,7},{7,8},{8,9},{9,10},{10,1... | collective-permute-start | bytes 56840 | tf_op jit(solution)/shard_map/ppermute | solution.py:28
  5.3 2.7 %copy_bitcast_fusion = f32[128,3,8,128]{3,2,1,0:T(8,128)} fusion(f32[1024,3,128]{2,0,1:T(8,128)} %param.22), kind=kLoop, calls=%fused_computation | loop fusion | bytes 3145728 | tf_op jit(solution)/shard_map/transpose | solution.py:415
  8.0 0.0 copy-start.11
  8.0 3.1 %collective-permute-done = f32[16,296]{1,0:T(8,128)S(1)} collective-permute-done((f32[16,296]{1,0:T(8,128)S(1)}, f32[16,296]{1,0:T(8,128)S(1)}, u32[]{:S(2)}, u32[]{:S(2)}) %collective-permute-start) | collective-permute-done | bytes 18976 | tf_op jit(solution)/shard_map/ppermute | solution.py:28
  11.1 7.5 %all-to-all-start.1 = ((f32[128,3,8,128]{3,2,1,0:T(8,128)}), f32[128,3,8,128]{3,2,1,0:T(8,128)S(1)}, u32[]{:S(2)}, u32[]{:S(2)}) async-start(f32[128,3,8,128]{3,2,1,0:T(8,128)} %copy_bitcast_fusion), calls=%async_computation.1 | async-start | bytes 3145728 | tf_op jit(solution)/shard_map/all_to_all | solution.py:417
  18.6 0.0 copy-start.3
  18.6 0.0 copy-start.12
  18.7 0.0 copy-start.13
  18.7 0.0 copy-start.9
  18.7 0.0 copy-done.11
  18.7 0.1 copy.17.center
  18.9 1.4 copy.16.m2l
  20.3 0.8 dynamic_slice.3.owner
  21.0 0.0 copy-done.3
  21.0 0.0 copy-start.4
  21.0 0.9 copy-done.4
  22.0 7.6 %pack.1 = (f32[128,9,4,128]{3,2,1,0:T(4,128)}, s32[512]{0:T(512)S(1)}) custom-call(s32[512]{0:T(512)S(1)} %dynamic_slice.3.owner, f32[3,512,128]{2,1,0:T(8,128)S(1)} %bitcast.23, f32[512,128]{1,0:T(8,128)S(1)} %copy-done.4, f32[512,3]{1,0:T(8,128)S(1)} %copy.17.center), custom_call_target="tpu_custom_call" | custom-call | tf_op jit(solution)/shard_map/pack/pallas_call | solution.py:70
  29.6 0.0 copy-done.12
  29.6 0.0 copy-done.13
  29.7 0.0 copy-done.9
  29.7 6.2 %fusion = f32[80,8,296]{2,0,1:T(8,128)S(1)} fusion(f32[8,296,296]{2,1,0:T(8,128)} %param.17, f32[64,296]{1,0:T(8,128)S(1)} %copy-done.9, f32[16,296]{1,0:T(8,128)S(1)} %collective-permute-done), kind=kOutput, calls=%fused_computation.2 | convolution fusion | flops 672914560 | bytes 3656192 | tf_op jit(solution)/shard_map/pr,oqr->opq/dot_general | solution.py:420
  35.9 2.9 %leaf_rows.1 = (f32[512,296]{1,0:T(8,128)S(1)}, f32[512,384]{1,0:T(8,128)S(1)}) custom-call(s32[512]{0:T(512)S(1)} %multiply_add_fusion.which, f32[640,296]{1,0:T(8,128)S(1)} %bitcast.21, f32[512,296]{1,0:T(8,128)S(1)} %copy.16.m2l), custom_call_target="tpu_custom_call" | custom-call | flops 262144 | bytes 8388608 | tf_op jit(solution)/shard_map/leaf_rows/pallas_call | solution.py:100
  38.8 0.0 copy-start.5
  38.8 0.9 copy-done.5
  39.7 0.0 copy-start.10
  39.7 0.0 copy-start.8
  39.7 3.0 %all-to-all-done.1.off = f32[128,3,8,128]{3,2,1,0:T(8,128)S(1)} async-done(((f32[128,3,8,128]{3,2,1,0:T(8,128)}), f32[128,3,8,128]{3,2,1,0:T(8,128)S(1)}, u32[]{:S(2)}, u32[]{:S(2)}) %all-to-all-start.1) | async-done | bytes 1572896 | tf_op jit(solution)/shard_map/all_to_all | solution.py:417
  42.7 0.0 copy-start.1
  42.7 1.1 copy-done.1
  43.9 6.7 %all-to-all-start = ((f32[128,9,4,128]{3,2,1,0:T(4,128)}), f32[128,9,4,128]{3,2,1,0:T(4,128)S(1)}, u32[]{:S(2)}, u32[]{:S(2)}) async-start(f32[128,9,4,128]{3,2,1,0:T(4,128)} %get-tuple-element.14), calls=%async_computation | async-start | bytes 4718592 | tf_op jit(solution)/shard_map/all_to_all | solution.py:425
  50.6 0.0 copy-done.10
  50.6 1.1 copy.18
  51.7 0.0 copy-done.8
  51.7 0.0 copy-start.2
  51.7 1.4 copy-done.2
  53.1 0.0 copy-start.6
  53.1 1.1 copy-done.6
  54.3 0.0 copy-start.7
  54.3 0.9 copy-done.7
  55.2 20.6 %far_field.1 = f32[1024,128]{1,0:T(8,128)S(1)} custom-call(s32[512]{0:T(512)S(1)} %get-tuple-element.15.dest, f32[128,3,8,128]{3,2,1,0:T(8,128)S(1)} %copy-done.2, f32[512,384]{1,0:T(8,128)S(1)} %copy-done.6, bf16[256,256]{1,0:T(8,128)(2,1)S(1)} %copy-done.8, bf16[256,512]{1,0:T(8,128)(2,1)S(1)} %copy-done.7), custom_call_target="tpu_custom_call" | custom-call | flops 12884901888 | bytes 4194304 | tf_op jit(solution)/shard_map/far_field/pallas_call | solution.py:372
  75.8 7.4 %all-to-all-done.src = f32[128,9,4,128]{3,2,1,0:T(4,128)S(1)} async-done(((f32[128,9,4,128]{3,2,1,0:T(4,128)}), f32[128,9,4,128]{3,2,1,0:T(4,128)S(1)}, u32[]{:S(2)}, u32[]{:S(2)}) %all-to-all-start) | async-done | bytes 2359328 | tf_op jit(solution)/shard_map/all_to_all | solution.py:425
  83.1 0.0 copy-start
  83.1 1.4 copy-done
  84.5 91.6 %near_field.1 = f32[1024,128]{1,0:T(8,128)S(1)} custom-call(s32[8192]{0:T(1024)S(1)} %bitcast.24, f32[128,9,4,128]{3,2,1,0:T(4,128)S(1)} %all-to-all-done.src, f32[3,1024,128]{2,1,0:T(8,128)S(1)} %bitcast.22, f32[128,8,128]{2,1,0:T(8,128)S(1)} %bitcast.25), custom_call_target="tpu_custom_call" | custom-call | flops 34359738368 | bytes 8388608 | tf_op jit(solution)/shard_map/near_field/pallas_call | solution.py:269
  176.2 0.8 copy.24
  (2 shorter events, 0.0 us)
Async XLA Ops:
  1.4 9.7 %collective-permute-start = (f32[16,296]{1,0:T(8,128)S(1)}, f32[16,296]{1,0:T(8,128)S(1)}, u32[]{:S(2)}, u32[]{:S(2)}) collective-permute-start(f32[16,296]{1,0:T(8,128)S(1)} %slice.3), channel_id=1, source_target_pairs={{0,1},{1,2},{2,3},{3,4},{4,5},{5,6},{6,7},{7,8},{8,9},{9,10},{10,1... | collective-permute-start | bytes 56840 | tf_op jit(solution)/shard_map/ppermute | solution.py:28
  8.0 10.7 %copy-start.11 = (f32[512,3]{0,1:T(4,128)S(1)}, f32[512,3]{0,1:T(4,128)}, u32[]{:S(2)}) copy-start(f32[512,3]{0,1:T(4,128)} %param.18) | copy-start | bytes 18436
  11.1 31.6 %all-to-all-start.1 = ((f32[128,3,8,128]{3,2,1,0:T(8,128)}), f32[128,3,8,128]{3,2,1,0:T(8,128)S(1)}, u32[]{:S(2)}, u32[]{:S(2)}) async-start(f32[128,3,8,128]{3,2,1,0:T(8,128)} %copy_bitcast_fusion), calls=%async_computation.1 | async-start | bytes 3145728 | tf_op jit(solution)/shard_map/all_to_all | solution.py:417
  18.6 2.4 %copy-start.3 = (f32[512,3,128]{2,0,1:T(8,128)S(1)}, f32[512,3,128]{2,0,1:T(8,128)}, u32[]{:S(2)}) copy-start(f32[512,3,128]{2,0,1:T(8,128)} %param.19) | copy-start | bytes 2359300
  18.6 11.0 %copy-start.12 = (s32[512]{0:T(512)S(1)}, s32[512]{0:T(512)}, u32[]{:S(2)}) copy-start(s32[512]{0:T(512)} %param.14) | copy-start | bytes 6148
  18.7 11.0 %copy-start.13 = (s32[512]{0:T(512)S(1)}, s32[512]{0:T(512)}, u32[]{:S(2)}) copy-start(s32[512]{0:T(512)} %param.15) | copy-start | bytes 6148
  18.7 11.0 %copy-start.9 = (f32[64,296]{1,0:T(8,128)S(1)}, f32[64,296]{1,0:T(8,128)}, u32[]{:S(2)}) copy-start(f32[64,296]{1,0:T(8,128)} %param.13) | copy-start | bytes 227332
  21.0 1.0 copy-start.4
  38.8 0.9 copy-start.5
  39.7 10.9 %copy-start.10 = (s32[1024,8]{0,1:T(8,128)S(1)}, s32[1024,8]{0,1:T(8,128)}, u32[]{:S(2)}) copy-start(s32[1024,8]{0,1:T(8,128)} %param.23) | copy-start | bytes 98308
  39.7 12.0 %copy-start.8 = (bf16[256,256]{1,0:T(8,128)(2,1)S(1)}, bf16[256,256]{1,0:T(8,128)(2,1)}, u32[]{:S(2)}) copy-start(bf16[256,256]{1,0:T(8,128)(2,1)} %constant.23.clone.main) | copy-start | bytes 393220
  42.7 1.1 copy-start.1
  43.9 39.3 %all-to-all-start = ((f32[128,9,4,128]{3,2,1,0:T(4,128)}), f32[128,9,4,128]{3,2,1,0:T(4,128)S(1)}, u32[]{:S(2)}, u32[]{:S(2)}) async-start(f32[128,9,4,128]{3,2,1,0:T(4,128)} %get-tuple-element.14), calls=%async_computation | async-start | bytes 4718592 | tf_op jit(solution)/shard_map/all_to_all | solution.py:425
  51.7 1.4 copy-start.2
  53.1 1.1 copy-start.6
  54.3 0.9 copy-start.7
  83.1 1.4 copy-start
